TPU v7x, 32 devices: a whole 2x2x4 slice. The times are simulated.
32 devices in a mesh: az: 16 (over z, y, x), wn: 2 (over core).
Axes of the slice: x: 2, y: 2, z: 4, core: 2. Of those that a mesh axis runs over, the one named last changes fastest.
Arguments:
- visc_wn: float32 [5, 32, 4096], P(None, 'wn', 'az'), may hold values from 0.5 to 2
- conv_wn: float32 [5, 5, 32, 4096], P(None, None, 'wn', 'az'), may hold values from -0.3 to 0.3
- spin: float32 [5, 5, 32, 4096], P(None, None, 'wn', 'az'), may hold values from -0.3 to 0.3
- visc_az: float32 [5, 32, 4096], P(None, 'wn', 'az'), may hold values from 0.001953125 to 0.015625
- flux_wn: float32 [5, 32, 4096], P(None, 'wn', 'az'), may hold values from -6 to 6
- flux_az: float32 [5, 32, 4096], P(None, 'wn', 'az'), may hold values from -0.375 to 0.375
- incr_prev: float32 [5, 32, 4096], P(None, 'wn', 'az'), may hold values from -12 to 12
- cell_type: int32 [32], P('wn'), may hold values from 0 to 1, as said below
- edge_index: int32 [4096], P('az'), may hold values from 8 to 23
Outputs:
- increment: float32 [5, 32, 4096], P(None, 'wn', 'az')
- defect: float32 [5, 32, 4096], P(None, 'wn', 'az')
Inputs may be any that keep to these rules, and one draw needn't show every extreme that they name: cell_type is 1 exactly at the first t wall-normal points and 0 at the others, for one t from 2 to 4 in each draw.
All inputs are finite; a program needn't handle non-finite values.
Results may differ from a plain program's by a relative error of at most 0.0023.
Values sent between devices are 32-bit elements; how exact they have to be, the bound alone decides.
No kernel may reach another device: no remote copies, remote signals or barrier semaphores. Data moves between devices by JAX's collectives and lax.ppermute only.
A program may use at most 64 MiB of HBM per device.

v0:
```python
import jax
import jax.numpy as jnp
from jax import lax
from jax.sharding import PartitionSpec as P

S = 8
SWEEPS = 2


OUTER_SCALE = 0.25


def from_behind(array, axis, by):
    size = lax.axis_size(axis)
    pairs = [(i, i + by) for i in range(size) if 0 <= i + by < size]
    return lax.ppermute(array, axis, pairs)


def shifted(value, axis, steps):
    count = lax.axis_size(axis)
    pairs = [(source, (source + steps) % count) for source in range(count)]
    return lax.ppermute(value, axis, pairs)


def with_halo(array, sides, width, wrap):
    for axis, dim in sides:
        size, length = (lax.axis_size(axis), array.shape[dim])
        up = [(i, (i + 1) % size) for i in range(size if wrap else size - 1)]
        down = [(j, i) for i, j in up]
        last = lax.slice_in_dim(array, length - width, length, axis=dim)
        leading = lax.slice_in_dim(array, 0, width, axis=dim)
        before = lax.ppermute(last, axis, up)
        after = lax.ppermute(leading, axis, down)
        array = jnp.concatenate([before, array, after], axis=dim)
    return array


def block_product(matrix, operand):
    return jnp.sum(matrix[:, :, None] * operand[None], axis=1)


def block_vector(matrix, vector):
    return jnp.sum(matrix * vector[None], axis=1)


def diagonal_of(vector):
    order_size = vector.shape[0]
    identity = jnp.eye(order_size, dtype=vector.dtype).reshape(
        (order_size, order_size) + (1,) * (vector.ndim - 1)
    )
    return identity * vector[None]


def identity_blocks(shape_full, dtype_name):
    order_size = shape_full[0]
    identity = jnp.eye(order_size, dtype=dtype_name).reshape(
        (order_size, order_size) + (1,) * (len(shape_full) - 2)
    )
    return jnp.broadcast_to(identity, shape_full)


def invert(matrix):
    order_size = matrix.shape[0]
    working = matrix
    result = identity_blocks(matrix.shape, matrix.dtype)
    for pivot_row in range(order_size):
        pivot_scale = 1.0 / working[pivot_row, pivot_row]
        row_working = working[pivot_row] * pivot_scale
        row_result = result[pivot_row] * pivot_scale
        column = working[:, pivot_row]
        working = working - column[:, None] * row_working[None]
        result = result - column[:, None] * row_result[None]
        working = working.at[pivot_row].set(row_working)
        result = result.at[pivot_row].set(row_result)
    return result


def factor_lines(lower_block, center_block, upper_block):
    points = center_block.shape[2]
    padded_size = 1
    while padded_size < points:
        padded_size = padded_size * 2
    levels = []
    while center_block.shape[2] > 1:
        odd_inverse = invert(center_block[:, :, 1::2])
        odd_lower = lower_block[:, :, 1::2]
        odd_upper = upper_block[:, :, 1::2]
        edge_shape = odd_lower.shape[:2] + (1,) + odd_lower.shape[3:]
        zero_edge = jnp.zeros(edge_shape, odd_lower.dtype)
        left_inverse = jnp.concatenate(
            [identity_blocks(edge_shape, odd_lower.dtype), odd_inverse[:, :, :-1]], 2
        )
        left_lower = jnp.concatenate([zero_edge, odd_lower[:, :, :-1]], 2)
        left_upper = jnp.concatenate([zero_edge, odd_upper[:, :, :-1]], 2)
        with_left = block_product(lower_block[:, :, 0::2], left_inverse)
        with_right = block_product(upper_block[:, :, 0::2], odd_inverse)
        center_block = (
            center_block[:, :, 0::2]
            - block_product(with_left, left_upper)
            - block_product(with_right, odd_lower)
        )
        lower_block = -block_product(with_left, left_lower)
        upper_block = -block_product(with_right, odd_upper)
        levels.append((odd_inverse, odd_lower, odd_upper, with_left, with_right))
    return (levels, invert(center_block), points)


def solve_lines(factors, right_side):
    levels, last_inverse, points = factors
    saved_odd = []
    for level_data in levels:
        odd_part = right_side[:, 1::2]
        left_odd = jnp.concatenate([jnp.zeros_like(odd_part[:, :1]), odd_part[:, :-1]], 1)
        right_side = (
            right_side[:, 0::2]
            - block_vector(level_data[3], left_odd)
            - block_vector(level_data[4], odd_part)
        )
        saved_odd.append(odd_part)
    solution = block_vector(last_inverse, right_side)
    for level_data, odd_part in zip(levels[::-1], saved_odd[::-1]):
        right_even = jnp.concatenate([solution[:, 1:], jnp.zeros_like(solution[:, :1])], 1)
        odd_solution = block_vector(
            level_data[0],
            odd_part
            - block_vector(level_data[1], solution)
            - block_vector(level_data[2], right_even),
        )
        solution = jnp.stack([solution, odd_solution], axis=2).reshape(
            solution.shape[0], -1, solution.shape[2]
        )
    return solution


def per_device(visc_wn, conv_wn, spin, visc_az, flux_wn, flux_az, incr_prev, cell_type, edge_index):
    components, points, line_count = visc_wn.shape
    stations = S
    wn_index = lax.axis_index("wn")
    wn_count = lax.axis_size("wn")
    position = wn_index * points + jnp.arange(points, dtype=jnp.int32)
    fluid_mask = (cell_type == 0).astype(jnp.float32)
    energy = (jnp.arange(components) == components - 1).astype(jnp.float32)
    keep_mask = jnp.maximum(fluid_mask[None, :], energy[:, None])
    keep_above = jnp.concatenate([keep_mask[:, 1:], jnp.ones((components, 1), jnp.float32)], 1)
    edge_scale = jnp.where(position[:, None] < edge_index[None, :], 1.0, OUTER_SCALE).astype(
        jnp.float32
    )
    face_visc = visc_wn * edge_scale[None] * (keep_mask * keep_above)[:, :, None]
    face_conv = conv_wn * (keep_mask[:, None] * keep_above[None])[:, :, :, None]
    twist = spin * (keep_mask[:, None] * keep_mask[None])[:, :, :, None]
    wall_rims = from_behind((face_visc[:, -1:], face_conv[:, :, -1:], flux_wn[:, -1:]), "wn", 1)
    visc_below = jnp.concatenate([wall_rims[0], face_visc[:, :-1]], 1)
    conv_below = jnp.concatenate([wall_rims[1], face_conv[:, :, :-1]], 2)
    flux_below = jnp.concatenate([wall_rims[2], flux_wn[:, :-1]], 1)
    azimuth_rims = shifted((visc_az[:, :, -stations:], flux_az[:, :, -stations:]), "az", 1)
    visc_minus = (
        jnp.concatenate([azimuth_rims[0], visc_az[:, :, :-stations]], 2) * keep_mask[:, :, None]
    )
    visc_plus = visc_az * keep_mask[:, :, None]
    flux_minus = jnp.concatenate([azimuth_rims[1], flux_az[:, :, :-stations]], 2)
    azimuthal_diagonal = visc_minus + visc_plus + (1.0 - keep_mask)[:, :, None]
    last_point = jnp.logical_and(wn_index == wn_count - 1, jnp.arange(points) == points - 1)
    upper_valid = jnp.where(last_point, 0.0, 1.0).astype(jnp.float32)
    upper_block = (-diagonal_of(face_visc) + face_conv) * upper_valid[None, None, :, None]
    lower_block = -diagonal_of(visc_below) - jnp.swapaxes(conv_below, 0, 1)
    center_block = (
        diagonal_of(visc_below + face_visc + azimuthal_diagonal) + twist - jnp.swapaxes(twist, 0, 1)
    )
    source = (flux_below - flux_wn + flux_minus - flux_az) * keep_mask[:, :, None]

    def offline(vector):
        padded = with_halo(vector, (("az", 2),), stations, True)
        return visc_minus * padded[:, :, :line_count] + visc_plus * padded[:, :, 2 * stations :]

    moved = (
        lax.all_to_all(lower_block, "wn", split_axis=3, concat_axis=2, tiled=True),
        lax.all_to_all(center_block, "wn", split_axis=3, concat_axis=2, tiled=True),
        lax.all_to_all(upper_block, "wn", split_axis=3, concat_axis=2, tiled=True),
    )
    factors = factor_lines(moved[0], moved[1], moved[2])
    increment = incr_prev
    for sweep_index in range(SWEEPS):
        line_rows = lax.all_to_all(
            source + offline(increment), "wn", split_axis=2, concat_axis=1, tiled=True
        )
        increment = lax.all_to_all(
            solve_lines(factors, line_rows), "wn", split_axis=1, concat_axis=2, tiled=True
        )
    padded_wall = with_halo(increment, (("wn", 1),), 1, False)
    applied = (
        block_vector(center_block, increment)
        + block_vector(lower_block, padded_wall[:, :-2])
        + block_vector(upper_block, padded_wall[:, 2:])
    )
    defect = (source + offline(increment) - applied) / azimuthal_diagonal
    return (increment, defect)


def solution(mesh):
    in_specs = (
        P(None, "wn", "az"),
        P(None, None, "wn", "az"),
        P(None, None, "wn", "az"),
        P(None, "wn", "az"),
        P(None, "wn", "az"),
        P(None, "wn", "az"),
        P(None, "wn", "az"),
        P("wn"),
        P("az"),
    )
    out_specs = (P(None, "wn", "az"), P(None, "wn", "az"))
    return jax.shard_map(
        per_device, mesh=mesh, in_specs=in_specs, out_specs=out_specs, check_vma=False
    )
```

profile of v0, /device:TPU:0, one launch (start us, length us, event | category | flops | bytes accessed | tf_op | source)
XLA Modules:
  0.0 191.3 jit_solution(12630636076469946186)
XLA Ops:
  0.6 0.9 slice.2072
  1.5 2.9 %collective-permute-start.1 = (f32[5,16,8]{2,1,0:T(8,128)S(1)}, f32[5,16,8]{2,1,0:T(8,128)S(1)}, u32[]{:S(2)}, u32[]{:S(2)}) collective-permute-start(f32[5,16,8]{2,1,0:T(8,128)S(1)} %slice.2072), channel_id=1, source_target_pairs={{0,2},{2,4},{4,6},{6,8},{8,10},{10,12},{12,14},{14,16},{16,18},{18... | collective-permute-start | bytes 7688 | tf_op jit(solution)/shard_map/ppermute | solution.py:22
  6.1 1.0 multiply_multiply_fusion
  7.1 1.2 add_multiply_fusion
  8.3 3.1 %copy.602 = f32[5,5,16,256]{2,0,1,3:T(8,128)} copy(f32[5,5,16,256]{3,2,1,0:T(8,128)S(1)} %get-tuple-element.680) | data formatting | bytes 819200 | tf_op jit(solution)/shard_map/mul | solution.py:164
  11.4 4.0 %reshape.2997 = f32[2,1,51200]{2,1,0:T(1,128)} reshape(f32[256,5,5,16]{3,2,1,0:T(8,128)} %bitcast.363) | data formatting | bytes 819200
  15.4 3.5 %all-to-all-start.2 = ((f32[2,1,51200]{2,1,0:T(1,128)}), f32[2,1,51200]{2,1,0:T(1,128)S(1)}, u32[]{:S(2)}, u32[]{:S(2)}) async-start(f32[2,1,51200]{2,1,0:T(1,128)} %reshape.2997), calls=%async_computation.2 | async-start | bytes 819200 | tf_op jit(solution)/shard_map/all_to_all | solution.py:178
  19.0 4.0 %collective-permute-start.6 = (f32[5,16,8]{2,1,0:T(8,128)S(1)}, f32[5,16,8]{2,1,0:T(8,128)S(1)}, u32[]{:S(2)}, u32[]{:S(2)}) collective-permute-start(f32[5,16,8]{2,1,0:T(8,128)S(1)} %get-tuple-element.693), channel_id=1, source_target_pairs={{2,0},{4,2},{6,4},{8,6},{10,8},{12,10},{14,12},{16,14},{18,16},{20... | collective-permute-start | bytes 7688 | tf_op jit(solution)/shard_map/ppermute | solution.py:33
  23.5 1.7 collective-permute-start.3
  25.3 0.9 copy_multiply_fusion
  26.8 1.9 %reduce.127 = f32[2,51200]{1,0:T(2,128)S(1)} reduce(f32[2,1,51200]{2,1,0:T(1,128)S(1)} %all-to-all-done.2, f32[]{:T(128)} %broadcast.1956), dimensions={1}, to_apply=%all_to_all.99.reduce_sub_computation | reduce | bytes 819204 | tf_op jit(solution)/shard_map/all_to_all | solution.py:178
  28.7 4.2 %reshape.2998 = f32[256,5,5,16]{3,2,1,0:T(8,128)} reshape(f32[2,51200]{1,0:T(2,128)S(1)} %reduce.127) | data formatting | bytes 819200
  32.9 4.3 %copy.634 = f32[5,5,16,2,128]{4,3,2,1,0:T(2,128)S(1)} copy(f32[5,5,16,2,128]{2,0,1,4,3:T(8,128)} %bitcast.360) | data formatting | bytes 819200 | tf_op jit(solution)/shard_map/all_to_all | solution.py:178
  37.4 1.9 slice.2102
  40.0 1.3 collective-permute-start
  41.3 1.3 collective-permute-start.2
  43.9 1.0 reshape.3001
  44.9 3.3 %all-to-all-start.3 = ((f32[2,1,10240]{2,1,0:T(1,128)}), f32[2,1,10240]{2,1,0:T(1,128)S(1)}, u32[]{:S(2)}, u32[]{:S(2)}) async-start(f32[2,1,10240]{2,1,0:T(1,128)} %reshape.3001), calls=%async_computation.3 | async-start | bytes 163840 | tf_op jit(solution)/shard_map/all_to_all | solution.py:183
  48.3 1.3 all-to-all-done.3
  49.6 0.9 reduce.129
  53.0 1.3 fusion
  54.3 3.1 %copy.594 = f32[5,5,16,256]{2,0,1,3:T(8,128)} copy(f32[5,5,16,256]{3,2,1,0:T(8,128)S(1)} %get-tuple-element.779) | data formatting | bytes 819200 | tf_op jit(solution)/shard_map/sub | solution.py:167
  57.4 3.4 %reshape.2995 = f32[2,1,51200]{2,1,0:T(1,128)S(1)} reshape(f32[256,5,5,16]{3,2,1,0:T(8,128)} %bitcast.364) | data formatting | bytes 819200
  60.8 4.0 %all_to_all.126 = f32[2,1,51200]{2,1,0:T(1,128)S(1)} all-to-all(f32[2,1,51200]{2,1,0:T(1,128)S(1)} %reshape.2995), channel_id=1, replica_groups=mesh['az'=16,'wn'=2] {'wn'}, dimensions={0} | all-to-all | bytes 819200 | tf_op jit(solution)/shard_map/all_to_all | solution.py:177
  64.8 1.9 reduce.126
  66.7 4.2 %reshape.2996 = f32[256,5,5,16]{3,2,1,0:T(8,128)} reshape(f32[2,51200]{1,0:T(2,128)S(1)} %reduce.126) | data formatting | bytes 819200
  70.9 3.0 %copy.595 = f32[5,5,16,2,128]{4,2,3,1,0:T(8,128)S(1)} copy(f32[5,5,16,2,128]{2,0,1,4,3:T(8,128)} %bitcast.361) | data formatting | bytes 819200 | tf_op jit(solution)/shard_map/all_to_all | solution.py:177
  74.7 3.1 %copy.599 = f32[5,5,16,256]{2,1,0,3:T(8,128)} copy(f32[5,5,16,256]{3,2,1,0:T(8,128)S(1)} %get-tuple-element.778) | data formatting | bytes 819200 | tf_op jit(solution)/shard_map/sub | solution.py:165
  77.8 3.4 %reshape.2999 = f32[2,1,51200]{2,1,0:T(1,128)S(1)} reshape(f32[256,5,5,16]{3,2,1,0:T(8,128)} %bitcast.365) | data formatting | bytes 819200
  81.2 4.0 %all_to_all.127 = f32[2,1,51200]{2,1,0:T(1,128)S(1)} all-to-all(f32[2,1,51200]{2,1,0:T(1,128)S(1)} %reshape.2999), channel_id=1, replica_groups=mesh['az'=16,'wn'=2] {'wn'}, dimensions={0} | all-to-all | bytes 819200 | tf_op jit(solution)/shard_map/all_to_all | solution.py:176
  85.2 1.9 reduce.128
  87.1 4.2 %reshape.3000 = f32[256,5,5,16]{3,2,1,0:T(8,128)} reshape(f32[2,51200]{1,0:T(2,128)S(1)} %reduce.128) | data formatting | bytes 819200
  91.3 4.5 %copy.633 = f32[5,5,16,2,128]{4,3,2,1,0:T(2,128)S(1)} copy(f32[5,5,16,2,128]{2,1,0,4,3:T(8,128)} %bitcast.362) | data formatting | bytes 819200 | tf_op jit(solution)/shard_map/all_to_all | solution.py:176
  96.0 1.9 slice.2077
  98.1 1.0 multiply_subtract_fusion
  100.1 1.0 multiply_reduce_fusion.5
  101.1 1.4 multiply_reduce_fusion
  109.5 1.9 slice.2183
  111.4 1.8 slice.2158
  121.0 0.8 multiply_reduce_fusion.29
  121.8 1.4 subtract_subtract_fusion.6
  124.0 1.4 slice.2238
  130.8 3.8 %all_to_all.128 = f32[5,32,128]{2,0,1:T(8,128)S(1)} all-to-all(f32[5,32,128]{2,0,1:T(8,128)S(1)} %copy.613), channel_id=1, replica_groups=mesh['az'=16,'wn'=2] {'wn'}, dimensions={1} | all-to-all | bytes 163840 | tf_op jit(solution)/shard_map/all_to_all | solution.py:186
  134.9 5.3 %collective-permute-start.8 = (f32[5,16,8]{2,1,0:T(8,128)S(1)}, f32[5,16,8]{2,1,0:T(8,128)S(1)}, u32[]{:S(2)}, u32[]{:S(2)}) collective-permute-start(f32[5,16,8]{2,1,0:T(8,128)S(1)} %get-tuple-element.691), channel_id=1, source_target_pairs={{2,0},{4,2},{6,4},{8,6},{10,8},{12,10},{14,12},{16,14},{18,16},{20... | collective-permute-start | bytes 7688 | tf_op jit(solution)/shard_map/ppermute | solution.py:33
  140.2 1.7 collective-permute-done.8
  141.9 5.9 %collective-permute-done.7 = f32[5,16,8]{2,1,0:T(8,128)S(1)} collective-permute-done((f32[5,16,8]{2,1,0:T(8,128)S(1)}, f32[5,16,8]{2,1,0:T(8,128)S(1)}, u32[]{:S(2)}, u32[]{:S(2)}) %collective-permute-start.7) | collective-permute-done | bytes 2592 | tf_op jit(solution)/shard_map/ppermute | solution.py:32
  148.7 1.3 copy.616
  150.0 1.0 reshape.3003
  151.0 4.7 %all_to_all.129 = f32[2,1,10240]{2,1,0:T(1,128)S(1)} all-to-all(f32[2,1,10240]{2,1,0:T(1,128)} %reshape.3003), channel_id=1, replica_groups=mesh['az'=16,'wn'=2] {'wn'}, dimensions={0} | all-to-all | bytes 163840 | tf_op jit(solution)/shard_map/all_to_all | solution.py:183
  155.7 1.5 reduce.130
  157.2 1.2 reshape.3004
  158.4 0.9 copy.637
  159.3 0.9 copy.618
  160.4 0.9 multiply_reduce_fusion.40
  161.3 0.9 multiply_reduce_fusion.41
  172.0 0.8 multiply_reduce_fusion.50
  172.8 0.9 multiply_reduce_fusion.39
  173.8 0.9 multiply_reduce_fusion.37
  175.0 3.8 %all_to_all.130 = f32[5,32,128]{2,0,1:T(8,128)S(1)} all-to-all(f32[5,32,128]{2,0,1:T(8,128)S(1)} %copy.624), channel_id=1, replica_groups=mesh['az'=16,'wn'=2] {'wn'}, dimensions={1} | all-to-all | bytes 163840 | tf_op jit(solution)/shard_map/all_to_all | solution.py:186
  179.1 2.1 %collective-permute-start.11 = (f32[5,1,256]{2,1,0:T(1,128)S(1)}, f32[5,1,256]{2,1,0:T(1,128)S(1)}, u32[]{:S(2)}, u32[]{:S(2)}) collective-permute-start(f32[5,1,256]{2,1,0:T(1,128)S(1)} %get-tuple-element.686), channel_id=1, source_target_pairs={{0,1},{2,3},{4,5},{6,7},{8,9},{10,11},{12,13},{14,15},{16,17},{18,... | collective-permute-start | bytes 15368 | tf_op jit(solution)/shard_map/ppermute | solution.py:32
  181.2 1.3 collective-permute-start.12
  182.6 2.0 %collective-permute-start.9 = (f32[5,16,8]{2,1,0:T(8,128)S(1)}, f32[5,16,8]{2,1,0:T(8,128)S(1)}, u32[]{:S(2)}, u32[]{:S(2)}) collective-permute-start(f32[5,16,8]{2,1,0:T(8,128)S(1)} %get-tuple-element.688), channel_id=1, source_target_pairs={{0,2},{2,4},{4,6},{6,8},{8,10},{10,12},{12,14},{14,16},{16,18},{18... | collective-permute-start | bytes 7688 | tf_op jit(solution)/shard_map/ppermute | solution.py:32
  184.7 2.1 %collective-permute-done.10 = f32[5,16,8]{2,1,0:T(8,128)S(1)} collective-permute-done((f32[5,16,8]{2,1,0:T(8,128)S(1)}, f32[5,16,8]{2,1,0:T(8,128)S(1)}, u32[]{:S(2)}, u32[]{:S(2)}) %collective-permute-start.10) | collective-permute-done | bytes 2592 | tf_op jit(solution)/shard_map/ppermute | solution.py:33
  186.9 3.7 %collective-permute-done.9 = f32[5,16,8]{2,1,0:T(8,128)S(1)} collective-permute-done((f32[5,16,8]{2,1,0:T(8,128)S(1)}, f32[5,16,8]{2,1,0:T(8,128)S(1)}, u32[]{:S(2)}, u32[]{:S(2)}) %collective-permute-start.9) | collective-permute-done | bytes 2592 | tf_op jit(solution)/shard_map/ppermute | solution.py:32
  (519 shorter events, 40.9 us)
Async XLA Ops:
  1.5 38.5 %collective-permute-start.1 = (f32[5,16,8]{2,1,0:T(8,128)S(1)}, f32[5,16,8]{2,1,0:T(8,128)S(1)}, u32[]{:S(2)}, u32[]{:S(2)}) collective-permute-start(f32[5,16,8]{2,1,0:T(8,128)S(1)} %slice.2072), channel_id=1, source_target_pairs={{0,2},{2,4},{4,6},{6,8},{8,10},{10,12},{12,14},{14,16},{16,18},{18... | collective-permute-start | bytes 7688 | tf_op jit(solution)/shard_map/ppermute | solution.py:22
  8.2 10.7 %copy-start.29 = (f32[5,16,256]{2,1,0:T(8,128)S(1)}, f32[5,16,256]{2,1,0:T(8,128)}, u32[]{:S(2)}) copy-start(f32[5,16,256]{2,1,0:T(8,128)} %param.123) | copy-start | bytes 245764
  8.3 14.8 %copy-start.22 = (f32[5,16,256]{2,1,0:T(8,128)S(1)}, f32[5,16,256]{2,1,0:T(8,128)}, u32[]{:S(2)}) copy-start(f32[5,16,256]{2,1,0:T(8,128)} %param.122) | copy-start | bytes 245764
  8.3 15.2 %copy-start.26 = (f32[5,16,256]{2,1,0:T(8,128)S(1)}, f32[5,16,256]{2,1,0:T(8,128)}, u32[]{:S(2)}) copy-start(f32[5,16,256]{2,1,0:T(8,128)} %param.121) | copy-start | bytes 245764
  8.3 17.0 %copy-start.23 = (f32[5,5,16,256]{3,2,1,0:T(8,128)S(1)}, f32[5,5,16,256]{3,2,1,0:T(8,128)}, u32[]{:S(2)}) copy-start(f32[5,5,16,256]{3,2,1,0:T(8,128)} %param.119) | copy-start | bytes 1228804
  15.4 10.7 %all-to-all-start.2 = ((f32[2,1,51200]{2,1,0:T(1,128)}), f32[2,1,51200]{2,1,0:T(1,128)S(1)}, u32[]{:S(2)}, u32[]{:S(2)}) async-start(f32[2,1,51200]{2,1,0:T(1,128)} %reshape.2997), calls=%async_computation.2 | async-start | bytes 819200 | tf_op jit(solution)/shard_map/all_to_all | solution.py:178
  19.0 22.3 %collective-permute-start.6 = (f32[5,16,8]{2,1,0:T(8,128)S(1)}, f32[5,16,8]{2,1,0:T(8,128)S(1)}, u32[]{:S(2)}, u32[]{:S(2)}) collective-permute-start(f32[5,16,8]{2,1,0:T(8,128)S(1)} %get-tuple-element.693), channel_id=1, source_target_pairs={{2,0},{4,2},{6,4},{8,6},{10,8},{12,10},{14,12},{16,14},{18,16},{20... | collective-permute-start | bytes 7688 | tf_op jit(solution)/shard_map/ppermute | solution.py:33
  23.0 19.6 %collective-permute-start.5 = (f32[5,16,8]{2,1,0:T(8,128)S(1)}, f32[5,16,8]{2,1,0:T(8,128)S(1)}, u32[]{:S(2)}, u32[]{:S(2)}) collective-permute-start(f32[5,16,8]{2,1,0:T(8,128)S(1)} %get-tuple-element.692), channel_id=1, source_target_pairs={{0,2},{2,4},{4,6},{6,8},{8,10},{10,12},{12,14},{14,16},{16,18},{18... | collective-permute-start | bytes 7688 | tf_op jit(solution)/shard_map/ppermute | solution.py:32
  23.1 19.5 %collective-permute-start.4 = (f32[5,16,8]{2,1,0:T(8,128)S(1)}, f32[5,16,8]{2,1,0:T(8,128)S(1)}, u32[]{:S(2)}, u32[]{:S(2)}) collective-permute-start(f32[5,16,8]{2,1,0:T(8,128)S(1)} %slice.2229), channel_id=1, source_target_pairs={{0,2},{2,4},{4,6},{6,8},{8,10},{10,12},{12,14},{14,16},{16,18},{18... | collective-permute-start | bytes 7688 | tf_op jit(solution)/shard_map/ppermute | solution.py:22
  23.5 19.1 %collective-permute-start.3 = (f32[5,1,256]{2,1,0:T(1,128)S(1)}, f32[5,1,256]{2,1,0:T(1,128)S(1)}, u32[]{:S(2)}, u32[]{:S(2)}) collective-permute-start(f32[5,1,256]{2,1,0:T(1,128)S(1)} %slice.2227), channel_id=1, source_target_pairs={{0,1},{2,3},{4,5},{6,7},{8,9},{10,11},{12,13},{14,15},{16,17},{18,... | collective-permute-start | bytes 15368 | tf_op jit(solution)/shard_map/ppermute | solution.py:16
  32.9 9.8 %copy-start = (f32[5,16,256]{2,1,0:T(8,128)S(1)}, f32[5,16,256]{2,1,0:T(8,128)}, u32[]{:S(2)}) copy-start(f32[5,16,256]{2,1,0:T(8,128)} %param.120) | copy-start | bytes 245764
  32.9 15.3 %copy-start.27 = (f32[5,16,256]{2,1,0:T(8,128)S(1)}, f32[5,16,256]{2,1,0:T(8,128)}, u32[]{:S(2)}) copy-start(f32[5,16,256]{2,1,0:T(8,128)} %param.117) | copy-start | bytes 245764
  40.0 17.4 %copy-start.14 = (f32[5,16,8]{2,1,0:T(8,128)}, f32[5,16,8]{2,1,0:T(8,128)S(1)}, u32[]{:S(2)}) copy-start(f32[5,16,8]{2,1,0:T(8,128)S(1)} %collective-permute-done.1) | copy-start | bytes 7684
  40.0 8.2 %collective-permute-start = (f32[5,1,256]{2,1,0:T(1,128)S(1)}, f32[5,1,256]{2,1,0:T(1,128)S(1)}, u32[]{:S(2)}, u32[]{:S(2)}) collective-permute-start(f32[5,1,256]{2,1,0:T(1,128)S(1)} %slice.2284), channel_id=1, source_target_pairs={{0,1},{2,3},{4,5},{6,7},{8,9},{10,11},{12,13},{14,15},{16,17},{18,... | collective-permute-start | bytes 15368 | tf_op jit(solution)/shard_map/ppermute | solution.py:16
  41.3 11.1 %collective-permute-start.2 = (f32[5,5,1,256]{3,2,1,0:T(1,128)S(1)}, f32[5,5,1,256]{3,2,1,0:T(1,128)S(1)}, u32[]{:S(2)}, u32[]{:S(2)}) collective-permute-start(f32[5,5,1,256]{3,2,1,0:T(1,128)S(1)} %slice.2286), channel_id=1, source_target_pairs={{0,1},{2,3},{4,5},{6,7},{8,9},{10,11},{12,13},{14,15},{16,17},{18,... | collective-permute-start | bytes 76808 | tf_op jit(solution)/shard_map/ppermute | solution.py:16
  44.9 4.7 %all-to-all-start.3 = ((f32[2,1,10240]{2,1,0:T(1,128)}), f32[2,1,10240]{2,1,0:T(1,128)S(1)}, u32[]{:S(2)}, u32[]{:S(2)}) async-start(f32[2,1,10240]{2,1,0:T(1,128)} %reshape.3001), calls=%async_computation.3 | async-start | bytes 163840 | tf_op jit(solution)/shard_map/all_to_all | solution.py:183
  51.1 9.7 %copy-start.17 = (f32[5,16,128]{2,1,0:T(8,128)}, f32[5,16,128]{2,1,0:T(8,128)S(1)}, u32[]{:S(2)}) copy-start(f32[5,16,128]{2,1,0:T(8,128)S(1)} %slice.2236) | copy-start | bytes 122884
  52.4 0.6 copy-start.35
  74.7 23.4 %copy-start.8 = (f32[5,5,16,128]{3,2,1,0:T(8,128)}, f32[5,5,16,128]{3,2,1,0:T(8,128)S(1)}, u32[]{:S(2)}) copy-start(f32[5,5,16,128]{3,2,1,0:T(8,128)S(1)} %get-tuple-element.723) | copy-start | bytes 614404
  91.3 8.5 %copy-start.9 = (f32[5,5,16,128]{3,2,1,0:T(8,128)S(1)}, f32[5,5,16,128]{3,2,1,0:T(8,128)}, u32[]{:S(2)}) copy-start(f32[5,5,16,128]{3,2,1,0:T(8,128)} %slice.2102) | copy-start | bytes 614404
  103.8 26.6 %copy-start.1 = (f32[5,5,8,128]{3,2,1,0:T(8,128)}, f32[5,5,8,128]{3,2,1,0:T(8,128)S(1)}, u32[]{:S(2)}) copy-start(f32[5,5,8,128]{3,2,1,0:T(8,128)S(1)} %slice.2130) | copy-start | bytes 307204
  103.9 17.0 %copy-start.18 = (f32[5,16,128]{2,1,0:T(8,128)S(1)}, f32[5,16,128]{2,1,0:T(8,128)}, u32[]{:S(2)}) copy-start(f32[5,16,128]{2,1,0:T(8,128)} %copy-done.17) | copy-start | bytes 122884
  104.0 26.5 %copy-start.2 = (f32[5,5,8,128]{3,2,1,0:T(8,128)}, f32[5,5,8,128]{3,2,1,0:T(8,128)S(1)}, u32[]{:S(2)}) copy-start(f32[5,5,8,128]{3,2,1,0:T(8,128)S(1)} %fusion.49) | copy-start | bytes 307204
  104.1 21.3 %copy-start.4 = (f32[5,5,8,128]{3,2,1,0:T(8,128)}, f32[5,5,8,128]{3,2,1,0:T(8,128)S(1)}, u32[]{:S(2)}) copy-start(f32[5,5,8,128]{3,2,1,0:T(8,128)S(1)} %multiply_reduce_fusion.9) | copy-start | bytes 307204
  104.2 25.9 %copy-start.5 = (f32[5,5,8,128]{3,2,1,0:T(8,128)}, f32[5,5,8,128]{3,2,1,0:T(8,128)S(1)}, u32[]{:S(2)}) copy-start(f32[5,5,8,128]{3,2,1,0:T(8,128)S(1)} %multiply_reduce_fusion.11) | copy-start | bytes 307204
  105.8 28.9 %copy-start.6 = (f32[5,5,4,128]{3,2,1,0:T(4,128)}, f32[5,5,4,128]{3,2,1,0:T(4,128)S(1)}, u32[]{:S(2)}) copy-start(f32[5,5,4,128]{3,2,1,0:T(4,128)S(1)} %slice.2157) | copy-start | bytes 153604
  106.1 28.7 %copy-start.7 = (f32[5,5,4,128]{3,2,1,0:T(4,128)}, f32[5,5,4,128]{3,2,1,0:T(4,128)S(1)}, u32[]{:S(2)}) copy-start(f32[5,5,4,128]{3,2,1,0:T(4,128)S(1)} %constant_dynamic-update-slice_fusion.27) | copy-start | bytes 153604
  106.2 41.7 %copy-start.10 = (f32[5,5,4,128]{3,2,1,0:T(4,128)}, f32[5,5,4,128]{3,2,1,0:T(4,128)S(1)}, u32[]{:S(2)}) copy-start(f32[5,5,4,128]{3,2,1,0:T(4,128)S(1)} %multiply_reduce_fusion.18) | copy-start | bytes 153604
  106.2 41.7 %copy-start.12 = (f32[5,16,256]{2,1,0:T(8,128)S(1)}, f32[5,16,256]{2,1,0:T(8,128)}, u32[]{:S(2)}) copy-start(f32[5,16,256]{2,1,0:T(8,128)} %get-tuple-element.679) | copy-start | bytes 245764
  106.2 41.7 %copy-start.15 = (f32[5,16,8]{2,1,0:T(8,128)S(1)}, f32[5,16,8]{2,1,0:T(8,128)}, u32[]{:S(2)}) copy-start(f32[5,16,8]{2,1,0:T(8,128)} %copy-done.14) | copy-start | bytes 7684
  107.1 40.8 %copy-start.11 = (f32[5,5,4,128]{3,2,1,0:T(4,128)}, f32[5,5,4,128]{3,2,1,0:T(4,128)S(1)}, u32[]{:S(2)}) copy-start(f32[5,5,4,128]{3,2,1,0:T(4,128)S(1)} %multiply_reduce_fusion.20) | copy-start | bytes 153604
  107.9 0.6 copy-start.32
  109.5 20.9 %copy-start.20 = (f32[5,5,2,128]{3,2,1,0:T(2,128)}, f32[5,5,2,128]{3,2,1,0:T(2,128)S(1)}, u32[]{:S(2)}) copy-start(f32[5,5,2,128]{3,2,1,0:T(2,128)S(1)} %slice.2181) | copy-start | bytes 76804
  113.4 17.3 %copy-start.21 = (f32[5,5,2,128]{3,2,1,0:T(2,128)}, f32[5,5,2,128]{3,2,1,0:T(2,128)S(1)}, u32[]{:S(2)}) copy-start(f32[5,5,2,128]{3,2,1,0:T(2,128)S(1)} %slice.2184) | copy-start | bytes 76804
  115.7 14.7 %copy-start.19 = (f32[5,5,2,128]{3,2,1,0:T(2,128)}, f32[5,5,2,128]{3,2,1,0:T(2,128)S(1)}, u32[]{:S(2)}) copy-start(f32[5,5,2,128]{3,2,1,0:T(2,128)S(1)} %constant_dynamic-update-slice_fusion.18) | copy-start | bytes 76804
  116.6 14.2 %copy-start.24 = (f32[5,5,2,128]{3,2,1,0:T(2,128)}, f32[5,5,2,128]{3,2,1,0:T(2,128)S(1)}, u32[]{:S(2)}) copy-start(f32[5,5,2,128]{3,2,1,0:T(2,128)S(1)} %multiply_reduce_fusion.34) | copy-start | bytes 76804
  116.9 13.9 %copy-start.25 = (f32[5,5,2,128]{3,2,1,0:T(2,128)}, f32[5,5,2,128]{3,2,1,0:T(2,128)S(1)}, u32[]{:S(2)}) copy-start(f32[5,5,2,128]{3,2,1,0:T(2,128)S(1)} %multiply_reduce_fusion.36) | copy-start | bytes 76804
  118.6 12.1 %copy-start.31 = (f32[5,5,1,128]{3,2,1,0:T(1,128)}, f32[5,5,1,128]{3,2,1,0:T(1,128)S(1)}, u32[]{:S(2)}) copy-start(f32[5,5,1,128]{3,2,1,0:T(1,128)S(1)} %constant_dynamic-update-slice_fusion.9) | copy-start | bytes 38404
  118.6 11.7 %copy-start.30 = (f32[5,5,2,128]{3,2,1,0:T(2,128)}, f32[5,5,2,128]{3,2,1,0:T(2,128)S(1)}, u32[]{:S(2)}) copy-start(f32[5,5,2,128]{3,2,1,0:T(2,128)S(1)} %neg.38) | copy-start | bytes 76804
  119.6 28.3 %copy-start.28 = (f32[5,5,128]{2,1,0:T(8,128)}, f32[5,5,128]{2,1,0:T(8,128)S(1)}, u32[]{:S(2)}) copy-start(f32[5,5,128]{2,1,0:T(8,128)S(1)} %multiply_reduce_fusion.48) | copy-start | bytes 38404
  120.9 6.0 %copy-start.36 = (f32[128]{0:T(128)}, f32[128]{0:T(128)S(1)}, u32[]{:S(2)}) copy-start(f32[128]{0:T(128)S(1)} %fusion.92) | copy-start | bytes 1540
  129.1 1.1 copy-start.33
  130.4 37.5 %copy-start.34 = (f32[5,128]{1,0:T(8,128)S(1)}, f32[5,128]{1,0:T(8,128)}, u32[]{:S(2)}) copy-start(f32[5,128]{1,0:T(8,128)} %get-tuple-element.702) | copy-start | bytes 7684
  134.9 7.0 %collective-permute-start.8 = (f32[5,16,8]{2,1,0:T(8,128)S(1)}, f32[5,16,8]{2,1,0:T(8,128)S(1)}, u32[]{:S(2)}, u32[]{:S(2)}) collective-permute-start(f32[5,16,8]{2,1,0:T(8,128)S(1)} %get-tuple-element.691), channel_id=1, source_target_pairs={{2,0},{4,2},{6,4},{8,6},{10,8},{12,10},{14,12},{16,14},{18,16},{20... | collective-permute-start | bytes 7688 | tf_op jit(solution)/shard_map/ppermute | solution.py:33
  140.2 7.6 %collective-permute-start.7 = (f32[5,16,8]{2,1,0:T(8,128)S(1)}, f32[5,16,8]{2,1,0:T(8,128)S(1)}, u32[]{:S(2)}, u32[]{:S(2)}) collective-permute-start(f32[5,16,8]{2,1,0:T(8,128)S(1)} %get-tuple-element.690), channel_id=1, source_target_pairs={{0,2},{2,4},{4,6},{6,8},{8,10},{10,12},{12,14},{14,16},{16,18},{18... | collective-permute-start | bytes 7688 | tf_op jit(solution)/shard_map/ppermute | solution.py:32
  159.3 31.2 %copy-start.13 = (f32[5,16,256]{2,1,0:T(8,128)S(1)}, f32[5,16,256]{2,1,0:T(8,128)}, u32[]{:S(2)}) copy-start(f32[5,16,256]{2,1,0:T(8,128)} %get-tuple-element.679) | copy-start | bytes 245764
  159.3 31.2 %copy-start.16 = (f32[5,16,8]{2,1,0:T(8,128)S(1)}, f32[5,16,8]{2,1,0:T(8,128)}, u32[]{:S(2)}) copy-start(f32[5,16,8]{2,1,0:T(8,128)} %copy-done.14) | copy-start | bytes 7684
  179.0 12.3 %copy-start.3 = (f32[5,16,256]{2,1,0:T(8,128)}, f32[5,16,256]{2,1,0:T(8,128)S(1)}, u32[]{:S(2)}) copy-start(f32[5,16,256]{2,1,0:T(8,128)S(1)} %all_to_all.118) | copy-start | bytes 245764
  179.1 5.5 %collective-permute-start.11 = (f32[5,1,256]{2,1,0:T(1,128)S(1)}, f32[5,1,256]{2,1,0:T(1,128)S(1)}, u32[]{:S(2)}, u32[]{:S(2)}) collective-permute-start(f32[5,1,256]{2,1,0:T(1,128)S(1)} %get-tuple-element.686), channel_id=1, source_target_pairs={{0,1},{2,3},{4,5},{6,7},{8,9},{10,11},{12,13},{14,15},{16,17},{18,... | collective-permute-start | bytes 15368 | tf_op jit(solution)/shard_map/ppermute | solution.py:32
  181.2 3.4 %collective-permute-start.12 = (f32[5,1,256]{2,1,0:T(1,128)S(1)}, f32[5,1,256]{2,1,0:T(1,128)S(1)}, u32[]{:S(2)}, u32[]{:S(2)}) collective-permute-start(f32[5,1,256]{2,1,0:T(1,128)S(1)} %get-tuple-element.687), channel_id=1, source_target_pairs={{1,0},{3,2},{5,4},{7,6},{9,8},{11,10},{13,12},{15,14},{17,16},{19,... | collective-permute-start | bytes 15368 | tf_op jit(solution)/shard_map/ppermute | solution.py:33
  182.5 4.3 %collective-permute-start.10 = (f32[5,16,8]{2,1,0:T(8,128)S(1)}, f32[5,16,8]{2,1,0:T(8,128)S(1)}, u32[]{:S(2)}, u32[]{:S(2)}) collective-permute-start(f32[5,16,8]{2,1,0:T(8,128)S(1)} %get-tuple-element.689), channel_id=1, source_target_pairs={{2,0},{4,2},{6,4},{8,6},{10,8},{12,10},{14,12},{16,14},{18,16},{20... | collective-permute-start | bytes 7688 | tf_op jit(solution)/shard_map/ppermute | solution.py:33
  182.6 7.9 %collective-permute-start.9 = (f32[5,16,8]{2,1,0:T(8,128)S(1)}, f32[5,16,8]{2,1,0:T(8,128)S(1)}, u32[]{:S(2)}, u32[]{:S(2)}) collective-permute-start(f32[5,16,8]{2,1,0:T(8,128)S(1)} %get-tuple-element.688), channel_id=1, source_target_pairs={{0,2},{2,4},{4,6},{6,8},{8,10},{10,12},{12,14},{14,16},{16,18},{18... | collective-permute-start | bytes 7688 | tf_op jit(solution)/shard_map/ppermute | solution.py:32
where the time goes:
time: 194 us; the launch traced here: 191 us
  local copies, waits for them, and re-layouts  71.8 us (37%)
  other arithmetic  51.6 us (27%)
  starting transfers between devices  29.2 us (15%)
  blocking collectives  20.5 us (11%)
  waiting for transfers between devices  14.7 us (8%)
  between operations  3.63 us (2%)
    unnamed x120, local copies, waits for them, and re-layouts  28.3 us
    reduce_sum x51, other arithmetic, block_vector(): return jnp.sum(matrix * vector[None], axis=1)  15.9 us
    ppermute x4, starting transfers between devices, with_halo(): after = lax.ppermute(leading, axis, down)  10.7 us
    ppermute x4, waiting for transfers between devices, with_halo(): before = lax.ppermute(last, axis, up)  9.59 us
    all_to_all x2, blocking collectives, per_device(): lax.all_to_all(solve_lines(factors, line_rows), 'wn', split_axis=1, conca...  7.68 us
    reduce_sum x19, other arithmetic, block_product(): return jnp.sum(matrix[:, :, None] * operand[None], axis=1)  5.09 us
    all_to_all x1, blocking collectives, per_device(): lax.all_to_all(source + offline(increment), 'wn', split_axis=2, concat_ax...  4.73 us
    all_to_all x2, local copies, waits for them, and re-layouts, per_device(): lax.all_to_all(lower_block, 'wn', split_axis=3, concat_axis=2, tiled=True)  4.54 us
  transfers between devices with their start and end apart: 15, of which 5 were waited for; matrix products, arithmetic and copies ran while one was open for 16% of the time, Pallas kernels for 0%

commit v1 on v0

v1 whole, which is shorter than its diff:
```python
import jax
import jax.numpy as jnp
from jax import lax
from jax.experimental import pallas as pl
from jax.experimental.pallas import tpu as pltpu
from jax.sharding import PartitionSpec as P

S = 8
SWEEPS = 2
OUTER_SCALE = 0.25
NC = 5
LANES = 128
SUB = 8
NEAR = 2 * S
FAR = 3 * S

CONV, SKEW, VISC, FLUX, EDGE = 0, 25, 35, 40, 45
NEAR_VALUES = 46
VAZ, FAZ, INC = 46, 51, 56
VALUES = 61
NEAR_SLOTS = LANES // NEAR
FAR_SLOTS = LANES // FAR
NEAR_PACKS = -(-NEAR_VALUES // NEAR_SLOTS)
FAR_PACKS = -(-(VALUES - NEAR_VALUES) // FAR_SLOTS)
PACKS = NEAR_PACKS + FAR_PACKS
PAIRS = [(a, b) for a in range(NC) for b in range(a + 1, NC)]


def slot_of(value):
    if value < NEAR_VALUES:
        return value // NEAR_SLOTS, value % NEAR_SLOTS, NEAR
    other = value - NEAR_VALUES
    return NEAR_PACKS + other // FAR_SLOTS, other % FAR_SLOTS, FAR


def tile_reader(visc, conv, spin, vaz, flux, faz, inc, edge):
    def read(value, t, lt):
        rows, lanes = pl.ds(SUB * t, SUB), pl.ds(LANES * lt, LANES)
        if value < SKEW:
            return conv[value, rows, lanes]
        if value < VISC:
            a, b = PAIRS[value - SKEW]
            return spin[a * NC + b, rows, lanes] - spin[b * NC + a, rows, lanes]
        if value == EDGE:
            return jnp.broadcast_to(edge[0:1, lanes].astype(jnp.float32), (SUB, LANES))
        for first, ref in ((VISC, visc), (FLUX, flux), (VAZ, vaz), (FAZ, faz), (INC, inc)):
            if first <= value < first + NC:
                return ref[value - first, rows, lanes]

    return read


def pack_kernel(visc, conv, spin, vaz, flux, faz, inc, edge, even_out, odd_out):
    odd_place = lax.rem(lax.axis_index("az"), 2) == 1
    read = tile_reader(visc, conv, spin, vaz, flux, faz, inc, edge)
    lane = lax.broadcasted_iota(jnp.int32, (SUB, LANES), 1)
    for t in range(2):
        first = [jnp.zeros((SUB, LANES), jnp.float32)] * PACKS
        last = [jnp.zeros((SUB, LANES), jnp.float32)] * PACKS
        for value in range(VALUES):
            pack, slot, width = slot_of(value)
            low = slot * width
            here = (lane >= low) & (lane < low + width)
            low = (LANES - width + slot * width) % LANES
            there = (lane >= low) & (lane < low + width)
            one, two = read(value, t, 0), read(value, t, 1)
            if slot:
                one, two = pltpu.roll(one, slot * width, 1), pltpu.roll(two, slot * width, 1)
            first[pack] = jnp.where(here, one, first[pack])
            last[pack] = jnp.where(there, two, last[pack])
        rows = pl.ds(SUB * t, SUB)
        for pack in range(PACKS):
            even_out[pack, rows, :] = jnp.where(odd_place, first[pack], last[pack])
            odd_out[pack, rows, :] = jnp.where(odd_place, last[pack], first[pack])


def factor(matrix):
    work = [list(row) for row in matrix]
    scale = []
    for p in range(NC):
        scale.append(1.0 / work[p][p])
        for i in range(p + 1, NC):
            work[i][p] = work[i][p] * scale[p]
            for j in range(p + 1, NC):
                work[i][j] = work[i][j] - work[i][p] * work[p][j]
    for p in range(NC):
        work[p][p] = scale[p]
    return work


def substitute(work, side):
    side = list(side)
    for p in range(NC):
        for i in range(p + 1, NC):
            side[i] = side[i] - work[i][p] * side[p]
    for i in reversed(range(NC)):
        for j in range(i + 1, NC):
            side[i] = side[i] - work[i][j] * side[j]
        side[i] = side[i] * work[i][i]
    return side


def dot(row, column):
    terms = [a * b for a, b in zip(row, column)]
    return (terms[0] + terms[1]) + (terms[2] + terms[3]) + terms[4]


def times(matrix, vector):
    return [dot(row, vector) for row in matrix]


def product(left, right):
    columns = [[right[i][j] for i in range(NC)] for j in range(NC)]
    return [[dot(left[i], columns[j]) for j in range(NC)] for i in range(NC)]


def main_kernel(points, *refs):
    (visc, conv, spin, vaz, flux, faz, inc, edge) = refs[0:8]
    sibling = refs[8:15]
    halo_even, halo_odd, sib_even, sib_odd = refs[15:19]
    cell_own, cell_sib = refs[19:21]
    out_inc, out_defect = refs[21:23]
    cells, couple, lower, centre, upper, lu, sides, solved, vmin, vplus, azd, src, out_cells = refs[23:]

    core = lax.axis_index("wn")
    odd_place = lax.rem(lax.axis_index("az"), 2)
    row = lax.broadcasted_iota(jnp.int32, (SUB, LANES), 0)
    lane = lax.broadcasted_iota(jnp.int32, (SUB, LANES), 1)
    is_a = lax.rem(row, 2) == 0

    def put(value, t, place, chain, tile):
        start = pl.multiple_of(SUB * (2 * place + chain), SUB)
        cells[2 * value + (t + chain) % 2 if isinstance(chain, int) else 2 * value + jnp.bitwise_xor(t, chain),
              pl.ds(start, SUB), :] = tile

    for chain, arrays, halos in (
        (core, (visc, conv, spin, vaz, flux, faz, inc), (halo_even, halo_odd)),
        (1 - core, sibling, (sib_even, sib_odd)),
    ):
        read = tile_reader(*arrays, edge)
        sign = jnp.where(chain == 0, 1.0, -1.0).astype(jnp.float32)
        for value in range(VALUES):
            pack, slot, width = slot_of(value)
            for t in range(2):
                tiles = [(0, read(value, t, 0)), (1, read(value, t, 1))]
                for halo, place in ((halos[0], 2 + odd_place), (halos[1], 3 - odd_place)):
                    tile = halo[pack, pl.ds(SUB * t, SUB), :]
                    if slot:
                        tile = pltpu.roll(tile, LANES - slot * width, 1)
                    tiles.append((place, tile))
                for place, tile in tiles:
                    put(value, t, place, chain, tile * sign if value < SKEW else tile)

    def at(value, k):
        return cells[2 * value + k // SUB, pl.ds(k % SUB, SUB, stride=SUB), :]

    def bt(value, k):
        return cells[2 * value + k // SUB, pl.ds(SUB - 1 - k % SUB, SUB, stride=SUB), :]

    def both(value, ka, kb, other=None):
        return jnp.where(is_a, at(value, ka), bt(value if other is None else other, kb))

    def before(x):
        y = pltpu.roll(x, S, 1)
        return jnp.where(lane < S, pltpu.roll(y, 2, 0), y)

    def after(x):
        y = pltpu.roll(x, LANES - S, 1)
        return jnp.where(lane >= LANES - S, pltpu.roll(y, SUB - 2, 0), y)

    def swap(x):
        return jnp.where(is_a, pltpu.roll(x, SUB - 1, 0), pltpu.roll(x, 1, 0))

    edges = cells[2 * EDGE, pl.ds(0, SUB, stride=SUB), :]

    def fluid(k):
        if k >= points:
            return jnp.ones((SUB, LANES), jnp.float32)
        kind = jnp.where(core == 0, cell_own[k], cell_sib[k])
        return jnp.where(is_a, jnp.where(kind == 0, 1.0, 0.0).astype(jnp.float32), 1.0)

    def edge_scale(face_a, face_b):
        face = jnp.where(is_a, float(face_a), float(face_b))
        return jnp.where(face < edges, 1.0, OUTER_SCALE)

    one = jnp.ones((SUB, LANES), jnp.float32)
    zero = jnp.zeros((SUB, LANES), jnp.float32)
    total = 2 * points
    last = points - 1
    previous = None
    for k in range(points):
        keep = [fluid(k)] * (NC - 1) + [one]
        keep_above = [fluid(k + 1)] * (NC - 1) + [one]
        if k < last:
            conv_out = [[both(a * NC + b, k, k + 1, b * NC + a) for b in range(NC)] for a in range(NC)]
            visc_out = [both(VISC + c, k, k + 1) for c in range(NC)]
        else:
            face = [[at(a * NC + b, k) for b in range(NC)] for a in range(NC)]
            conv_out = [[jnp.where(is_a, face[a][b], -pltpu.roll(face[b][a], 1, 0)) for b in range(NC)] for a in range(NC)]
            raw = [at(VISC + c, k) for c in range(NC)]
            visc_out = [jnp.where(is_a, raw[c], pltpu.roll(raw[c], 1, 0)) for c in range(NC)]
        conv_out = [[conv_out[a][b] * (keep[a] * keep_above[b]) for b in range(NC)] for a in range(NC)]
        scale = edge_scale(k, total - 2 - k)
        visc_out = [visc_out[c] * scale * (keep[c] * keep_above[c]) for c in range(NC)]
        if k == 0:
            scale = edge_scale(0, total - 1)
            visc_in = [jnp.where(is_a, 0.0, bt(VISC + c, 0) * scale) for c in range(NC)]

        vm, vp, az_diag, source, side = [], [], [], [], []
        for c in range(NC):
            here = both(VAZ + c, k, k)
            vm.append(before(here) * keep[c])
            vp.append(here * keep[c])
            az_diag.append(vm[c] + vp[c] + (1.0 - keep[c]))
            flux_here = both(FLUX + c, k, k)
            if k == 0:
                flux_below = jnp.where(is_a, 0.0, bt(FLUX + c, 1))
            elif k < last:
                flux_below = both(FLUX + c, k - 1, k + 1)
            else:
                flux_below = jnp.where(is_a, at(FLUX + c, k - 1), pltpu.roll(at(FLUX + c, k), 1, 0))
            flux_side = both(FAZ + c, k, k)
            source.append((flux_below - flux_here + before(flux_side) - flux_side) * keep[c])
            start = both(INC + c, k, k)
            side.append(source[c] + (vm[c] * before(start) + vp[c] * after(start)))
            vmin[k * NC + c], vplus[k * NC + c] = vm[c], vp[c]
            azd[k * NC + c], src[k * NC + c] = az_diag[c], source[c]

        matrix = [[None] * NC for _ in range(NC)]
        for c in range(NC):
            matrix[c][c] = visc_in[c] + visc_out[c] + az_diag[c]
        for n, (a, b) in enumerate(PAIRS):
            skew = both(SKEW + n, k, k) * (keep[a] * keep[b])
            matrix[a][b], matrix[b][a] = skew, -skew
        up = [[conv_out[a][b] - visc_out[a] if a == b else conv_out[a][b] for b in range(NC)] for a in range(NC)]
        for a in range(NC):
            for b in range(NC):
                centre[k * 25 + a * NC + b] = matrix[a][b]
                upper[k * 25 + a * NC + b] = up[a][b]
        if previous is not None:
            conv_in, couple_in, y_in = previous
            low = [[-visc_in[a] - conv_in[a][a] if a == b else -conv_in[b][a] for b in range(NC)] for a in range(NC)]
            for a in range(NC):
                for b in range(NC):
                    lower[k * 25 + a * NC + b] = low[a][b]
            moved = product(low, couple_in)
            matrix = [[matrix[a][b] - moved[a][b] for b in range(NC)] for a in range(NC)]
            shift = times(low, y_in)
            side = [side[c] - shift[c] for c in range(NC)]
        work = factor(matrix)
        columns = [substitute(work, [up[i][j] for i in range(NC)]) for j in range(NC)]
        couple_now = [[columns[j][i] for j in range(NC)] for i in range(NC)]
        y = substitute(work, side)
        for a in range(NC):
            sides[k * NC + a] = y[a]
            for b in range(NC):
                lu[k * 25 + a * NC + b] = work[a][b]
                couple[k * 25 + a * NC + b] = couple_now[a][b]
        previous = (conv_out, couple_now, y)
        visc_in = visc_out

    def block(ref, k):
        return [[ref[k * 25 + a * NC + b] for b in range(NC)] for a in range(NC)]

    def vector(ref, k):
        return [ref[k * NC + c] for c in range(NC)]

    couple_end = couple_now
    crossed = product(couple_end, [[swap(couple_end[a][b]) for b in range(NC)] for a in range(NC)])
    meeting = factor([[(1.0 if a == b else 0.0) - crossed[a][b] for b in range(NC)] for a in range(NC)])

    def finish(y):
        shift = times(couple_end, [swap(v) for v in y])
        x = substitute(meeting, [y[c] - shift[c] for c in range(NC)])
        for c in range(NC):
            solved[last * NC + c] = x[c]
        for k in reversed(range(last)):
            shift = times(block(couple, k), x)
            y_here = vector(sides, k)
            x = [y_here[c] - shift[c] for c in range(NC)]
            for c in range(NC):
                solved[k * NC + c] = x[c]

    finish(y)
    for sweep in range(1, SWEEPS):
        for k in range(points):
            source, vm, vp, x = vector(src, k), vector(vmin, k), vector(vplus, k), vector(solved, k)
            side = [source[c] + (vm[c] * before(x[c]) + vp[c] * after(x[c])) for c in range(NC)]
            if k:
                shift = times(block(lower, k), y)
                side = [side[c] - shift[c] for c in range(NC)]
            y = substitute(block(lu, k), side)
            for c in range(NC):
                sides[k * NC + c] = y[c]
        finish(y)

    for k in range(points):
        source, vm, vp, x = vector(src, k), vector(vmin, k), vector(vplus, k), vector(solved, k)
        diag = vector(azd, k)
        beyond = vector(solved, k + 1) if k < last else [swap(v) for v in x]
        inner = times(block(centre, k), x)
        outer = times(block(upper, k), beyond)
        under = times(block(lower, k), vector(solved, k - 1)) if k else [zero] * NC
        place = jnp.where(core == 0, k % SUB, SUB - 1 - k % SUB)
        t = jnp.where(core == 0, k // SUB, 1 - k // SUB)
        for c in range(NC):
            offline = vm[c] * before(x[c]) + vp[c] * after(x[c])
            defect = (source[c] + offline - (inner[c] + under[c] + outer[c])) / diag[c]
            out_cells[2 * c + t, pl.ds(place, SUB, stride=SUB), :] = x[c]
            out_cells[2 * (NC + c) + t, pl.ds(place, SUB, stride=SUB), :] = defect
    for c in range(NC):
        for t in range(2):
            for lt in range(2):
                start = pl.multiple_of(SUB * (2 * lt + core), SUB)
                rows, lanes = pl.ds(SUB * t, SUB), pl.ds(LANES * lt, LANES)
                out_inc[c, rows, lanes] = out_cells[2 * c + t, pl.ds(start, SUB), :]
                out_defect[c, rows, lanes] = out_cells[2 * (NC + c) + t, pl.ds(start, SUB), :]


def per_device(visc_wn, conv_wn, spin, visc_az, flux_wn, flux_az, incr_prev, cell_type, edge_index):
    components, points, line_count = visc_wn.shape
    assert components == NC and points == 2 * SUB and line_count == 2 * LANES
    count = lax.axis_size("az")
    assert count % 2 == 0
    even_pairs = [(a, a ^ 1) for a in range(count)]
    odd_pairs = [(a, (a + 1 if a % 2 else a - 1) % count) for a in range(count)]
    vmem, smem = pl.BlockSpec(memory_space=pltpu.VMEM), pl.BlockSpec(memory_space=pltpu.SMEM)

    blocks = (NC * NC, points, line_count)
    own = (visc_wn, conv_wn.reshape(blocks), spin.reshape(blocks), visc_az, flux_wn, flux_az, incr_prev)
    edge = edge_index.reshape(1, line_count)
    pack = jax.ShapeDtypeStruct((PACKS, points, LANES), jnp.float32)
    even, odd = pl.pallas_call(
        pack_kernel,
        out_shape=(pack, pack),
        in_specs=[vmem] * 8,
        out_specs=(vmem, vmem),
        name="pack_halo",
        compiler_params=pltpu.CompilerParams(vmem_limit_bytes=32 << 20),
    )(*own, edge)
    halo_even = lax.ppermute(even, "az", even_pairs)
    halo_odd = lax.ppermute(odd, "az", odd_pairs)

    def cross(array):
        return lax.ppermute(array, "wn", [(0, 1), (1, 0)])

    sibling = tuple(cross(array) for array in own)
    cell_sib = cross(cell_type)
    sib_even, sib_odd = cross(halo_even), cross(halo_odd)

    step = pltpu.VMEM((points * NC * NC, SUB, LANES), jnp.float32)
    line = pltpu.VMEM((points * NC, SUB, LANES), jnp.float32)
    out = jax.ShapeDtypeStruct((NC, points, line_count), jnp.float32)
    return pl.pallas_call(
        lambda *refs: main_kernel(points, *refs),
        out_shape=(out, out),
        in_specs=[vmem] * 19 + [smem] * 2,
        out_specs=(vmem, vmem),
        scratch_shapes=[pltpu.VMEM((2 * VALUES, SUB * SUB, LANES), jnp.float32)]
        + [step] * 5
        + [line] * 6
        + [pltpu.VMEM((4 * NC, SUB * SUB, LANES), jnp.float32)],
        name="relax_lines",
        compiler_params=pltpu.CompilerParams(vmem_limit_bytes=40 << 20),
    )(*own, edge, *sibling, halo_even, halo_odd, sib_even, sib_odd, cell_type, cell_sib)


def solution(mesh):
    in_specs = (
        P(None, "wn", "az"),
        P(None, None, "wn", "az"),
        P(None, None, "wn", "az"),
        P(None, "wn", "az"),
        P(None, "wn", "az"),
        P(None, "wn", "az"),
        P(None, "wn", "az"),
        P("wn"),
        P("az"),
    )
    out_specs = (P(None, "wn", "az"), P(None, "wn", "az"))
    return jax.shard_map(
        per_device, mesh=mesh, in_specs=in_specs, out_specs=out_specs, check_vma=False
    )
```

time: 194 us -> 29.5 us (0.15); the launches traced: 191 us -> 29.1 us
  local copies, waits for them, and re-layouts: 71.8 us -> 7.06 us
  other arithmetic: 51.6 us -> 0 us
  blocking collectives: 20.5 us -> 0 us
  starting transfers between devices: 29.2 us -> 9.38 us
  waiting for transfers between devices: 14.7 us -> 5.9 us
  Pallas kernels: 0 us -> 6.05 us
  between operations: 3.63 us -> 0.75 us
    unnamed x120 -> x32, local copies, waits for them, and re-layouts: 28.3 us -> 7.06 us
    reduce_sum x70 -> x0, other arithmetic: 21 us -> none  [the longest x51 15.9 us: block_vector(): return jnp.sum(matrix * vector[None], axis=1)]
    all_to_all x5 -> x0, blocking collectives: 20.5 us -> none  [the longest x2 7.68 us: per_device(): lax.all_to_all(solve_lines(factors, line_rows), 'wn', split_axis=1, conca...]
    slice x77 -> x0, local copies, waits for them, and re-layouts: 14.9 us -> none  [the longest x4 4.03 us: factor_lines(): with_right = block_product(upper_block[:, :, 0::2], odd_inverse)]
    all_to_all x14 -> x0, local copies, waits for them, and re-layouts: 14.8 us -> none  [the longest x2 4.54 us: per_device(): lax.all_to_all(lower_block, 'wn', split_axis=3, concat_axis=2, tiled=True)]
    ppermute x13 -> x12, starting transfers between devices: 22.4 us -> 9.38 us  [the longest x1 4.58 us: per_device(): halo_odd = lax.ppermute(odd, 'az', odd_pairs)]
    sub x56 -> x0, other arithmetic: 9.27 us -> none  [the longest x6 2.47 us: invert(): result = result - column[:, None] * row_result[None]]
    all_to_all x5 -> x0, other arithmetic: 8.07 us -> none  [the longest x2 2.36 us: per_device(): lax.all_to_all(source + offline(increment), 'wn', split_axis=2, concat_ax...]
  transfers between devices with their start and end apart: 15 -> 12, of which waited for: 5 -> 5; matrix products, arithmetic and copies ran while one was open for 16% -> 0% of each run, Pallas kernels for 0% -> 1%
where the time goes in v1:
time: 29.5 us; the launch traced here: 29.1 us
  starting transfers between devices  9.38 us (32%)
  local copies, waits for them, and re-layouts  7.06 us (24%)
  Pallas kernels  6.05 us (21%)
  waiting for transfers between devices  5.9 us (20%)
  between operations  0.75 us (3%)
    unnamed x32, local copies, waits for them, and re-layouts  7.06 us
    pallas_call x1, Pallas kernels, per_device(): pl.pallas_call(lambda *refs: main_kernel(points, *refs), out_shape=(out,...  5.76 us
    ppermute x1, starting transfers between devices, per_device(): halo_odd = lax.ppermute(odd, 'az', odd_pairs)  4.58 us
    ppermute x1, waiting for transfers between devices, per_device(): halo_odd = lax.ppermute(odd, 'az', odd_pairs)  3.45 us
    ppermute x1, starting transfers between devices, per_device(): halo_even = lax.ppermute(even, 'az', even_pairs)  2.56 us
    ppermute x10, waiting for transfers between devices, cross(): return lax.ppermute(array, 'wn', [(0, 1), (1, 0)])  2.44 us
    ppermute x10, starting transfers between devices, cross(): return lax.ppermute(array, 'wn', [(0, 1), (1, 0)])  2.23 us
  transfers between devices with their start and end apart: 12, of which 5 were waited for; matrix products, arithmetic and copies ran while one was open for 0% of the time, Pallas kernels for 1%

profile of v1, /device:TPU:0, one launch (start us, length us, event | category | flops | bytes accessed | tf_op | source)
XLA Modules:
  0.0 29.1 jit_solution(13345019316127046714)
XLA Ops:
  0.6 0.5 %collective-permute-start.1 = (f32[25,16,256]{2,1,0:T(8,128)}, f32[25,16,256]{2,1,0:T(8,128)S(1)}, u32[]{:S(2)}, u32[]{:S(2)}) collective-permute-start(f32[25,16,256]{2,1,0:T(8,128)} %bitcast.3), channel_id=1, source_target_pairs={{0,1},{1,0},{2,3},{3,2},{4,5},{5,4},{6,7},{7,6},{8,9},{9,8},{10,11... | collective-permute-start | bytes 1228808 | tf_op jit(solution)/shard_map/ppermute | solution.py:345
  1.2 0.0 copy-start.14
  1.2 0.1 collective-permute-start.2
  1.2 0.6 %copy-done.14 = s32[256]{0:T(256)S(1)} copy-done((s32[256]{0:T(256)S(1)}, s32[256]{0:T(256)}, u32[]{:S(2)}) %copy-start.14) | copy-done | bytes 1048
  1.8 0.0 copy-start
  1.8 1.0 %copy-done = f32[5,5,16,256]{3,2,1,0:T(8,128)S(1)} copy-done((f32[5,5,16,256]{3,2,1,0:T(8,128)S(1)}, f32[5,5,16,256]{3,2,1,0:T(8,128)}, u32[]{:S(2)}) %copy-start) | copy-done | bytes 409624
  2.8 0.0 copy-start.2
  2.8 1.0 %copy-done.2 = f32[5,5,16,256]{3,2,1,0:T(8,128)S(1)} copy-done((f32[5,5,16,256]{3,2,1,0:T(8,128)S(1)}, f32[5,5,16,256]{3,2,1,0:T(8,128)}, u32[]{:S(2)}) %copy-start.2) | copy-done | bytes 409624
  3.8 0.0 copy-start.4
  3.8 0.9 %copy-done.4 = f32[5,16,256]{2,1,0:T(8,128)S(1)} copy-done((f32[5,16,256]{2,1,0:T(8,128)S(1)}, f32[5,16,256]{2,1,0:T(8,128)}, u32[]{:S(2)}) %copy-start.4) | copy-done | bytes 81944
  4.7 0.0 copy-start.6
  4.7 0.9 %copy-done.6 = f32[5,16,256]{2,1,0:T(8,128)S(1)} copy-done((f32[5,16,256]{2,1,0:T(8,128)S(1)}, f32[5,16,256]{2,1,0:T(8,128)}, u32[]{:S(2)}) %copy-start.6) | copy-done | bytes 81944
  5.6 0.0 copy-start.8
  5.6 0.9 %copy-done.8 = f32[5,16,256]{2,1,0:T(8,128)S(1)} copy-done((f32[5,16,256]{2,1,0:T(8,128)S(1)}, f32[5,16,256]{2,1,0:T(8,128)}, u32[]{:S(2)}) %copy-start.8) | copy-done | bytes 81944
  6.5 0.0 copy-start.10
  6.5 0.9 %copy-done.10 = f32[5,16,256]{2,1,0:T(8,128)S(1)} copy-done((f32[5,16,256]{2,1,0:T(8,128)S(1)}, f32[5,16,256]{2,1,0:T(8,128)}, u32[]{:S(2)}) %copy-start.10) | copy-done | bytes 81944
  7.4 0.0 copy-start.12
  7.4 0.9 %copy-done.12 = f32[5,16,256]{2,1,0:T(8,128)S(1)} copy-done((f32[5,16,256]{2,1,0:T(8,128)S(1)}, f32[5,16,256]{2,1,0:T(8,128)}, u32[]{:S(2)}) %copy-start.12) | copy-done | bytes 81944
  8.3 0.0 copy-start.1
  8.3 0.0 copy-start.3
  8.3 0.0 copy-start.5
  8.3 0.0 copy-start.7
  8.3 0.0 copy-start.9
  8.3 0.0 copy-start.11
  8.3 0.0 copy-start.13
  8.3 0.3 pack_halo.1
  8.6 0.0 copy-start.15
  8.6 2.6 %collective-permute-start.7 = (f32[9,16,128]{2,1,0:T(8,128)S(1)}, f32[9,16,128]{2,1,0:T(8,128)S(1)}, u32[]{:S(2)}, u32[]{:S(2)}) collective-permute-start(f32[9,16,128]{2,1,0:T(8,128)S(1)} %get-tuple-element.4), channel_id=1, source_target_pairs={{0,2},{2,0},{4,6},{6,4},{8,10},{10,8},{12,14},{14,12},{16,18},{18,... | collective-permute-start | bytes 221192 | tf_op jit(solution)/shard_map/ppermute | solution.py:341
  11.2 0.2 collective-permute-start
  11.4 0.0 copy-done.15
  11.4 0.3 %collective-permute-start.11 = (s32[16]{0:T(128)S(1)}, s32[16]{0:T(128)S(1)}, u32[]{:S(2)}, u32[]{:S(2)}) collective-permute-start(s32[16]{0:T(128)S(1)} %copy-done.15), channel_id=1, source_target_pairs={{0,1},{1,0},{2,3},{3,2},{4,5},{5,4},{6,7},{7,6},{8,9},{9,8},{10,11... | collective-permute-start | bytes 200 | tf_op jit(solution)/shard_map/ppermute | solution.py:345
  11.7 0.8 %collective-permute-done.11.refs_20_ = s32[16]{0:T(128)S(1)} collective-permute-done((s32[16]{0:T(128)S(1)}, s32[16]{0:T(128)S(1)}, u32[]{:S(2)}, u32[]{:S(2)}) %collective-permute-start.11) | collective-permute-done | bytes 96 | tf_op jit(solution)/shard_map/ppermute | solution.py:345
  12.5 4.6 %collective-permute-start.8 = (f32[9,16,128]{2,1,0:T(8,128)S(1)}, f32[9,16,128]{2,1,0:T(8,128)S(1)}, u32[]{:S(2)}, u32[]{:S(2)}) collective-permute-start(f32[9,16,128]{2,1,0:T(8,128)S(1)} %get-tuple-element.5), channel_id=1, source_target_pairs={{0,30},{2,4},{4,2},{6,8},{8,6},{10,12},{12,10},{14,16},{16,14},{18... | collective-permute-start | bytes 221192 | tf_op jit(solution)/shard_map/ppermute | solution.py:342
  17.1 0.0 collective-permute-done.7.refs_15_
  17.1 0.0 collective-permute-start.3
  17.1 3.5 %collective-permute-done.8.refs_16_ = f32[9,16,128]{2,1,0:T(8,128)S(1)} collective-permute-done((f32[9,16,128]{2,1,0:T(8,128)S(1)}, f32[9,16,128]{2,1,0:T(8,128)S(1)}, u32[]{:S(2)}, u32[]{:S(2)}) %collective-permute-start.8) | collective-permute-done | bytes 73760 | tf_op jit(solution)/shard_map/ppermute | solution.py:342
  20.6 0.0 collective-permute-start.4
  20.6 0.0 collective-permute-done.refs_8_
  20.6 0.5 %collective-permute-start.5 = (f32[5,16,256]{2,1,0:T(8,128)S(1)}, f32[5,16,256]{2,1,0:T(8,128)S(1)}, u32[]{:S(2)}, u32[]{:S(2)}) collective-permute-start(f32[5,16,256]{2,1,0:T(8,128)S(1)} %copy-done.10), channel_id=1, source_target_pairs={{0,1},{1,0},{2,3},{3,2},{4,5},{5,4},{6,7},{7,6},{8,9},{9,8},{10,11... | collective-permute-start | bytes 245768 | tf_op jit(solution)/shard_map/ppermute | solution.py:345
  21.1 0.0 collective-permute-done.3.refs_11_
  21.1 0.1 collective-permute-start.6
  21.2 0.7 %collective-permute-done.4.refs_12_ = f32[5,16,256]{2,1,0:T(8,128)S(1)} collective-permute-done((f32[5,16,256]{2,1,0:T(8,128)S(1)}, f32[5,16,256]{2,1,0:T(8,128)S(1)}, u32[]{:S(2)}, u32[]{:S(2)}) %collective-permute-start.4) | collective-permute-done | bytes 81952 | tf_op jit(solution)/shard_map/ppermute | solution.py:345
  21.9 0.2 collective-permute-start.9
  22.0 0.0 collective-permute-done.5.refs_13_
  22.0 0.4 %collective-permute-start.10 = (f32[9,16,128]{2,1,0:T(8,128)S(1)}, f32[9,16,128]{2,1,0:T(8,128)S(1)}, u32[]{:S(2)}, u32[]{:S(2)}) collective-permute-start(f32[9,16,128]{2,1,0:T(8,128)S(1)} %collective-permute-done.8.refs_16_), channel_id=1, source_target_pairs={{0,1},{1,0},{2,3},{3,2},{4,5},{5,4},{6,7},{7,6},{8,9},{9,8},{10,11... | collective-permute-start | bytes 221192 | tf_op jit(solution)/shard_map/ppermute | solution.py:345
  22.4 0.0 collective-permute-done.6.refs_14_
  22.4 0.7 %collective-permute-done.9.refs_17_ = f32[9,16,128]{2,1,0:T(8,128)S(1)} collective-permute-done((f32[9,16,128]{2,1,0:T(8,128)S(1)}, f32[9,16,128]{2,1,0:T(8,128)S(1)}, u32[]{:S(2)}, u32[]{:S(2)}) %collective-permute-start.9) | collective-permute-done | bytes 73760 | tf_op jit(solution)/shard_map/ppermute | solution.py:345
  23.1 0.2 collective-permute-done.10.refs_18_
  23.3 0.0 collective-permute-done.1.refs_9_
  23.3 0.0 collective-permute-done.2.refs_10_
  23.3 0.0 copy-done.1
  23.3 0.0 copy-done.3
  23.3 0.0 copy-done.5
  23.3 0.0 copy-done.7
  23.3 0.0 copy-done.9
  23.3 0.0 copy-done.11
  23.4 0.0 copy-done.13
  23.4 5.8 %relax_lines.1 = (f32[5,16,256]{2,1,0:T(8,128)}, f32[5,16,256]{2,1,0:T(8,128)}) custom-call(f32[5,16,256]{2,1,0:T(8,128)S(1)} %copy-done.5, f32[25,16,256]{2,1,0:T(8,128)S(1)} %bitcast.5, f32[25,16,256]{2,1,0:T(8,128)S(1)} %bitcast.8, f32[5,16,256]{2,1,0:T(8,128)S(1)} %copy-done.7, f32[5,16,256]{2,1,0:T(8,128)S(1)} %copy-done.9, ...), custom_call_target="tpu_custom_call" | custom-call | tf_op jit(solution)/shard_map/relax_lines/pallas_call | solution.py:354
Async XLA Ops:
  0.6 22.7 %collective-permute-start.1 = (f32[25,16,256]{2,1,0:T(8,128)}, f32[25,16,256]{2,1,0:T(8,128)S(1)}, u32[]{:S(2)}, u32[]{:S(2)}) collective-permute-start(f32[25,16,256]{2,1,0:T(8,128)} %bitcast.3), channel_id=1, source_target_pairs={{0,1},{1,0},{2,3},{3,2},{4,5},{5,4},{6,7},{7,6},{8,9},{9,8},{10,11... | collective-permute-start | bytes 1228808 | tf_op jit(solution)/shard_map/ppermute | solution.py:345
  1.2 0.7 %copy-start.14 = (s32[256]{0:T(256)S(1)}, s32[256]{0:T(256)}, u32[]{:S(2)}) copy-start(s32[256]{0:T(256)} %param.17) | copy-start | bytes 3076
  1.2 22.1 %collective-permute-start.2 = (f32[25,16,256]{2,1,0:T(8,128)}, f32[25,16,256]{2,1,0:T(8,128)S(1)}, u32[]{:S(2)}, u32[]{:S(2)}) collective-permute-start(f32[25,16,256]{2,1,0:T(8,128)} %bitcast.6), channel_id=1, source_target_pairs={{0,1},{1,0},{2,3},{3,2},{4,5},{5,4},{6,7},{7,6},{8,9},{9,8},{10,11... | collective-permute-start | bytes 1228808 | tf_op jit(solution)/shard_map/ppermute | solution.py:345
  1.8 1.0 %copy-start = (f32[5,5,16,256]{3,2,1,0:T(8,128)S(1)}, f32[5,5,16,256]{3,2,1,0:T(8,128)}, u32[]{:S(2)}) copy-start(f32[5,5,16,256]{3,2,1,0:T(8,128)} %param.10) | copy-start | bytes 1228804
  2.8 1.0 %copy-start.2 = (f32[5,5,16,256]{3,2,1,0:T(8,128)S(1)}, f32[5,5,16,256]{3,2,1,0:T(8,128)}, u32[]{:S(2)}) copy-start(f32[5,5,16,256]{3,2,1,0:T(8,128)} %param.11) | copy-start | bytes 1228804
  3.8 0.9 %copy-start.4 = (f32[5,16,256]{2,1,0:T(8,128)S(1)}, f32[5,16,256]{2,1,0:T(8,128)}, u32[]{:S(2)}) copy-start(f32[5,16,256]{2,1,0:T(8,128)} %refs_0_.1) | copy-start | bytes 245764
  4.7 0.9 %copy-start.6 = (f32[5,16,256]{2,1,0:T(8,128)S(1)}, f32[5,16,256]{2,1,0:T(8,128)}, u32[]{:S(2)}) copy-start(f32[5,16,256]{2,1,0:T(8,128)} %refs_3_.1) | copy-start | bytes 245764
  5.6 0.9 %copy-start.8 = (f32[5,16,256]{2,1,0:T(8,128)S(1)}, f32[5,16,256]{2,1,0:T(8,128)}, u32[]{:S(2)}) copy-start(f32[5,16,256]{2,1,0:T(8,128)} %refs_4_.1) | copy-start | bytes 245764
  6.5 0.9 %copy-start.10 = (f32[5,16,256]{2,1,0:T(8,128)S(1)}, f32[5,16,256]{2,1,0:T(8,128)}, u32[]{:S(2)}) copy-start(f32[5,16,256]{2,1,0:T(8,128)} %refs_5_.1) | copy-start | bytes 245764
  7.4 0.9 %copy-start.12 = (f32[5,16,256]{2,1,0:T(8,128)S(1)}, f32[5,16,256]{2,1,0:T(8,128)}, u32[]{:S(2)}) copy-start(f32[5,16,256]{2,1,0:T(8,128)} %refs_6_.1) | copy-start | bytes 245764
  8.3 15.0 %copy-start.1 = (f32[5,5,16,256]{3,2,1,0:T(8,128)S(1)}, f32[5,5,16,256]{3,2,1,0:T(8,128)}, u32[]{:S(2)}) copy-start(f32[5,5,16,256]{3,2,1,0:T(8,128)} %param.10) | copy-start | bytes 1228804
  8.3 15.0 %copy-start.3 = (f32[5,5,16,256]{3,2,1,0:T(8,128)S(1)}, f32[5,5,16,256]{3,2,1,0:T(8,128)}, u32[]{:S(2)}) copy-start(f32[5,5,16,256]{3,2,1,0:T(8,128)} %param.11) | copy-start | bytes 1228804
  8.3 15.0 %copy-start.5 = (f32[5,16,256]{2,1,0:T(8,128)S(1)}, f32[5,16,256]{2,1,0:T(8,128)}, u32[]{:S(2)}) copy-start(f32[5,16,256]{2,1,0:T(8,128)} %refs_0_.1) | copy-start | bytes 245764
  8.3 15.1 %copy-start.7 = (f32[5,16,256]{2,1,0:T(8,128)S(1)}, f32[5,16,256]{2,1,0:T(8,128)}, u32[]{:S(2)}) copy-start(f32[5,16,256]{2,1,0:T(8,128)} %refs_3_.1) | copy-start | bytes 245764
  8.3 15.1 %copy-start.9 = (f32[5,16,256]{2,1,0:T(8,128)S(1)}, f32[5,16,256]{2,1,0:T(8,128)}, u32[]{:S(2)}) copy-start(f32[5,16,256]{2,1,0:T(8,128)} %refs_4_.1) | copy-start | bytes 245764
  8.3 15.1 %copy-start.11 = (f32[5,16,256]{2,1,0:T(8,128)S(1)}, f32[5,16,256]{2,1,0:T(8,128)}, u32[]{:S(2)}) copy-start(f32[5,16,256]{2,1,0:T(8,128)} %refs_5_.1) | copy-start | bytes 245764
  8.3 15.1 %copy-start.13 = (f32[5,16,256]{2,1,0:T(8,128)S(1)}, f32[5,16,256]{2,1,0:T(8,128)}, u32[]{:S(2)}) copy-start(f32[5,16,256]{2,1,0:T(8,128)} %refs_6_.1) | copy-start | bytes 245764
  8.6 2.8 %copy-start.15 = (s32[16]{0:T(128)S(1)}, s32[16]{0:T(128)}, u32[]{:S(2)}) copy-start(s32[16]{0:T(128)} %refs_19_.1) | copy-start | bytes 196
  8.6 8.5 %collective-permute-start.7 = (f32[9,16,128]{2,1,0:T(8,128)S(1)}, f32[9,16,128]{2,1,0:T(8,128)S(1)}, u32[]{:S(2)}, u32[]{:S(2)}) collective-permute-start(f32[9,16,128]{2,1,0:T(8,128)S(1)} %get-tuple-element.4), channel_id=1, source_target_pairs={{0,2},{2,0},{4,6},{6,4},{8,10},{10,8},{12,14},{14,12},{16,18},{18,... | collective-permute-start | bytes 221192 | tf_op jit(solution)/shard_map/ppermute | solution.py:341
  11.2 9.4 %collective-permute-start = (f32[5,16,256]{2,1,0:T(8,128)S(1)}, f32[5,16,256]{2,1,0:T(8,128)S(1)}, u32[]{:S(2)}, u32[]{:S(2)}) collective-permute-start(f32[5,16,256]{2,1,0:T(8,128)S(1)} %copy-done.4), channel_id=1, source_target_pairs={{0,1},{1,0},{2,3},{3,2},{4,5},{5,4},{6,7},{7,6},{8,9},{9,8},{10,11... | collective-permute-start | bytes 245768 | tf_op jit(solution)/shard_map/ppermute | solution.py:345
  11.4 1.1 %collective-permute-start.11 = (s32[16]{0:T(128)S(1)}, s32[16]{0:T(128)S(1)}, u32[]{:S(2)}, u32[]{:S(2)}) collective-permute-start(s32[16]{0:T(128)S(1)} %copy-done.15), channel_id=1, source_target_pairs={{0,1},{1,0},{2,3},{3,2},{4,5},{5,4},{6,7},{7,6},{8,9},{9,8},{10,11... | collective-permute-start | bytes 200 | tf_op jit(solution)/shard_map/ppermute | solution.py:345
  12.5 8.1 %collective-permute-start.8 = (f32[9,16,128]{2,1,0:T(8,128)S(1)}, f32[9,16,128]{2,1,0:T(8,128)S(1)}, u32[]{:S(2)}, u32[]{:S(2)}) collective-permute-start(f32[9,16,128]{2,1,0:T(8,128)S(1)} %get-tuple-element.5), channel_id=1, source_target_pairs={{0,30},{2,4},{4,2},{6,8},{8,6},{10,12},{12,10},{14,16},{16,14},{18... | collective-permute-start | bytes 221192 | tf_op jit(solution)/shard_map/ppermute | solution.py:342
  17.1 4.0 %collective-permute-start.3 = (f32[5,16,256]{2,1,0:T(8,128)S(1)}, f32[5,16,256]{2,1,0:T(8,128)S(1)}, u32[]{:S(2)}, u32[]{:S(2)}) collective-permute-start(f32[5,16,256]{2,1,0:T(8,128)S(1)} %copy-done.6), channel_id=1, source_target_pairs={{0,1},{1,0},{2,3},{3,2},{4,5},{5,4},{6,7},{7,6},{8,9},{9,8},{10,11... | collective-permute-start | bytes 245768 | tf_op jit(solution)/shard_map/ppermute | solution.py:345
  20.6 1.3 %collective-permute-start.4 = (f32[5,16,256]{2,1,0:T(8,128)S(1)}, f32[5,16,256]{2,1,0:T(8,128)S(1)}, u32[]{:S(2)}, u32[]{:S(2)}) collective-permute-start(f32[5,16,256]{2,1,0:T(8,128)S(1)} %copy-done.8), channel_id=1, source_target_pairs={{0,1},{1,0},{2,3},{3,2},{4,5},{5,4},{6,7},{7,6},{8,9},{9,8},{10,11... | collective-permute-start | bytes 245768 | tf_op jit(solution)/shard_map/ppermute | solution.py:345
  20.6 1.4 %collective-permute-start.5 = (f32[5,16,256]{2,1,0:T(8,128)S(1)}, f32[5,16,256]{2,1,0:T(8,128)S(1)}, u32[]{:S(2)}, u32[]{:S(2)}) collective-permute-start(f32[5,16,256]{2,1,0:T(8,128)S(1)} %copy-done.10), channel_id=1, source_target_pairs={{0,1},{1,0},{2,3},{3,2},{4,5},{5,4},{6,7},{7,6},{8,9},{9,8},{10,11... | collective-permute-start | bytes 245768 | tf_op jit(solution)/shard_map/ppermute | solution.py:345
  21.1 1.3 %collective-permute-start.6 = (f32[5,16,256]{2,1,0:T(8,128)S(1)}, f32[5,16,256]{2,1,0:T(8,128)S(1)}, u32[]{:S(2)}, u32[]{:S(2)}) collective-permute-start(f32[5,16,256]{2,1,0:T(8,128)S(1)} %copy-done.12), channel_id=1, source_target_pairs={{0,1},{1,0},{2,3},{3,2},{4,5},{5,4},{6,7},{7,6},{8,9},{9,8},{10,11... | collective-permute-start | bytes 245768 | tf_op jit(solution)/shard_map/ppermute | solution.py:345
  21.9 1.3 %collective-permute-start.9 = (f32[9,16,128]{2,1,0:T(8,128)S(1)}, f32[9,16,128]{2,1,0:T(8,128)S(1)}, u32[]{:S(2)}, u32[]{:S(2)}) collective-permute-start(f32[9,16,128]{2,1,0:T(8,128)S(1)} %collective-permute-done.7.refs_15_), channel_id=1, source_target_pairs={{0,1},{1,0},{2,3},{3,2},{4,5},{5,4},{6,7},{7,6},{8,9},{9,8},{10,11... | collective-permute-start | bytes 221192 | tf_op jit(solution)/shard_map/ppermute | solution.py:345
  22.0 1.3 %collective-permute-start.10 = (f32[9,16,128]{2,1,0:T(8,128)S(1)}, f32[9,16,128]{2,1,0:T(8,128)S(1)}, u32[]{:S(2)}, u32[]{:S(2)}) collective-permute-start(f32[9,16,128]{2,1,0:T(8,128)S(1)} %collective-permute-done.8.refs_16_), channel_id=1, source_target_pairs={{0,1},{1,0},{2,3},{3,2},{4,5},{5,4},{6,7},{7,6},{8,9},{9,8},{10,11... | collective-permute-start | bytes 221192 | tf_op jit(solution)/shard_map/ppermute | solution.py:345

commit v2 on v1

--- a/solution.py
+++ b/solution.py
@@ -14,10 +14,11 @@
 NEAR = 2 * S
 FAR = 3 * S
 
-CONV, SKEW, VISC, FLUX, EDGE = 0, 25, 35, 40, 45
-NEAR_VALUES = 46
-VAZ, FAZ, INC = 46, 51, 56
-VALUES = 61
+CONV, SKEW, VISC, FLUX, EDGE, FLUID = 0, 25, 35, 40, 45, 46
+NEAR_VALUES = 47
+VAZ, FAZ, INC = 47, 52, 57
+VALUES = 62
+SOLID_MOST = 4
 NEAR_SLOTS = LANES // NEAR
 FAR_SLOTS = LANES // FAR
 NEAR_PACKS = -(-NEAR_VALUES // NEAR_SLOTS)
@@ -33,7 +34,7 @@
     return NEAR_PACKS + other // FAR_SLOTS, other % FAR_SLOTS, FAR
 
 
-def tile_reader(visc, conv, spin, vaz, flux, faz, inc, edge):
+def tile_reader(conv, spin, edge, lines):
     def read(value, t, lt):
         rows, lanes = pl.ds(SUB * t, SUB), pl.ds(LANES * lt, LANES)
         if value < SKEW:
@@ -43,18 +44,44 @@
             return spin[a * NC + b, rows, lanes] - spin[b * NC + a, rows, lanes]
         if value == EDGE:
             return jnp.broadcast_to(edge[0:1, lanes].astype(jnp.float32), (SUB, LANES))
-        for first, ref in ((VISC, visc), (FLUX, flux), (VAZ, vaz), (FAZ, faz), (INC, inc)):
+        for first, ref in zip((VISC, FLUX, VAZ, FAZ, INC), lines):
             if first <= value < first + NC:
                 return ref[value - first, rows, lanes]
 
     return read
 
 
-def pack_kernel(visc, conv, spin, vaz, flux, faz, inc, edge, even_out, odd_out):
+def lines_of(ref):
+    return [ref.at[pl.ds(NC * n, NC)] for n in range(5)]
+
+
+def pack_kernel(conv_hbm, spin_hbm, edge_hbm, visc_hbm, flux_hbm, vaz_hbm, faz_hbm, inc_hbm, cells_hbm,
+                even_out, odd_out, stack_out, conv, spin, edge, stack, cells, sems, stack_sem):
     odd_place = lax.rem(lax.axis_index("az"), 2) == 1
-    read = tile_reader(visc, conv, spin, vaz, flux, faz, inc, edge)
+    copies = []
+    for n, ref in enumerate((visc_hbm, flux_hbm, vaz_hbm, faz_hbm, inc_hbm)):
+        copies.append(pltpu.make_async_copy(ref, stack.at[pl.ds(NC * n, NC)], sems.at[n]))
+    copies.append(pltpu.make_async_copy(edge_hbm, edge, sems.at[5]))
+    for n in range(NC):
+        part = pl.ds(NC * n, NC)
+        copies.append(pltpu.make_async_copy(conv_hbm.at[part], conv.at[part], sems.at[6 + n]))
+        copies.append(pltpu.make_async_copy(spin_hbm.at[part], spin.at[part], sems.at[11 + n]))
+    copies.append(pltpu.make_async_copy(cells_hbm, cells, sems.at[16]))
+    for copy in copies:
+        copy.start()
+    for copy in copies[:5]:
+        copy.wait()
+    stacked = pltpu.make_async_copy(stack, stack_out, stack_sem)
+    stacked.start()
+    for copy in copies[5:]:
+        copy.wait()
+    read = tile_reader(conv, spin, edge, lines_of(stack))
     lane = lax.broadcasted_iota(jnp.int32, (SUB, LANES), 1)
+    row = lax.broadcasted_iota(jnp.int32, (SUB, LANES), 0)
     for t in range(2):
+        fluid = jnp.ones((SUB, LANES), jnp.float32)
+        for p in range(SOLID_MOST if t == 0 else 0):
+            fluid = jnp.where(row == p, jnp.where(cells[p] == 0, 1.0, 0.0).astype(jnp.float32), fluid)
         first = [jnp.zeros((SUB, LANES), jnp.float32)] * PACKS
         last = [jnp.zeros((SUB, LANES), jnp.float32)] * PACKS
         for value in range(VALUES):
@@ -63,15 +90,19 @@
             here = (lane >= low) & (lane < low + width)
             low = (LANES - width + slot * width) % LANES
             there = (lane >= low) & (lane < low + width)
-            one, two = read(value, t, 0), read(value, t, 1)
-            if slot:
-                one, two = pltpu.roll(one, slot * width, 1), pltpu.roll(two, slot * width, 1)
+            if value == FLUID:
+                one, two = fluid, fluid
+            else:
+                one, two = read(value, t, 0), read(value, t, 1)
+                if slot:
+                    one, two = pltpu.roll(one, slot * width, 1), pltpu.roll(two, slot * width, 1)
             first[pack] = jnp.where(here, one, first[pack])
             last[pack] = jnp.where(there, two, last[pack])
         rows = pl.ds(SUB * t, SUB)
         for pack in range(PACKS):
             even_out[pack, rows, :] = jnp.where(odd_place, first[pack], last[pack])
             odd_out[pack, rows, :] = jnp.where(odd_place, last[pack], first[pack])
+    stacked.wait()
 
 
 def factor(matrix):
@@ -115,12 +146,11 @@
 
 
 def main_kernel(points, *refs):
-    (visc, conv, spin, vaz, flux, faz, inc, edge) = refs[0:8]
-    sibling = refs[8:15]
-    halo_even, halo_odd, sib_even, sib_odd = refs[15:19]
-    cell_own, cell_sib = refs[19:21]
-    out_inc, out_defect = refs[21:23]
-    cells, couple, lower, centre, upper, lu, sides, solved, vmin, vplus, azd, src, out_cells = refs[23:]
+    conv, spin, edge, *lines = refs[0:8]
+    sib_conv, sib_spin, sib_stack = refs[8:11]
+    halo_even, halo_odd, sib_even, sib_odd = refs[11:15]
+    out_inc, out_defect = refs[15:17]
+    cells, couple, lower, centre, upper, lu, sides, solved, vmin, vplus, azd, src, out_cells = refs[17:]
 
     core = lax.axis_index("wn")
     odd_place = lax.rem(lax.axis_index("az"), 2)
@@ -130,16 +160,17 @@
 
     def put(value, t, place, chain, tile):
         start = pl.multiple_of(SUB * (2 * place + chain), SUB)
-        cells[2 * value + (t + chain) % 2 if isinstance(chain, int) else 2 * value + jnp.bitwise_xor(t, chain),
-              pl.ds(start, SUB), :] = tile
+        cells[2 * value + jnp.bitwise_xor(t, chain), pl.ds(start, SUB), :] = tile
 
     for chain, arrays, halos in (
-        (core, (visc, conv, spin, vaz, flux, faz, inc), (halo_even, halo_odd)),
-        (1 - core, sibling, (sib_even, sib_odd)),
+        (core, (conv, spin, edge, lines), (halo_even, halo_odd)),
+        (1 - core, (sib_conv, sib_spin, edge, lines_of(sib_stack)), (sib_even, sib_odd)),
     ):
-        read = tile_reader(*arrays, edge)
+        read = tile_reader(*arrays)
         sign = jnp.where(chain == 0, 1.0, -1.0).astype(jnp.float32)
         for value in range(VALUES):
+            if value == FLUID:
+                continue
             pack, slot, width = slot_of(value)
             for t in range(2):
                 tiles = [(0, read(value, t, 0)), (1, read(value, t, 1))]
@@ -173,11 +204,13 @@
 
     edges = cells[2 * EDGE, pl.ds(0, SUB, stride=SUB), :]
 
+    fluid_pack, fluid_slot, fluid_width = slot_of(FLUID)
+    fluid_tile = jnp.where(core == 0, halo_even[fluid_pack, 0:SUB, :], sib_even[fluid_pack, 0:SUB, :])
+    fluid_lane = jnp.where(odd_place == 0, fluid_slot * fluid_width, (fluid_slot - 1) * fluid_width)
+    fluid_tile = jnp.max(jnp.where(lane == fluid_lane, fluid_tile, 0.0), axis=1, keepdims=True)
+
     def fluid(k):
-        if k >= points:
-            return jnp.ones((SUB, LANES), jnp.float32)
-        kind = jnp.where(core == 0, cell_own[k], cell_sib[k])
-        return jnp.where(is_a, jnp.where(kind == 0, 1.0, 0.0).astype(jnp.float32), 1.0)
+        return jnp.where(is_a, jnp.broadcast_to(fluid_tile[k : k + 1, :], (SUB, LANES)), 1.0)
 
     def edge_scale(face_a, face_b):
         face = jnp.where(is_a, float(face_a), float(face_b))
@@ -189,8 +222,10 @@
     last = points - 1
     previous = None
     for k in range(points):
-        keep = [fluid(k)] * (NC - 1) + [one]
-        keep_above = [fluid(k + 1)] * (NC - 1) + [one]
+        solid = k < SOLID_MOST
+        if solid:
+            keep = [fluid(k)] * (NC - 1) + [one]
+            keep_above = [fluid(k + 1) if k + 1 < SOLID_MOST else one] * (NC - 1) + [one]
         if k < last:
             conv_out = [[both(a * NC + b, k, k + 1, b * NC + a) for b in range(NC)] for a in range(NC)]
             visc_out = [both(VISC + c, k, k + 1) for c in range(NC)]
@@ -199,9 +234,11 @@
             conv_out = [[jnp.where(is_a, face[a][b], -pltpu.roll(face[b][a], 1, 0)) for b in range(NC)] for a in range(NC)]
             raw = [at(VISC + c, k) for c in range(NC)]
             visc_out = [jnp.where(is_a, raw[c], pltpu.roll(raw[c], 1, 0)) for c in range(NC)]
-        conv_out = [[conv_out[a][b] * (keep[a] * keep_above[b]) for b in range(NC)] for a in range(NC)]
         scale = edge_scale(k, total - 2 - k)
-        visc_out = [visc_out[c] * scale * (keep[c] * keep_above[c]) for c in range(NC)]
+        visc_out = [visc_out[c] * scale for c in range(NC)]
+        if solid:
+            conv_out = [[conv_out[a][b] * (keep[a] * keep_above[b]) for b in range(NC)] for a in range(NC)]
+            visc_out = [visc_out[c] * (keep[c] * keep_above[c]) for c in range(NC)]
         if k == 0:
             scale = edge_scale(0, total - 1)
             visc_in = [jnp.where(is_a, 0.0, bt(VISC + c, 0) * scale) for c in range(NC)]
@@ -209,9 +246,9 @@
         vm, vp, az_diag, source, side = [], [], [], [], []
         for c in range(NC):
             here = both(VAZ + c, k, k)
-            vm.append(before(here) * keep[c])
-            vp.append(here * keep[c])
-            az_diag.append(vm[c] + vp[c] + (1.0 - keep[c]))
+            vm.append(before(here) * keep[c] if solid else before(here))
+            vp.append(here * keep[c] if solid else here)
+            az_diag.append(vm[c] + vp[c] + (1.0 - keep[c]) if solid else vm[c] + vp[c])
             flux_here = both(FLUX + c, k, k)
             if k == 0:
                 flux_below = jnp.where(is_a, 0.0, bt(FLUX + c, 1))
@@ -220,7 +257,8 @@
             else:
                 flux_below = jnp.where(is_a, at(FLUX + c, k - 1), pltpu.roll(at(FLUX + c, k), 1, 0))
             flux_side = both(FAZ + c, k, k)
-            source.append((flux_below - flux_here + before(flux_side) - flux_side) * keep[c])
+            flow = flux_below - flux_here + before(flux_side) - flux_side
+            source.append(flow * keep[c] if solid else flow)
             start = both(INC + c, k, k)
             side.append(source[c] + (vm[c] * before(start) + vp[c] * after(start)))
             vmin[k * NC + c], vplus[k * NC + c] = vm[c], vp[c]
@@ -230,7 +268,9 @@
         for c in range(NC):
             matrix[c][c] = visc_in[c] + visc_out[c] + az_diag[c]
         for n, (a, b) in enumerate(PAIRS):
-            skew = both(SKEW + n, k, k) * (keep[a] * keep[b])
+            skew = both(SKEW + n, k, k)
+            if solid:
+                skew = skew * (keep[a] * keep[b])
             matrix[a][b], matrix[b][a] = skew, -skew
         up = [[conv_out[a][b] - visc_out[a] if a == b else conv_out[a][b] for b in range(NC)] for a in range(NC)]
         for a in range(NC):
@@ -324,28 +364,39 @@
     assert count % 2 == 0
     even_pairs = [(a, a ^ 1) for a in range(count)]
     odd_pairs = [(a, (a + 1 if a % 2 else a - 1) % count) for a in range(count)]
-    vmem, smem = pl.BlockSpec(memory_space=pltpu.VMEM), pl.BlockSpec(memory_space=pltpu.SMEM)
+    vmem, hbm = (pl.BlockSpec(memory_space=m) for m in (pltpu.VMEM, pltpu.HBM))
 
     blocks = (NC * NC, points, line_count)
-    own = (visc_wn, conv_wn.reshape(blocks), spin.reshape(blocks), visc_az, flux_wn, flux_az, incr_prev)
+    conv, spin = conv_wn.reshape(blocks), spin.reshape(blocks)
     edge = edge_index.reshape(1, line_count)
+    lines = (visc_wn, flux_wn, visc_az, flux_az, incr_prev)
     pack = jax.ShapeDtypeStruct((PACKS, points, LANES), jnp.float32)
-    even, odd = pl.pallas_call(
+    block_array = pltpu.VMEM(blocks, jnp.float32)
+    even, odd, stack = pl.pallas_call(
         pack_kernel,
-        out_shape=(pack, pack),
-        in_specs=[vmem] * 8,
-        out_specs=(vmem, vmem),
+        out_shape=(pack, pack, jax.ShapeDtypeStruct(blocks, jnp.float32)),
+        in_specs=[hbm] * 9,
+        out_specs=(vmem, vmem, hbm),
+        scratch_shapes=[
+            block_array,
+            block_array,
+            pltpu.VMEM((1, line_count), jnp.int32),
+            block_array,
+            pltpu.SMEM((points,), jnp.int32),
+            pltpu.SemaphoreType.DMA((17,)),
+            pltpu.SemaphoreType.DMA,
+        ],
         name="pack_halo",
         compiler_params=pltpu.CompilerParams(vmem_limit_bytes=32 << 20),
-    )(*own, edge)
+    )(*(pltpu.with_memory_space_constraint(array, pltpu.HBM) for array in (conv, spin, edge, *lines, cell_type)))
+    even, odd, *late = lax.optimization_barrier((even, odd, conv, spin, stack))
     halo_even = lax.ppermute(even, "az", even_pairs)
     halo_odd = lax.ppermute(odd, "az", odd_pairs)
 
     def cross(array):
         return lax.ppermute(array, "wn", [(0, 1), (1, 0)])
 
-    sibling = tuple(cross(array) for array in own)
-    cell_sib = cross(cell_type)
+    sibling = tuple(cross(array) for array in late)
     sib_even, sib_odd = cross(halo_even), cross(halo_odd)
 
     step = pltpu.VMEM((points * NC * NC, SUB, LANES), jnp.float32)
@@ -354,7 +405,7 @@
     return pl.pallas_call(
         lambda *refs: main_kernel(points, *refs),
         out_shape=(out, out),
-        in_specs=[vmem] * 19 + [smem] * 2,
+        in_specs=[vmem] * 15,
         out_specs=(vmem, vmem),
         scratch_shapes=[pltpu.VMEM((2 * VALUES, SUB * SUB, LANES), jnp.float32)]
         + [step] * 5
@@ -362,7 +413,7 @@
         + [pltpu.VMEM((4 * NC, SUB * SUB, LANES), jnp.float32)],
         name="relax_lines",
         compiler_params=pltpu.CompilerParams(vmem_limit_bytes=40 << 20),
-    )(*own, edge, *sibling, halo_even, halo_odd, sib_even, sib_odd, cell_type, cell_sib)
+    )(conv, spin, edge, *lines, *sibling, halo_even, halo_odd, sib_even, sib_odd)
 
 
 def solution(mesh):

time: 29.5 us -> 20.8 us (0.71)
  local copies, waits for them, and re-layouts: 7.06 us -> 0.04 us
  starting transfers between devices: 9.38 us -> 8.13 us
  waiting for transfers between devices: 5.9 us -> 4.69 us
  Pallas kernels: 6.05 us -> 7.01 us
    unnamed x32 -> x16, local copies, waits for them, and re-layouts: 7.06 us -> 0.04 us
    pallas_call x1, Pallas kernels: 0.29 us -> 1.88 us  [per_device(): pl.pallas_call(pack_kernel, out_shape=(pack, pack, jax.ShapeDtypeStruct(b...]
    ppermute x10 -> x5, starting transfers between devices: 2.23 us -> 1.03 us  [cross(): return lax.ppermute(array, 'wn', [(0, 1), (1, 0)])]
    ppermute x10 -> x5, waiting for transfers between devices: 2.44 us -> 1.27 us  [cross(): return lax.ppermute(array, 'wn', [(0, 1), (1, 0)])]
    pallas_call x1, Pallas kernels: 5.76 us -> 5.13 us  [per_device(): pl.pallas_call(lambda *refs: main_kernel(points, *refs), out_shape=(out,...]
  transfers between devices with their start and end apart: 12 -> 7, of which waited for: 5 -> 2; matrix products, arithmetic and copies ran while one was open for 0% -> 0% of each run, Pallas kernels for 1% -> 0%
where the time goes in v2:
time: 20.8 us; the launch traced here: 20.6 us
  starting transfers between devices  8.13 us (39%)
  Pallas kernels  7.01 us (34%)
  waiting for transfers between devices  4.69 us (23%)
  between operations  0.77 us (4%)
    pallas_call x1, Pallas kernels, per_device(): pl.pallas_call(lambda *refs: main_kernel(points, *refs), out_shape=(out,...  5.13 us
    ppermute x1, starting transfers between devices, per_device(): halo_odd = lax.ppermute(odd, 'az', odd_pairs)  4.53 us
    ppermute x1, waiting for transfers between devices, per_device(): halo_odd = lax.ppermute(odd, 'az', odd_pairs)  3.41 us
    ppermute x1, starting transfers between devices, per_device(): halo_even = lax.ppermute(even, 'az', even_pairs)  2.57 us
    pallas_call x1, Pallas kernels, per_device(): pl.pallas_call(pack_kernel, out_shape=(pack, pack, jax.ShapeDtypeStruct(b...  1.88 us
    ppermute x5, waiting for transfers between devices, cross(): return lax.ppermute(array, 'wn', [(0, 1), (1, 0)])  1.27 us
    ppermute x5, starting transfers between devices, cross(): return lax.ppermute(array, 'wn', [(0, 1), (1, 0)])  1.03 us
  transfers between devices with their start and end apart: 7, of which 2 were waited for; matrix products, arithmetic and copies ran while one was open for 0% of the time, Pallas kernels for 0%

profile of v2, /device:TPU:0, one launch (start us, length us, event | category | flops | bytes accessed | tf_op | source)
XLA Modules:
  0.0 20.6 jit_solution(14288931249006752408)
XLA Ops:
  0.6 0.0 copy-start
  0.6 0.0 copy-start.1
  0.7 0.0 copy-start.2
  0.7 0.0 copy-start.3
  0.7 0.0 copy-start.4
  0.7 0.0 copy-start.5
  0.7 0.0 copy-start.6
  0.7 1.9 %pack_halo.1 = (f32[9,16,128]{2,1,0:T(8,128)S(1)}, f32[9,16,128]{2,1,0:T(8,128)S(1)}, f32[25,16,256]{2,1,0:T(8,128)S(1)}) custom-call(f32[25,16,256]{2,1,0:T(8,128)} %bitcast.3, f32[25,16,256]{2,1,0:T(8,128)} %bitcast.6, s32[1,256]{1,0:T(1,128)} %bitcast.9, f32[5,16,256]{2,1,0:T(8,128)} %refs_3_.1, f32[5,16,256]{2,1,0:T(8,128)} %refs_4_.1, ...), custom_call_target="tpu_custom_call" | custom-call | tf_op jit(solution)/shard_map/pack_halo/pallas_call | solution.py:375
  2.6 0.0 copy-start.7
  2.6 0.0 copy-done
  2.6 0.5 %collective-permute-start = (f32[25,16,256]{2,1,0:T(8,128)S(1)}, f32[25,16,256]{2,1,0:T(8,128)S(1)}, u32[]{:S(2)}, u32[]{:S(2)}) collective-permute-start(f32[25,16,256]{2,1,0:T(8,128)S(1)} %bitcast.4), channel_id=1, source_target_pairs={{0,1},{1,0},{2,3},{3,2},{4,5},{5,4},{6,7},{7,6},{8,9},{9,8},{10,11... | collective-permute-start | bytes 1228808 | tf_op jit(solution)/shard_map/ppermute | solution.py:397
  3.1 0.0 copy-done.1
  3.1 0.1 collective-permute-start.1
  3.2 0.4 %collective-permute-start.2 = (f32[25,16,256]{2,1,0:T(8,128)S(1)}, f32[25,16,256]{2,1,0:T(8,128)S(1)}, u32[]{:S(2)}, u32[]{:S(2)}) collective-permute-start(f32[25,16,256]{2,1,0:T(8,128)S(1)} %get-tuple-element.15), channel_id=1, source_target_pairs={{0,1},{1,0},{2,3},{3,2},{4,5},{5,4},{6,7},{7,6},{8,9},{9,8},{10,11... | collective-permute-start | bytes 1228808 | tf_op jit(solution)/shard_map/ppermute | solution.py:397
  3.6 2.6 %collective-permute-start.3 = (f32[9,16,128]{2,1,0:T(8,128)S(1)}, f32[9,16,128]{2,1,0:T(8,128)S(1)}, u32[]{:S(2)}, u32[]{:S(2)}) collective-permute-start(f32[9,16,128]{2,1,0:T(8,128)S(1)} %get-tuple-element.16), channel_id=1, source_target_pairs={{0,2},{2,0},{4,6},{6,4},{8,10},{10,8},{12,14},{14,12},{16,18},{18,... | collective-permute-start | bytes 221192 | tf_op jit(solution)/shard_map/ppermute | solution.py:393
  6.2 4.5 %collective-permute-start.4 = (f32[9,16,128]{2,1,0:T(8,128)S(1)}, f32[9,16,128]{2,1,0:T(8,128)S(1)}, u32[]{:S(2)}, u32[]{:S(2)}) collective-permute-start(f32[9,16,128]{2,1,0:T(8,128)S(1)} %get-tuple-element.17), channel_id=1, source_target_pairs={{0,30},{2,4},{4,2},{6,8},{8,6},{10,12},{12,10},{14,16},{16,14},{18... | collective-permute-start | bytes 221192 | tf_op jit(solution)/shard_map/ppermute | solution.py:394
  10.7 0.0 collective-permute-done.3.refs_11_
  10.7 0.0 collective-permute-start.5
  10.7 3.4 %collective-permute-done.4.refs_12_ = f32[9,16,128]{2,1,0:T(8,128)S(1)} collective-permute-done((f32[9,16,128]{2,1,0:T(8,128)S(1)}, f32[9,16,128]{2,1,0:T(8,128)S(1)}, u32[]{:S(2)}, u32[]{:S(2)}) %collective-permute-start.4) | collective-permute-done | bytes 73760 | tf_op jit(solution)/shard_map/ppermute | solution.py:394
  14.2 0.0 collective-permute-start.6
  14.2 0.0 collective-permute-done.5.refs_13_
  14.2 1.3 %collective-permute-done.6.refs_14_ = f32[9,16,128]{2,1,0:T(8,128)S(1)} collective-permute-done((f32[9,16,128]{2,1,0:T(8,128)S(1)}, f32[9,16,128]{2,1,0:T(8,128)S(1)}, u32[]{:S(2)}, u32[]{:S(2)}) %collective-permute-start.6) | collective-permute-done | bytes 73760 | tf_op jit(solution)/shard_map/ppermute | solution.py:397
  15.4 0.0 collective-permute-done.refs_8_
  15.4 0.0 collective-permute-done.1.refs_9_
  15.4 0.0 collective-permute-done.2.refs_10_
  15.4 0.0 copy-done.2
  15.5 0.0 copy-done.3
  15.5 0.0 copy-done.4
  15.5 0.0 copy-done.5
  15.5 0.0 copy-done.6
  15.5 0.0 copy-done.7
  15.5 5.1 %relax_lines.1 = (f32[5,16,256]{2,1,0:T(8,128)}, f32[5,16,256]{2,1,0:T(8,128)}) custom-call(f32[25,16,256]{2,1,0:T(8,128)S(1)} %bitcast.5, f32[25,16,256]{2,1,0:T(8,128)S(1)} %bitcast.8, s32[1,256]{1,0:T(1,128)S(1)} %bitcast.10, f32[5,16,256]{2,1,0:T(8,128)S(1)} %copy-done.2, f32[5,16,256]{2,1,0:T(8,128)S(1)} %copy-done.3, f32[5,16,256]{2,1,0:T(8,128)S(1)} %copy-done.4, ...), custom_call_target="tpu_custom_call" | custom-call | tf_op jit(solution)/shard_map/relax_lines/pallas_call | solution.py:405
Async XLA Ops:
  0.6 2.0 %copy-start = (f32[5,5,16,256]{3,2,1,0:T(8,128)S(1)}, f32[5,5,16,256]{3,2,1,0:T(8,128)}, u32[]{:S(2)}) copy-start(f32[5,5,16,256]{3,2,1,0:T(8,128)} %param.10) | copy-start | bytes 1228804
  0.6 2.5 %copy-start.1 = (f32[5,5,16,256]{3,2,1,0:T(8,128)S(1)}, f32[5,5,16,256]{3,2,1,0:T(8,128)}, u32[]{:S(2)}) copy-start(f32[5,5,16,256]{3,2,1,0:T(8,128)} %param.11) | copy-start | bytes 1228804
  0.7 14.8 %copy-start.2 = (f32[5,16,256]{2,1,0:T(8,128)S(1)}, f32[5,16,256]{2,1,0:T(8,128)}, u32[]{:S(2)}) copy-start(f32[5,16,256]{2,1,0:T(8,128)} %refs_3_.1) | copy-start | bytes 245764
  0.7 14.8 %copy-start.3 = (f32[5,16,256]{2,1,0:T(8,128)S(1)}, f32[5,16,256]{2,1,0:T(8,128)}, u32[]{:S(2)}) copy-start(f32[5,16,256]{2,1,0:T(8,128)} %refs_4_.1) | copy-start | bytes 245764
  0.7 14.8 %copy-start.4 = (f32[5,16,256]{2,1,0:T(8,128)S(1)}, f32[5,16,256]{2,1,0:T(8,128)}, u32[]{:S(2)}) copy-start(f32[5,16,256]{2,1,0:T(8,128)} %refs_5_.1) | copy-start | bytes 245764
  0.7 14.8 %copy-start.5 = (f32[5,16,256]{2,1,0:T(8,128)S(1)}, f32[5,16,256]{2,1,0:T(8,128)}, u32[]{:S(2)}) copy-start(f32[5,16,256]{2,1,0:T(8,128)} %refs_6_.1) | copy-start | bytes 245764
  0.7 14.8 %copy-start.6 = (f32[5,16,256]{2,1,0:T(8,128)S(1)}, f32[5,16,256]{2,1,0:T(8,128)}, u32[]{:S(2)}) copy-start(f32[5,16,256]{2,1,0:T(8,128)} %refs_7_.1) | copy-start | bytes 245764
  2.6 12.9 %copy-start.7 = (s32[256]{0:T(256)S(1)}, s32[256]{0:T(256)}, u32[]{:S(2)}) copy-start(s32[256]{0:T(256)} %param.17) | copy-start | bytes 3076
  2.6 12.8 %collective-permute-start = (f32[25,16,256]{2,1,0:T(8,128)S(1)}, f32[25,16,256]{2,1,0:T(8,128)S(1)}, u32[]{:S(2)}, u32[]{:S(2)}) collective-permute-start(f32[25,16,256]{2,1,0:T(8,128)S(1)} %bitcast.4), channel_id=1, source_target_pairs={{0,1},{1,0},{2,3},{3,2},{4,5},{5,4},{6,7},{7,6},{8,9},{9,8},{10,11... | collective-permute-start | bytes 1228808 | tf_op jit(solution)/shard_map/ppermute | solution.py:397
  3.1 12.3 %collective-permute-start.1 = (f32[25,16,256]{2,1,0:T(8,128)S(1)}, f32[25,16,256]{2,1,0:T(8,128)S(1)}, u32[]{:S(2)}, u32[]{:S(2)}) collective-permute-start(f32[25,16,256]{2,1,0:T(8,128)S(1)} %bitcast.7), channel_id=1, source_target_pairs={{0,1},{1,0},{2,3},{3,2},{4,5},{5,4},{6,7},{7,6},{8,9},{9,8},{10,11... | collective-permute-start | bytes 1228808 | tf_op jit(solution)/shard_map/ppermute | solution.py:397
  3.2 12.2 %collective-permute-start.2 = (f32[25,16,256]{2,1,0:T(8,128)S(1)}, f32[25,16,256]{2,1,0:T(8,128)S(1)}, u32[]{:S(2)}, u32[]{:S(2)}) collective-permute-start(f32[25,16,256]{2,1,0:T(8,128)S(1)} %get-tuple-element.15), channel_id=1, source_target_pairs={{0,1},{1,0},{2,3},{3,2},{4,5},{5,4},{6,7},{7,6},{8,9},{9,8},{10,11... | collective-permute-start | bytes 1228808 | tf_op jit(solution)/shard_map/ppermute | solution.py:397
  3.6 7.1 %collective-permute-start.3 = (f32[9,16,128]{2,1,0:T(8,128)S(1)}, f32[9,16,128]{2,1,0:T(8,128)S(1)}, u32[]{:S(2)}, u32[]{:S(2)}) collective-permute-start(f32[9,16,128]{2,1,0:T(8,128)S(1)} %get-tuple-element.16), channel_id=1, source_target_pairs={{0,2},{2,0},{4,6},{6,4},{8,10},{10,8},{12,14},{14,12},{16,18},{18,... | collective-permute-start | bytes 221192 | tf_op jit(solution)/shard_map/ppermute | solution.py:393
  6.2 7.9 %collective-permute-start.4 = (f32[9,16,128]{2,1,0:T(8,128)S(1)}, f32[9,16,128]{2,1,0:T(8,128)S(1)}, u32[]{:S(2)}, u32[]{:S(2)}) collective-permute-start(f32[9,16,128]{2,1,0:T(8,128)S(1)} %get-tuple-element.17), channel_id=1, source_target_pairs={{0,30},{2,4},{4,2},{6,8},{8,6},{10,12},{12,10},{14,16},{16,14},{18... | collective-permute-start | bytes 221192 | tf_op jit(solution)/shard_map/ppermute | solution.py:394
  10.7 3.4 %collective-permute-start.5 = (f32[9,16,128]{2,1,0:T(8,128)S(1)}, f32[9,16,128]{2,1,0:T(8,128)S(1)}, u32[]{:S(2)}, u32[]{:S(2)}) collective-permute-start(f32[9,16,128]{2,1,0:T(8,128)S(1)} %collective-permute-done.3.refs_11_), channel_id=1, source_target_pairs={{0,1},{1,0},{2,3},{3,2},{4,5},{5,4},{6,7},{7,6},{8,9},{9,8},{10,11... | collective-permute-start | bytes 221192 | tf_op jit(solution)/shard_map/ppermute | solution.py:397
  14.2 1.3 %collective-permute-start.6 = (f32[9,16,128]{2,1,0:T(8,128)S(1)}, f32[9,16,128]{2,1,0:T(8,128)S(1)}, u32[]{:S(2)}, u32[]{:S(2)}) collective-permute-start(f32[9,16,128]{2,1,0:T(8,128)S(1)} %collective-permute-done.4.refs_12_), channel_id=1, source_target_pairs={{0,1},{1,0},{2,3},{3,2},{4,5},{5,4},{6,7},{7,6},{8,9},{9,8},{10,11... | collective-permute-start | bytes 221192 | tf_op jit(solution)/shard_map/ppermute | solution.py:397

commit v3 on v2

v3 whole, which is shorter than its diff:
```python
import jax
import jax.numpy as jnp
from jax import lax
from jax.experimental import pallas as pl
from jax.experimental.pallas import tpu as pltpu
from jax.sharding import PartitionSpec as P

S = 8
SWEEPS = 2
OUTER_SCALE = 0.25
NC = 5
LANES = 128
SUB = 8
NEAR = 2 * S
FAR = 3 * S

CONV, SKEW, VISC, FLUX, EDGE, FLUID = 0, 25, 35, 40, 45, 46
NEAR_VALUES = 47
VAZ, FAZ, INC = 47, 52, 57
VALUES = 62
BELOW, STORED = 62, 67
SLOTS = 18
SOLID_MOST = 4
NEAR_SLOTS = LANES // NEAR
FAR_SLOTS = LANES // FAR
NEAR_PACKS = -(-NEAR_VALUES // NEAR_SLOTS)
FAR_PACKS = -(-(VALUES - NEAR_VALUES) // FAR_SLOTS)
PACKS = NEAR_PACKS + FAR_PACKS
PAIRS = [(a, b) for a in range(NC) for b in range(a + 1, NC)]


def slot_of(value):
    if value < NEAR_VALUES:
        return value // NEAR_SLOTS, value % NEAR_SLOTS, NEAR
    other = value - NEAR_VALUES
    return NEAR_PACKS + other // FAR_SLOTS, other % FAR_SLOTS, FAR


def tile_reader(conv, spin, edge, lines):
    def read(value, t, lt):
        rows, lanes = pl.ds(SUB * t, SUB), pl.ds(LANES * lt, LANES)
        if value < SKEW:
            return conv[value, rows, lanes]
        if value < VISC:
            a, b = PAIRS[value - SKEW]
            return spin[a * NC + b, rows, lanes] - spin[b * NC + a, rows, lanes]
        if value == EDGE:
            return jnp.broadcast_to(edge[0:1, lanes].astype(jnp.float32), (SUB, LANES))
        for first, ref in zip((VISC, FLUX, VAZ, FAZ, INC), lines):
            if first <= value < first + NC:
                return ref[value - first, rows, lanes]

    return read


def parts_of(ref):
    lines = [ref.at[pl.ds(2 * NC * NC + NC * n, NC)] for n in range(5)]
    return ref.at[pl.ds(0, NC * NC)], ref.at[pl.ds(NC * NC, NC * NC)], lines


def mirror(tile, chain):
    row = lax.broadcasted_iota(jnp.int32, (SUB, LANES), 0)
    return jnp.take_along_axis(tile, jnp.where(chain == 0, row, SUB - 1 - row), axis=0)


def pack_kernel(conv_hbm, spin_hbm, edge_hbm, visc_hbm, flux_hbm, vaz_hbm, faz_hbm, inc_hbm, cells_hbm,
                even_out, odd_out, bulk, edge, cells, sems):
    odd_place = lax.rem(lax.axis_index("az"), 2) == 1
    core = lax.axis_index("wn")
    conv, spin, lines = parts_of(bulk)
    copies = []
    for n in range(NC):
        part = pl.ds(NC * n, NC)
        copies.append(pltpu.make_async_copy(conv_hbm.at[part], conv.at[part], sems.at[n]))
    for n, ref in enumerate((visc_hbm, flux_hbm, vaz_hbm, faz_hbm, inc_hbm)):
        copies.append(pltpu.make_async_copy(ref, lines[n], sems.at[NC + n]))
    for n in range(NC):
        part = pl.ds(NC * n, NC)
        copies.append(pltpu.make_async_copy(spin_hbm.at[part], spin.at[part], sems.at[2 * NC + n]))
    copies.append(pltpu.make_async_copy(edge_hbm, edge, sems.at[3 * NC]))
    copies.append(pltpu.make_async_copy(cells_hbm, cells, sems.at[3 * NC + 1]))
    for copy in copies:
        copy.start()
    read = tile_reader(conv, spin, edge, lines)
    lane = lax.broadcasted_iota(jnp.int32, (SUB, LANES), 1)
    row = lax.broadcasted_iota(jnp.int32, (SUB, LANES), 0)
    blank = jnp.zeros((SUB, LANES), jnp.float32)
    first = [[blank] * PACKS for _ in range(2)]
    last = [[blank] * PACKS for _ in range(2)]
    late = list(range(SKEW, VISC)) + [EDGE, FLUID]
    for value in [v for v in range(VALUES) if v not in late] + late:
        for group, begin in enumerate([NC * n for n in range(NC)] + [VISC, FLUX, VAZ, FAZ, INC]):
            if value == begin:
                copies[group].wait()
        if value == late[0]:
            for copy in copies[2 * NC :]:
                copy.wait()
        pack, slot, width = slot_of(value)
        low = slot * width
        here = (lane >= low) & (lane < low + width)
        low = (LANES - width + slot * width) % LANES
        there = (lane >= low) & (lane < low + width)
        for t in range(2):
            if value == FLUID:
                one = jnp.ones((SUB, LANES), jnp.float32)
                for p in range(SOLID_MOST if t == 0 else 0):
                    one = jnp.where(row == p, jnp.where(cells[p] == 0, 1.0, 0.0).astype(jnp.float32), one)
                two = one
            else:
                one, two = read(value, t, 0), read(value, t, 1)
                if slot:
                    one, two = pltpu.roll(one, slot * width, 1), pltpu.roll(two, slot * width, 1)
            first[t][pack] = jnp.where(here, one, first[t][pack])
            last[t][pack] = jnp.where(there, two, last[t][pack])
    for pack in range(PACKS):
        for t in range(2):
            rows = pl.ds(SUB * t, SUB)
            one = mirror(jnp.where(core == 0, first[t][pack], first[1 - t][pack]), core)
            two = mirror(jnp.where(core == 0, last[t][pack], last[1 - t][pack]), core)
            even_out[pack, rows, :] = jnp.where(odd_place, one, two)
            odd_out[pack, rows, :] = jnp.where(odd_place, two, one)


def factor(matrix):
    work = [list(row) for row in matrix]
    scale = []
    for p in range(NC):
        scale.append(1.0 / work[p][p])
        for i in range(p + 1, NC):
            work[i][p] = work[i][p] * scale[p]
            for j in range(p + 1, NC):
                work[i][j] = work[i][j] - work[i][p] * work[p][j]
    for p in range(NC):
        work[p][p] = scale[p]
    return work


def substitute(work, side):
    side = list(side)
    for p in range(NC):
        for i in range(p + 1, NC):
            side[i] = side[i] - work[i][p] * side[p]
    for i in reversed(range(NC)):
        for j in range(i + 1, NC):
            side[i] = side[i] - work[i][j] * side[j]
        side[i] = side[i] * work[i][i]
    return side


def dot(row, column):
    terms = [a * b for a, b in zip(row, column)]
    return (terms[0] + terms[1]) + (terms[2] + terms[3]) + terms[4]


def times(matrix, vector):
    return [dot(row, vector) for row in matrix]


def product(left, right):
    columns = [[right[i][j] for i in range(NC)] for j in range(NC)]
    return [[dot(left[i], columns[j]) for j in range(NC)] for i in range(NC)]


def put(cells, value, t, place, chain, tile):
    is_a = chain == 0
    copies = [(value, 1, 0 if value < SKEW or VISC <= value < VISC + NC else 1)]
    if FLUX <= value < FLUX + NC:
        copies.append((value - FLUX + BELOW, 2, 0))
    for target, slot_a, slot_b in copies:
        if value < SKEW:
            target = jnp.where(is_a, value, value % NC * NC + value // NC)
            tile = tile * jnp.where(is_a, 1.0, -1.0).astype(jnp.float32)
        start = SUB * (SUB * t + jnp.where(is_a, slot_a, slot_b)) + 2 * place + chain
        cells[target, pl.ds(start, SUB, stride=SUB), :] = tile


def put_halo(cells, halo, place, chain):
    for value in range(VALUES):
        if value == FLUID:
            continue
        pack, slot, width = slot_of(value)
        for t in range(2):
            tile = halo[pack, pl.ds(SUB * t, SUB), :]
            if slot:
                tile = pltpu.roll(tile, LANES - slot * width, 1)
            put(cells, value, t, place, chain, tile)


def collect_kernel(bulk, sib_bulk, edge, halo_even, sib_even, cells):
    core = lax.axis_index("wn")
    even_place = 2 + lax.rem(lax.axis_index("az"), 2)
    for chain, array, halo in ((core, bulk, halo_even), (1 - core, sib_bulk, sib_even)):
        conv, spin, lines = parts_of(array)
        read = tile_reader(conv, spin, edge, lines)
        for value in range(VALUES):
            if value == FLUID:
                continue
            for t in range(2):
                for lt in range(2):
                    tile = mirror(read(value, t, lt), chain)
                    put(cells, value, jnp.bitwise_xor(t, chain), lt, chain, tile)
        put_halo(cells, halo, even_place, chain)


def main_kernel(points, *refs):
    cells_in, halo_odd, sib_odd, out_inc, out_defect, cells = refs[0:6]
    couple, conv_face, visc_face, diagonal, skews, lu, sides, solved, vmin, vplus, azd, src, out_cells = refs[6:]

    core = lax.axis_index("wn")
    odd_place = lax.rem(lax.axis_index("az"), 2)
    row = lax.broadcasted_iota(jnp.int32, (SUB, LANES), 0)
    lane = lax.broadcasted_iota(jnp.int32, (SUB, LANES), 1)
    is_a = lax.rem(row, 2) == 0
    put_halo(cells, halo_odd, 3 - odd_place, core)
    put_halo(cells, sib_odd, 3 - odd_place, 1 - core)

    def at(value, k):
        return cells[value, pl.ds(SUB * (k + 1), SUB), :]

    def before(x):
        y = pltpu.roll(x, S, 1)
        return jnp.where(lane < S, pltpu.roll(y, 2, 0), y)

    def after(x):
        y = pltpu.roll(x, LANES - S, 1)
        return jnp.where(lane >= LANES - S, pltpu.roll(y, SUB - 2, 0), y)

    def swap(x):
        return jnp.where(is_a, pltpu.roll(x, SUB - 1, 0), pltpu.roll(x, 1, 0))

    edges = at(EDGE, 0)

    fluid_pack, fluid_slot, fluid_width = slot_of(FLUID)
    fluid_tile = jnp.where(core == 0, halo_odd[fluid_pack, 0:SUB, :], sib_odd[fluid_pack, 0:SUB, :])
    fluid_lane = jnp.where(odd_place == 0, (fluid_slot - 1) * fluid_width, fluid_slot * fluid_width)
    fluid_tile = jnp.max(jnp.where(lane == fluid_lane, fluid_tile, 0.0), axis=1, keepdims=True)

    def fluid(k):
        return jnp.where(is_a, jnp.broadcast_to(fluid_tile[k : k + 1, :], (SUB, LANES)), 1.0)

    def edge_scale(face_a, face_b):
        face = jnp.where(is_a, float(face_a), float(face_b))
        return jnp.where(face < edges, 1.0, OUTER_SCALE)

    one = jnp.ones((SUB, LANES), jnp.float32)
    total = 2 * points
    last = points - 1
    previous = None
    for k in range(points):
        solid = k < SOLID_MOST
        if solid:
            keep = [fluid(k)] * (NC - 1) + [one]
            keep_above = [fluid(k + 1) if k + 1 < SOLID_MOST else one] * (NC - 1) + [one]
        if k < last:
            conv_out = [[at(a * NC + b, k) for b in range(NC)] for a in range(NC)]
            visc_out = [at(VISC + c, k) for c in range(NC)]
        else:
            face = [[at(a * NC + b, k) for b in range(NC)] for a in range(NC)]
            conv_out = [[jnp.where(is_a, face[a][b], -pltpu.roll(face[b][a], 1, 0)) for b in range(NC)] for a in range(NC)]
            raw = [at(VISC + c, k) for c in range(NC)]
            visc_out = [jnp.where(is_a, raw[c], pltpu.roll(raw[c], 1, 0)) for c in range(NC)]
        scale = edge_scale(k, total - 2 - k)
        visc_out = [visc_out[c] * scale for c in range(NC)]
        if solid:
            conv_out = [[conv_out[a][b] * (keep[a] * keep_above[b]) for b in range(NC)] for a in range(NC)]
            visc_out = [visc_out[c] * (keep[c] * keep_above[c]) for c in range(NC)]
        if k == 0:
            scale = edge_scale(0, total - 1)
            visc_in = [jnp.where(is_a, 0.0, at(VISC + c, -1) * scale) for c in range(NC)]

        vm, vp, az_diag, source, side = [], [], [], [], []
        for c in range(NC):
            here = at(VAZ + c, k)
            vm.append(before(here) * keep[c] if solid else before(here))
            vp.append(here * keep[c] if solid else here)
            az_diag.append(vm[c] + vp[c] + (1.0 - keep[c]) if solid else vm[c] + vp[c])
            flux_here, flux_below = at(FLUX + c, k), at(BELOW + c, k)
            if k == 0:
                flux_below = jnp.where(is_a, 0.0, flux_below)
            elif k == last:
                flux_below = jnp.where(is_a, flux_below, pltpu.roll(flux_here, 1, 0))
            flux_side = at(FAZ + c, k)
            flow = flux_below - flux_here + before(flux_side) - flux_side
            source.append(flow * keep[c] if solid else flow)
            start = at(INC + c, k)
            side.append(source[c] + (vm[c] * before(start) + vp[c] * after(start)))
            vmin[k * NC + c], vplus[k * NC + c] = vm[c], vp[c]
            azd[k * NC + c], src[k * NC + c] = az_diag[c], source[c]

        matrix = [[None] * NC for _ in range(NC)]
        for c in range(NC):
            matrix[c][c] = visc_in[c] + visc_out[c] + az_diag[c]
        for n, (a, b) in enumerate(PAIRS):
            skew = at(SKEW + n, k)
            if solid:
                skew = skew * (keep[a] * keep[b])
            skews[k * len(PAIRS) + n] = skew
            matrix[a][b], matrix[b][a] = skew, -skew
        up = [[conv_out[a][b] - visc_out[a] if a == b else conv_out[a][b] for b in range(NC)] for a in range(NC)]
        for a in range(NC):
            diagonal[k * NC + a], visc_face[k * NC + a] = matrix[a][a], visc_out[a]
            for b in range(NC):
                conv_face[k * 25 + a * NC + b] = conv_out[a][b]
        if previous is not None:
            conv_in, couple_in, y_in = previous
            low = [[-visc_in[a] - conv_in[a][a] if a == b else -conv_in[b][a] for b in range(NC)] for a in range(NC)]
            moved = product(low, couple_in)
            matrix = [[matrix[a][b] - moved[a][b] for b in range(NC)] for a in range(NC)]
            shift = times(low, y_in)
            side = [side[c] - shift[c] for c in range(NC)]
        work = factor(matrix)
        columns = [substitute(work, [up[i][j] for i in range(NC)]) for j in range(NC)]
        couple_now = [[columns[j][i] for j in range(NC)] for i in range(NC)]
        y = substitute(work, side)
        for a in range(NC):
            sides[k * NC + a] = y[a]
            for b in range(NC):
                lu[k * 25 + a * NC + b] = work[a][b]
                couple[k * 25 + a * NC + b] = couple_now[a][b]
        previous = (conv_out, couple_now, y)
        visc_in = visc_out

    def block(ref, k):
        return [[ref[k * 25 + a * NC + b] for b in range(NC)] for a in range(NC)]

    def below(k, x):
        face, visc = block(conv_face, k - 1), vector(visc_face, k - 1)
        return [visc[c] * x[c] + dot([face[r][c] for r in range(NC)], x) for c in range(NC)]

    def vector(ref, k):
        return [ref[k * NC + c] for c in range(NC)]

    couple_end = couple_now
    crossed = product(couple_end, [[swap(couple_end[a][b]) for b in range(NC)] for a in range(NC)])
    meeting = factor([[(1.0 if a == b else 0.0) - crossed[a][b] for b in range(NC)] for a in range(NC)])

    def finish(y):
        shift = times(couple_end, [swap(v) for v in y])
        x = substitute(meeting, [y[c] - shift[c] for c in range(NC)])
        for c in range(NC):
            solved[last * NC + c] = x[c]
        for k in reversed(range(last)):
            shift = times(block(couple, k), x)
            y_here = vector(sides, k)
            x = [y_here[c] - shift[c] for c in range(NC)]
            for c in range(NC):
                solved[k * NC + c] = x[c]

    finish(y)
    for sweep in range(1, SWEEPS):
        for k in range(points):
            source, vm, vp, x = vector(src, k), vector(vmin, k), vector(vplus, k), vector(solved, k)
            side = [source[c] + (vm[c] * before(x[c]) + vp[c] * after(x[c])) for c in range(NC)]
            if k:
                shift = below(k, y)
                side = [side[c] + shift[c] for c in range(NC)]
            y = substitute(block(lu, k), side)
            for c in range(NC):
                sides[k * NC + c] = y[c]
        finish(y)

    for k in range(points):
        source, vm, vp, x = vector(src, k), vector(vmin, k), vector(vplus, k), vector(solved, k)
        diag = vector(azd, k)
        beyond = vector(solved, k + 1) if k < last else [swap(v) for v in x]
        visc_out, main = vector(visc_face, k), vector(diagonal, k)
        applied = [main[c] * x[c] - visc_out[c] * beyond[c] for c in range(NC)]
        outer = times(block(conv_face, k), beyond)
        applied = [applied[c] + outer[c] for c in range(NC)]
        for n, (a, b) in enumerate(PAIRS):
            skew = skews[k * len(PAIRS) + n]
            applied[a] = applied[a] + skew * x[b]
            applied[b] = applied[b] - skew * x[a]
        if k:
            under = below(k, vector(solved, k - 1))
            applied = [applied[c] - under[c] for c in range(NC)]
        place = jnp.where(core == 0, k % SUB, SUB - 1 - k % SUB)
        t = jnp.where(core == 0, k // SUB, 1 - k // SUB)
        for c in range(NC):
            offline = vm[c] * before(x[c]) + vp[c] * after(x[c])
            defect = (source[c] + offline - applied[c]) / diag[c]
            out_cells[2 * c + t, pl.ds(place, SUB, stride=SUB), :] = x[c]
            out_cells[2 * (NC + c) + t, pl.ds(place, SUB, stride=SUB), :] = defect
    for c in range(NC):
        for t in range(2):
            for lt in range(2):
                start = pl.multiple_of(SUB * (2 * lt + core), SUB)
                rows, lanes = pl.ds(SUB * t, SUB), pl.ds(LANES * lt, LANES)
                out_inc[c, rows, lanes] = out_cells[2 * c + t, pl.ds(start, SUB), :]
                out_defect[c, rows, lanes] = out_cells[2 * (NC + c) + t, pl.ds(start, SUB), :]


def per_device(visc_wn, conv_wn, spin, visc_az, flux_wn, flux_az, incr_prev, cell_type, edge_index):
    components, points, line_count = visc_wn.shape
    assert components == NC and points == 2 * SUB and line_count == 2 * LANES
    count = lax.axis_size("az")
    assert count % 2 == 0
    even_pairs = [(a, a ^ 1) for a in range(count)]
    odd_pairs = [(a, (a + 1 if a % 2 else a - 1) % count) for a in range(count)]
    vmem, hbm = (pl.BlockSpec(memory_space=m) for m in (pltpu.VMEM, pltpu.HBM))

    blocks = (NC * NC, points, line_count)
    conv, spin = conv_wn.reshape(blocks), spin.reshape(blocks)
    edge = edge_index.reshape(1, line_count)
    lines = (visc_wn, flux_wn, visc_az, flux_az, incr_prev)
    pack = jax.ShapeDtypeStruct((PACKS, points, LANES), jnp.float32)
    block_array = pltpu.VMEM(blocks, jnp.float32)
    bulk = jax.ShapeDtypeStruct((2 * NC * NC + 5 * NC, points, line_count), jnp.float32)
    from_hbm = [pltpu.with_memory_space_constraint(array, pltpu.HBM) for array in (conv, spin, edge, *lines, cell_type)]
    even, odd, bulk, edge = pl.pallas_call(
        pack_kernel,
        out_shape=(pack, pack, bulk, jax.ShapeDtypeStruct((1, line_count), jnp.int32)),
        in_specs=[hbm] * 9,
        out_specs=(vmem,) * 4,
        scratch_shapes=[pltpu.SMEM((points,), jnp.int32), pltpu.SemaphoreType.DMA((3 * NC + 2,))],
        name="pack_halo",
        compiler_params=pltpu.CompilerParams(vmem_limit_bytes=16 << 20),
    )(*from_hbm)
    halo_even = lax.ppermute(even, "az", even_pairs)
    halo_odd = lax.ppermute(odd, "az", odd_pairs)

    def cross(array):
        return lax.ppermute(array, "wn", [(0, 1), (1, 0)])

    sib_bulk = cross(bulk)
    sib_even, sib_odd = cross(halo_even), cross(halo_odd)

    tiles = jax.ShapeDtypeStruct((STORED, SLOTS * SUB, LANES), jnp.float32)
    cells = pl.pallas_call(
        collect_kernel,
        out_shape=tiles,
        in_specs=[vmem] * 5,
        out_specs=vmem,
        name="collect_lines",
        compiler_params=pltpu.CompilerParams(vmem_limit_bytes=16 << 20),
    )(bulk, sib_bulk, edge, halo_even, sib_even)

    def step(count):
        return pltpu.VMEM((points * count, SUB, LANES), jnp.float32)

    out = jax.ShapeDtypeStruct((NC, points, line_count), jnp.float32)
    increment, defect, _ = pl.pallas_call(
        lambda *refs: main_kernel(points, *refs),
        out_shape=(out, out, tiles),
        in_specs=[vmem] * 3,
        out_specs=(vmem, vmem, vmem),
        input_output_aliases={0: 2},
        scratch_shapes=[step(n) for n in (NC * NC, NC * NC, NC, NC, len(PAIRS), NC * NC)]
        + [step(NC)] * 6
        + [pltpu.VMEM((4 * NC, SUB * SUB, LANES), jnp.float32)],
        name="relax_lines",
        compiler_params=pltpu.CompilerParams(vmem_limit_bytes=24 << 20),
    )(cells, halo_odd, sib_odd)
    return increment, defect


def solution(mesh):
    in_specs = (
        P(None, "wn", "az"),
        P(None, None, "wn", "az"),
        P(None, None, "wn", "az"),
        P(None, "wn", "az"),
        P(None, "wn", "az"),
        P(None, "wn", "az"),
        P(None, "wn", "az"),
        P("wn"),
        P("az"),
    )
    out_specs = (P(None, "wn", "az"), P(None, "wn", "az"))
    return jax.shard_map(
        per_device, mesh=mesh, in_specs=in_specs, out_specs=out_specs, check_vma=False
    )
```

time: 20.8 us -> 19.4 us (0.933)
  waiting for transfers between devices: 4.69 us -> 4.01 us
  starting transfers between devices: 8.13 us -> 7.62 us
    pallas_call x1, Pallas kernels: 5.13 us -> 4.24 us  [per_device(): pl.pallas_call(lambda *refs: main_kernel(points, *refs), out_shape=(out,...]
    pallas_call x1 -> x2, Pallas kernels: 1.88 us -> 2.67 us  [the longest x1 2.02 us: per_device(): pl.pallas_call(pack_kernel, out_shape=(pack, pack, bulk, jax.ShapeDtypeSt...]
    ppermute x5 -> x3, waiting for transfers between devices: 1.27 us -> 0.6 us  [cross(): return lax.ppermute(array, 'wn', [(0, 1), (1, 0)])]
    ppermute x5 -> x3, starting transfers between devices: 1.03 us -> 0.52 us  [cross(): return lax.ppermute(array, 'wn', [(0, 1), (1, 0)])]
  transfers between devices with their start and end apart: 7 -> 5, of which waited for: 2 -> 2; matrix products, arithmetic and copies ran while one was open for 0% -> 0% of each run, Pallas kernels for 0% -> 3%
where the time goes in v3:
time: 19.4 us; the launch traced here: 19.2 us
  starting transfers between devices  7.62 us (39%)
  Pallas kernels  6.91 us (36%)
  waiting for transfers between devices  4.01 us (21%)
  between operations  0.66 us (3%)
    ppermute x1, starting transfers between devices, per_device(): halo_odd = lax.ppermute(odd, 'az', odd_pairs)  4.53 us
    pallas_call x1, Pallas kernels, per_device(): pl.pallas_call(lambda *refs: main_kernel(points, *refs), out_shape=(out,...  4.24 us
    ppermute x1, waiting for transfers between devices, per_device(): halo_odd = lax.ppermute(odd, 'az', odd_pairs)  3.41 us
    ppermute x1, starting transfers between devices, per_device(): halo_even = lax.ppermute(even, 'az', even_pairs)  2.56 us
    pallas_call x1, Pallas kernels, per_device(): pl.pallas_call(pack_kernel, out_shape=(pack, pack, bulk, jax.ShapeDtypeSt...  2.02 us
    pallas_call x1, Pallas kernels, per_device(): pl.pallas_call(collect_kernel, out_shape=tiles, in_specs=[vmem] * 5, out_...  0.65 us
    ppermute x3, waiting for transfers between devices, cross(): return lax.ppermute(array, 'wn', [(0, 1), (1, 0)])  0.6 us
    ppermute x3, starting transfers between devices, cross(): return lax.ppermute(array, 'wn', [(0, 1), (1, 0)])  0.52 us
  transfers between devices with their start and end apart: 5, of which 2 were waited for; matrix products, arithmetic and copies ran while one was open for 0% of the time, Pallas kernels for 3%

profile of v3, /device:TPU:0, one launch (start us, length us, event | category | flops | bytes accessed | tf_op | source)
XLA Modules:
  0.0 19.2 jit_solution(10815809905705530656)
XLA Ops:
  0.6 2.0 %pack_halo.1 = (f32[9,16,128]{2,1,0:T(8,128)S(1)}, f32[9,16,128]{2,1,0:T(8,128)S(1)}, f32[75,16,256]{2,1,0:T(8,128)S(1)}, s32[1,256]{1,0:T(1,128)S(1)}) custom-call(f32[25,16,256]{2,1,0:T(8,128)} %bitcast.3, f32[25,16,256]{2,1,0:T(8,128)} %bitcast.4, s32[1,256]{1,0:T(1,128)} %bitcast.5, f32[5,16,256]{2,1,0:T(8,128)} %visc_hbm.1, f32[5,16,256]{2,1,0:T(8,128)} %flux_hbm.1, ...), custom_call_target="tpu_custom_call" | custom-call | tf_op jit(solution)/shard_map/pack_halo/pallas_call | solution.py:410
  2.7 0.5 %collective-permute-start = (f32[75,16,256]{2,1,0:T(8,128)S(1)}, f32[75,16,256]{2,1,0:T(8,128)S(1)}, u32[]{:S(2)}, u32[]{:S(2)}) collective-permute-start(f32[75,16,256]{2,1,0:T(8,128)S(1)} %get-tuple-element.8.bulk), channel_id=1, source_target_pairs={{0,1},{1,0},{2,3},{3,2},{4,5},{5,4},{6,7},{7,6},{8,9},{9,8},{10,11... | collective-permute-start | bytes 3686408 | tf_op jit(solution)/shard_map/ppermute | solution.py:423
  3.2 2.6 %collective-permute-start.1 = (f32[9,16,128]{2,1,0:T(8,128)S(1)}, f32[9,16,128]{2,1,0:T(8,128)S(1)}, u32[]{:S(2)}, u32[]{:S(2)}) collective-permute-start(f32[9,16,128]{2,1,0:T(8,128)S(1)} %get-tuple-element.10), channel_id=1, source_target_pairs={{0,2},{2,0},{4,6},{6,4},{8,10},{10,8},{12,14},{14,12},{16,18},{18,... | collective-permute-start | bytes 221192 | tf_op jit(solution)/shard_map/ppermute | solution.py:419
  5.7 4.5 %collective-permute-start.3 = (f32[9,16,128]{2,1,0:T(8,128)S(1)}, f32[9,16,128]{2,1,0:T(8,128)S(1)}, u32[]{:S(2)}, u32[]{:S(2)}) collective-permute-start(f32[9,16,128]{2,1,0:T(8,128)S(1)} %get-tuple-element.11), channel_id=1, source_target_pairs={{0,30},{2,4},{4,2},{6,8},{8,6},{10,12},{12,10},{14,16},{16,14},{18... | collective-permute-start | bytes 221192 | tf_op jit(solution)/shard_map/ppermute | solution.py:420
  10.3 0.0 collective-permute-done.1.halo_even
  10.3 0.0 collective-permute-start.2
  10.3 3.4 %collective-permute-done.3.refs_1_ = f32[9,16,128]{2,1,0:T(8,128)S(1)} collective-permute-done((f32[9,16,128]{2,1,0:T(8,128)S(1)}, f32[9,16,128]{2,1,0:T(8,128)S(1)}, u32[]{:S(2)}, u32[]{:S(2)}) %collective-permute-start.3) | collective-permute-done | bytes 73760 | tf_op jit(solution)/shard_map/ppermute | solution.py:420
  13.7 0.0 collective-permute-start.4
  13.7 0.0 collective-permute-done.2.sib_even
  13.7 0.0 collective-permute-done.sib_bulk
  13.7 0.7 %collect_lines.1.refs_0_ = f32[67,144,128]{2,1,0:T(8,128)S(1)} custom-call(f32[75,16,256]{2,1,0:T(8,128)S(1)} %get-tuple-element.8.bulk, f32[75,16,256]{2,1,0:T(8,128)S(1)} %collective-permute-done.sib_bulk, s32[1,256]{1,0:T(1,128)S(1)} %get-tuple-element.9.edge, f32[9,16,128]{2,1,0:T(8,128)S(1)} %collective-permute-done.1.halo_even, ...), custom_call_target="tpu_custom_call" | custom-call | tf_op jit(solution)/shard_map/collect_lines/pallas_call | solution.py:429
  14.4 0.6 %collective-permute-done.4.refs_2_ = f32[9,16,128]{2,1,0:T(8,128)S(1)} collective-permute-done((f32[9,16,128]{2,1,0:T(8,128)S(1)}, f32[9,16,128]{2,1,0:T(8,128)S(1)}, u32[]{:S(2)}, u32[]{:S(2)}) %collective-permute-start.4) | collective-permute-done | bytes 73760 | tf_op jit(solution)/shard_map/ppermute | solution.py:423
  15.0 4.2 %relax_lines.1 = (f32[5,16,256]{2,1,0:T(8,128)}, f32[5,16,256]{2,1,0:T(8,128)}, f32[67,144,128]{2,1,0:T(8,128)S(1)}) custom-call(f32[67,144,128]{2,1,0:T(8,128)S(1)} %collect_lines.1.refs_0_, f32[9,16,128]{2,1,0:T(8,128)S(1)} %collective-permute-done.3.refs_1_, f32[9,16,128]{2,1,0:T(8,128)S(1)} %collective-permute-done.4.refs_2_), custom_call_target="tpu_custom_call", output_to_operand_aliasing={{2}: (0, {})} | custom-call | tf_op jit(solution)/shard_map/relax_lines/pallas_call | solution.py:442
Async XLA Ops:
  2.7 11.0 %collective-permute-start = (f32[75,16,256]{2,1,0:T(8,128)S(1)}, f32[75,16,256]{2,1,0:T(8,128)S(1)}, u32[]{:S(2)}, u32[]{:S(2)}) collective-permute-start(f32[75,16,256]{2,1,0:T(8,128)S(1)} %get-tuple-element.8.bulk), channel_id=1, source_target_pairs={{0,1},{1,0},{2,3},{3,2},{4,5},{5,4},{6,7},{7,6},{8,9},{9,8},{10,11... | collective-permute-start | bytes 3686408 | tf_op jit(solution)/shard_map/ppermute | solution.py:423
  3.2 7.1 %collective-permute-start.1 = (f32[9,16,128]{2,1,0:T(8,128)S(1)}, f32[9,16,128]{2,1,0:T(8,128)S(1)}, u32[]{:S(2)}, u32[]{:S(2)}) collective-permute-start(f32[9,16,128]{2,1,0:T(8,128)S(1)} %get-tuple-element.10), channel_id=1, source_target_pairs={{0,2},{2,0},{4,6},{6,4},{8,10},{10,8},{12,14},{14,12},{16,18},{18,... | collective-permute-start | bytes 221192 | tf_op jit(solution)/shard_map/ppermute | solution.py:419
  5.7 7.9 %collective-permute-start.3 = (f32[9,16,128]{2,1,0:T(8,128)S(1)}, f32[9,16,128]{2,1,0:T(8,128)S(1)}, u32[]{:S(2)}, u32[]{:S(2)}) collective-permute-start(f32[9,16,128]{2,1,0:T(8,128)S(1)} %get-tuple-element.11), channel_id=1, source_target_pairs={{0,30},{2,4},{4,2},{6,8},{8,6},{10,12},{12,10},{14,16},{16,14},{18... | collective-permute-start | bytes 221192 | tf_op jit(solution)/shard_map/ppermute | solution.py:420
  10.3 3.4 %collective-permute-start.2 = (f32[9,16,128]{2,1,0:T(8,128)S(1)}, f32[9,16,128]{2,1,0:T(8,128)S(1)}, u32[]{:S(2)}, u32[]{:S(2)}) collective-permute-start(f32[9,16,128]{2,1,0:T(8,128)S(1)} %collective-permute-done.1.halo_even), channel_id=1, source_target_pairs={{0,1},{1,0},{2,3},{3,2},{4,5},{5,4},{6,7},{7,6},{8,9},{9,8},{10,11... | collective-permute-start | bytes 221192 | tf_op jit(solution)/shard_map/ppermute | solution.py:423
  13.7 1.3 %collective-permute-start.4 = (f32[9,16,128]{2,1,0:T(8,128)S(1)}, f32[9,16,128]{2,1,0:T(8,128)S(1)}, u32[]{:S(2)}, u32[]{:S(2)}) collective-permute-start(f32[9,16,128]{2,1,0:T(8,128)S(1)} %collective-permute-done.3.refs_1_), channel_id=1, source_target_pairs={{0,1},{1,0},{2,3},{3,2},{4,5},{5,4},{6,7},{7,6},{8,9},{9,8},{10,11... | collective-permute-start | bytes 221192 | tf_op jit(solution)/shard_map/ppermute | solution.py:423

commit v4 on v3

--- a/solution.py
+++ b/solution.py
@@ -69,16 +69,12 @@
     core = lax.axis_index("wn")
     conv, spin, lines = parts_of(bulk)
     copies = []
-    for n in range(NC):
-        part = pl.ds(NC * n, NC)
-        copies.append(pltpu.make_async_copy(conv_hbm.at[part], conv.at[part], sems.at[n]))
+    copies.append(pltpu.make_async_copy(conv_hbm, conv, sems.at[0]))
     for n, ref in enumerate((visc_hbm, flux_hbm, vaz_hbm, faz_hbm, inc_hbm)):
-        copies.append(pltpu.make_async_copy(ref, lines[n], sems.at[NC + n]))
-    for n in range(NC):
-        part = pl.ds(NC * n, NC)
-        copies.append(pltpu.make_async_copy(spin_hbm.at[part], spin.at[part], sems.at[2 * NC + n]))
-    copies.append(pltpu.make_async_copy(edge_hbm, edge, sems.at[3 * NC]))
-    copies.append(pltpu.make_async_copy(cells_hbm, cells, sems.at[3 * NC + 1]))
+        copies.append(pltpu.make_async_copy(ref, lines[n], sems.at[1 + n]))
+    copies.append(pltpu.make_async_copy(spin_hbm, spin, sems.at[NC + 1]))
+    copies.append(pltpu.make_async_copy(edge_hbm, edge, sems.at[NC + 2]))
+    copies.append(pltpu.make_async_copy(cells_hbm, cells, sems.at[NC + 3]))
     for copy in copies:
         copy.start()
     read = tile_reader(conv, spin, edge, lines)
@@ -89,11 +85,11 @@
     last = [[blank] * PACKS for _ in range(2)]
     late = list(range(SKEW, VISC)) + [EDGE, FLUID]
     for value in [v for v in range(VALUES) if v not in late] + late:
-        for group, begin in enumerate([NC * n for n in range(NC)] + [VISC, FLUX, VAZ, FAZ, INC]):
+        for group, begin in enumerate([CONV, VISC, FLUX, VAZ, FAZ, INC]):
             if value == begin:
                 copies[group].wait()
         if value == late[0]:
-            for copy in copies[2 * NC :]:
+            for copy in copies[NC + 1 :]:
                 copy.wait()
         pack, slot, width = slot_of(value)
         low = slot * width
@@ -107,9 +103,10 @@
                     one = jnp.where(row == p, jnp.where(cells[p] == 0, 1.0, 0.0).astype(jnp.float32), one)
                 two = one
             else:
-                one, two = read(value, t, 0), read(value, t, 1)
+                one = jnp.where(lane < LANES // 2, read(value, t, 0), read(value, t, 1))
                 if slot:
-                    one, two = pltpu.roll(one, slot * width, 1), pltpu.roll(two, slot * width, 1)
+                    one = pltpu.roll(one, slot * width, 1)
+                two = one
             first[t][pack] = jnp.where(here, one, first[t][pack])
             last[t][pack] = jnp.where(there, two, last[t][pack])
     for pack in range(PACKS):
@@ -132,6 +129,8 @@
                 work[i][j] = work[i][j] - work[i][p] * work[p][j]
     for p in range(NC):
         work[p][p] = scale[p]
+        for j in range(p + 1, NC):
+            work[p][j] = work[p][j] * scale[p]
     return work
 
 
@@ -140,10 +139,10 @@
     for p in range(NC):
         for i in range(p + 1, NC):
             side[i] = side[i] - work[i][p] * side[p]
-    for i in reversed(range(NC)):
-        for j in range(i + 1, NC):
-            side[i] = side[i] - work[i][j] * side[j]
-        side[i] = side[i] * work[i][i]
+    side = [side[p] * work[p][p] for p in range(NC)]
+    for p in reversed(range(NC)):
+        for i in range(p):
+            side[i] = side[i] - work[i][p] * side[p]
     return side
 
 
@@ -186,7 +185,7 @@
             put(cells, value, t, place, chain, tile)
 
 
-def collect_kernel(bulk, sib_bulk, edge, halo_even, sib_even, cells):
+def collect_kernel(bulk, sib_bulk, edge, halo_even, sib_even, halo_odd, cells):
     core = lax.axis_index("wn")
     even_place = 2 + lax.rem(lax.axis_index("az"), 2)
     for chain, array, halo in ((core, bulk, halo_even), (1 - core, sib_bulk, sib_even)):
@@ -200,18 +199,18 @@
                     tile = mirror(read(value, t, lt), chain)
                     put(cells, value, jnp.bitwise_xor(t, chain), lt, chain, tile)
         put_halo(cells, halo, even_place, chain)
+    put_halo(cells, halo_odd, 5 - even_place, core)
 
 
 def main_kernel(points, *refs):
     cells_in, halo_odd, sib_odd, out_inc, out_defect, cells = refs[0:6]
-    couple, conv_face, visc_face, diagonal, skews, lu, sides, solved, vmin, vplus, azd, src, out_cells = refs[6:]
+    couple, conv_face, skews, lu, diagonal, upper_diag, lower_diag, sides, solved, vmin, vplus, azd, src, out_cells = refs[6:]
 
     core = lax.axis_index("wn")
     odd_place = lax.rem(lax.axis_index("az"), 2)
     row = lax.broadcasted_iota(jnp.int32, (SUB, LANES), 0)
     lane = lax.broadcasted_iota(jnp.int32, (SUB, LANES), 1)
     is_a = lax.rem(row, 2) == 0
-    put_halo(cells, halo_odd, 3 - odd_place, core)
     put_halo(cells, sib_odd, 3 - odd_place, 1 - core)
 
     def at(value, k):
@@ -290,24 +289,30 @@
         matrix = [[None] * NC for _ in range(NC)]
         for c in range(NC):
             matrix[c][c] = visc_in[c] + visc_out[c] + az_diag[c]
+            diagonal[k * NC + c] = matrix[c][c]
+        up = [[conv_out[a][b] - visc_out[a] if a == b else conv_out[a][b] for b in range(NC)] for a in range(NC)]
+        low = [[conv_out[a][b] + visc_out[a] if a == b else conv_out[a][b] for b in range(NC)] for a in range(NC)]
+        for a in range(NC):
+            upper_diag[k * NC + a], lower_diag[k * NC + a] = up[a][a], low[a][a]
+            for b in range(NC):
+                if a != b:
+                    conv_face[k * 25 + a * NC + b] = conv_out[a][b]
+        if previous is not None:
+            low_in, couple_in, y_in = previous
+            moved = product([[low_in[b][a] for b in range(NC)] for a in range(NC)], couple_in)
+            shift = times([[low_in[b][a] for b in range(NC)] for a in range(NC)], y_in)
+            side = [side[c] + shift[c] for c in range(NC)]
+            for c in range(NC):
+                matrix[c][c] = matrix[c][c] + moved[c][c]
         for n, (a, b) in enumerate(PAIRS):
             skew = at(SKEW + n, k)
             if solid:
                 skew = skew * (keep[a] * keep[b])
             skews[k * len(PAIRS) + n] = skew
-            matrix[a][b], matrix[b][a] = skew, -skew
-        up = [[conv_out[a][b] - visc_out[a] if a == b else conv_out[a][b] for b in range(NC)] for a in range(NC)]
-        for a in range(NC):
-            diagonal[k * NC + a], visc_face[k * NC + a] = matrix[a][a], visc_out[a]
-            for b in range(NC):
-                conv_face[k * 25 + a * NC + b] = conv_out[a][b]
-        if previous is not None:
-            conv_in, couple_in, y_in = previous
-            low = [[-visc_in[a] - conv_in[a][a] if a == b else -conv_in[b][a] for b in range(NC)] for a in range(NC)]
-            moved = product(low, couple_in)
-            matrix = [[matrix[a][b] - moved[a][b] for b in range(NC)] for a in range(NC)]
-            shift = times(low, y_in)
-            side = [side[c] - shift[c] for c in range(NC)]
+            if previous is None:
+                matrix[a][b], matrix[b][a] = skew, -skew
+            else:
+                matrix[a][b], matrix[b][a] = moved[a][b] + skew, moved[b][a] - skew
         work = factor(matrix)
         columns = [substitute(work, [up[i][j] for i in range(NC)]) for j in range(NC)]
         couple_now = [[columns[j][i] for j in range(NC)] for i in range(NC)]
@@ -317,70 +322,82 @@
             for b in range(NC):
                 lu[k * 25 + a * NC + b] = work[a][b]
                 couple[k * 25 + a * NC + b] = couple_now[a][b]
-        previous = (conv_out, couple_now, y)
+        previous = (low, couple_now, y)
         visc_in = visc_out
 
     def block(ref, k):
         return [[ref[k * 25 + a * NC + b] for b in range(NC)] for a in range(NC)]
 
-    def below(k, x):
-        face, visc = block(conv_face, k - 1), vector(visc_face, k - 1)
-        return [visc[c] * x[c] + dot([face[r][c] for r in range(NC)], x) for c in range(NC)]
-
     def vector(ref, k):
         return [ref[k * NC + c] for c in range(NC)]
+
+    def face(diagonal_ref, k):
+        corner = vector(diagonal_ref, k)
+        return [[corner[a] if a == b else conv_face[k * 25 + a * NC + b] for b in range(NC)] for a in range(NC)]
+
+    def below(k, x, total=(None,) * NC):
+        low, total = face(lower_diag, k - 1), list(total)
+        for r in reversed(range(NC)):
+            for c in range(NC):
+                term = low[r][c] * x[r]
+                total[c] = term if total[c] is None else total[c] + term
+        return total
 
     couple_end = couple_now
     crossed = product(couple_end, [[swap(couple_end[a][b]) for b in range(NC)] for a in range(NC)])
     meeting = factor([[(1.0 if a == b else 0.0) - crossed[a][b] for b in range(NC)] for a in range(NC)])
 
-    def finish(y):
+    def finish(y, visit):
         shift = times(couple_end, [swap(v) for v in y])
         x = substitute(meeting, [y[c] - shift[c] for c in range(NC)])
+        beyond = [swap(v) for v in x]
+        for k in reversed(range(points)):
+            inner = None
+            if k:
+                shift = times(block(couple, k - 1), x)
+                y_here = vector(sides, k - 1)
+                inner = [y_here[c] - shift[c] for c in range(NC)]
+            visit(k, inner, x, beyond)
+            x, beyond = inner, x
+
+    def offline(k, x):
+        vm, vp = vector(vmin, k), vector(vplus, k)
+        return [vm[c] * before(x[c]) + vp[c] * after(x[c]) for c in range(NC)]
+
+    def next_side(k, inner, x, beyond):
+        source, moved = vector(src, k), offline(k, x)
         for c in range(NC):
-            solved[last * NC + c] = x[c]
-        for k in reversed(range(last)):
-            shift = times(block(couple, k), x)
-            y_here = vector(sides, k)
-            x = [y_here[c] - shift[c] for c in range(NC)]
-            for c in range(NC):
-                solved[k * NC + c] = x[c]
-
-    finish(y)
-    for sweep in range(1, SWEEPS):
-        for k in range(points):
-            source, vm, vp, x = vector(src, k), vector(vmin, k), vector(vplus, k), vector(solved, k)
-            side = [source[c] + (vm[c] * before(x[c]) + vp[c] * after(x[c])) for c in range(NC)]
-            if k:
-                shift = below(k, y)
-                side = [side[c] + shift[c] for c in range(NC)]
-            y = substitute(block(lu, k), side)
-            for c in range(NC):
-                sides[k * NC + c] = y[c]
-        finish(y)
-
-    for k in range(points):
-        source, vm, vp, x = vector(src, k), vector(vmin, k), vector(vplus, k), vector(solved, k)
-        diag = vector(azd, k)
-        beyond = vector(solved, k + 1) if k < last else [swap(v) for v in x]
-        visc_out, main = vector(visc_face, k), vector(diagonal, k)
-        applied = [main[c] * x[c] - visc_out[c] * beyond[c] for c in range(NC)]
-        outer = times(block(conv_face, k), beyond)
-        applied = [applied[c] + outer[c] for c in range(NC)]
+            solved[k * NC + c] = source[c] + moved[c]
+
+    def result(k, inner, x, beyond):
+        source, moved, diag = vector(src, k), offline(k, x), vector(azd, k)
+        main = vector(diagonal, k)
+        applied = times(face(upper_diag, k), beyond)
+        applied = [applied[c] + main[c] * x[c] for c in range(NC)]
         for n, (a, b) in enumerate(PAIRS):
             skew = skews[k * len(PAIRS) + n]
             applied[a] = applied[a] + skew * x[b]
             applied[b] = applied[b] - skew * x[a]
         if k:
-            under = below(k, vector(solved, k - 1))
+            under = below(k, inner)
             applied = [applied[c] - under[c] for c in range(NC)]
         place = jnp.where(core == 0, k % SUB, SUB - 1 - k % SUB)
         t = jnp.where(core == 0, k // SUB, 1 - k // SUB)
         for c in range(NC):
-            offline = vm[c] * before(x[c]) + vp[c] * after(x[c])
-            defect = (source[c] + offline - applied[c]) / diag[c]
+            defect = (source[c] + moved[c] - applied[c]) / diag[c]
             out_cells[2 * c + t, pl.ds(place, SUB, stride=SUB), :] = x[c]
             out_cells[2 * (NC + c) + t, pl.ds(place, SUB, stride=SUB), :] = defect
+
+    for sweep in range(1, SWEEPS):
+        finish(y, next_side)
+        for k in range(points):
+            side = vector(solved, k)
+            if k:
+                side = below(k, y, side)
+            y = substitute(block(lu, k), side)
+            for c in range(NC):
+                sides[k * NC + c] = y[c]
+    finish(y, result)
     for c in range(NC):
         for t in range(2):
             for lt in range(2):
@@ -412,7 +429,7 @@
         out_shape=(pack, pack, bulk, jax.ShapeDtypeStruct((1, line_count), jnp.int32)),
         in_specs=[hbm] * 9,
         out_specs=(vmem,) * 4,
-        scratch_shapes=[pltpu.SMEM((points,), jnp.int32), pltpu.SemaphoreType.DMA((3 * NC + 2,))],
+        scratch_shapes=[pltpu.SMEM((points,), jnp.int32), pltpu.SemaphoreType.DMA((NC + 4,))],
         name="pack_halo",
         compiler_params=pltpu.CompilerParams(vmem_limit_bytes=16 << 20),
     )(*from_hbm)
@@ -429,11 +446,11 @@
     cells = pl.pallas_call(
         collect_kernel,
         out_shape=tiles,
-        in_specs=[vmem] * 5,
+        in_specs=[vmem] * 6,
         out_specs=vmem,
         name="collect_lines",
         compiler_params=pltpu.CompilerParams(vmem_limit_bytes=16 << 20),
-    )(bulk, sib_bulk, edge, halo_even, sib_even)
+    )(bulk, sib_bulk, edge, halo_even, sib_even, halo_odd)
 
     def step(count):
         return pltpu.VMEM((points * count, SUB, LANES), jnp.float32)
@@ -445,8 +462,8 @@
         in_specs=[vmem] * 3,
         out_specs=(vmem, vmem, vmem),
         input_output_aliases={0: 2},
-        scratch_shapes=[step(n) for n in (NC * NC, NC * NC, NC, NC, len(PAIRS), NC * NC)]
-        + [step(NC)] * 6
+        scratch_shapes=[step(n) for n in (NC * NC, NC * NC, len(PAIRS), NC * NC)]
+        + [step(NC)] * 9
         + [pltpu.VMEM((4 * NC, SUB * SUB, LANES), jnp.float32)],
         name="relax_lines",
         compiler_params=pltpu.CompilerParams(vmem_limit_bytes=24 << 20),

time: 19.4 us -> 18.8 us (0.969)
  Pallas kernels: 6.91 us -> 6.47 us
    pallas_call x1, Pallas kernels: 2.02 us -> 1.69 us  [per_device(): pl.pallas_call(pack_kernel, out_shape=(pack, pack, bulk, jax.ShapeDtypeSt...]
    pallas_call x1, Pallas kernels: 4.24 us -> 3.98 us  [per_device(): pl.pallas_call(lambda *refs: main_kernel(points, *refs), out_shape=(out,...]
  transfers between devices with their start and end apart: 5 -> 5, of which waited for: 2 -> 2; matrix products, arithmetic and copies ran while one was open for 0% -> 0% of each run, Pallas kernels for 3% -> 4%
where the time goes in v4:
time: 18.8 us; the launch traced here: 18.6 us
  starting transfers between devices  7.62 us (41%)
  Pallas kernels  6.47 us (34%)
  waiting for transfers between devices  3.86 us (21%)
  between operations  0.66 us (4%)
    ppermute x1, starting transfers between devices, per_device(): halo_odd = lax.ppermute(odd, 'az', odd_pairs)  4.53 us
    pallas_call x1, Pallas kernels, per_device(): pl.pallas_call(lambda *refs: main_kernel(points, *refs), out_shape=(out,...  3.98 us
    ppermute x1, waiting for transfers between devices, per_device(): halo_odd = lax.ppermute(odd, 'az', odd_pairs)  3.41 us
    ppermute x1, starting transfers between devices, per_device(): halo_even = lax.ppermute(even, 'az', even_pairs)  2.56 us
    pallas_call x1, Pallas kernels, per_device(): pl.pallas_call(pack_kernel, out_shape=(pack, pack, bulk, jax.ShapeDtypeSt...  1.69 us
    pallas_call x1, Pallas kernels, per_device(): pl.pallas_call(collect_kernel, out_shape=tiles, in_specs=[vmem] * 6, out_...  0.81 us
    ppermute x3, starting transfers between devices, cross(): return lax.ppermute(array, 'wn', [(0, 1), (1, 0)])  0.52 us
    ppermute x3, waiting for transfers between devices, cross(): return lax.ppermute(array, 'wn', [(0, 1), (1, 0)])  0.45 us
  transfers between devices with their start and end apart: 5, of which 2 were waited for; matrix products, arithmetic and copies ran while one was open for 0% of the time, Pallas kernels for 4%

profile of v4, /device:TPU:0, one launch (start us, length us, event | category | flops | bytes accessed | tf_op | source)
XLA Modules:
  0.0 18.6 jit_solution(6047324368789591383)
XLA Ops:
  0.6 1.7 %pack_halo.1 = (f32[9,16,128]{2,1,0:T(8,128)S(1)}, f32[9,16,128]{2,1,0:T(8,128)S(1)}, f32[75,16,256]{2,1,0:T(8,128)S(1)}, s32[1,256]{1,0:T(1,128)S(1)}) custom-call(f32[25,16,256]{2,1,0:T(8,128)} %bitcast.3, f32[25,16,256]{2,1,0:T(8,128)} %bitcast.4, s32[1,256]{1,0:T(1,128)} %bitcast.5, f32[5,16,256]{2,1,0:T(8,128)} %visc_hbm.1, f32[5,16,256]{2,1,0:T(8,128)} %flux_hbm.1, ...), custom_call_target="tpu_custom_call" | custom-call | tf_op jit(solution)/shard_map/pack_halo/pallas_call | solution.py:427
  2.3 0.5 %collective-permute-start = (f32[75,16,256]{2,1,0:T(8,128)S(1)}, f32[75,16,256]{2,1,0:T(8,128)S(1)}, u32[]{:S(2)}, u32[]{:S(2)}) collective-permute-start(f32[75,16,256]{2,1,0:T(8,128)S(1)} %get-tuple-element.8.bulk), channel_id=1, source_target_pairs={{0,1},{1,0},{2,3},{3,2},{4,5},{5,4},{6,7},{7,6},{8,9},{9,8},{10,11... | collective-permute-start | bytes 3686408 | tf_op jit(solution)/shard_map/ppermute | solution.py:440
  2.8 2.6 %collective-permute-start.1 = (f32[9,16,128]{2,1,0:T(8,128)S(1)}, f32[9,16,128]{2,1,0:T(8,128)S(1)}, u32[]{:S(2)}, u32[]{:S(2)}) collective-permute-start(f32[9,16,128]{2,1,0:T(8,128)S(1)} %get-tuple-element.10), channel_id=1, source_target_pairs={{0,2},{2,0},{4,6},{6,4},{8,10},{10,8},{12,14},{14,12},{16,18},{18,... | collective-permute-start | bytes 221192 | tf_op jit(solution)/shard_map/ppermute | solution.py:436
  5.4 4.5 %collective-permute-start.3 = (f32[9,16,128]{2,1,0:T(8,128)S(1)}, f32[9,16,128]{2,1,0:T(8,128)S(1)}, u32[]{:S(2)}, u32[]{:S(2)}) collective-permute-start(f32[9,16,128]{2,1,0:T(8,128)S(1)} %get-tuple-element.11), channel_id=1, source_target_pairs={{0,30},{2,4},{4,2},{6,8},{8,6},{10,12},{12,10},{14,16},{16,14},{18... | collective-permute-start | bytes 221192 | tf_op jit(solution)/shard_map/ppermute | solution.py:437
  9.9 0.0 collective-permute-done.1.halo_even
  9.9 0.0 collective-permute-start.2
  9.9 3.4 %collective-permute-done.3.halo_odd.refs_1_ = f32[9,16,128]{2,1,0:T(8,128)S(1)} collective-permute-done((f32[9,16,128]{2,1,0:T(8,128)S(1)}, f32[9,16,128]{2,1,0:T(8,128)S(1)}, u32[]{:S(2)}, u32[]{:S(2)}) %collective-permute-start.3) | collective-permute-done | bytes 73760 | tf_op jit(solution)/shard_map/ppermute | solution.py:437
  13.4 0.0 collective-permute-start.4
  13.4 0.0 collective-permute-done.2.sib_even
  13.4 0.0 collective-permute-done.sib_bulk
  13.4 0.8 %collect_lines.1.refs_0_ = f32[67,144,128]{2,1,0:T(8,128)S(1)} custom-call(f32[75,16,256]{2,1,0:T(8,128)S(1)} %get-tuple-element.8.bulk, f32[75,16,256]{2,1,0:T(8,128)S(1)} %collective-permute-done.sib_bulk, s32[1,256]{1,0:T(1,128)S(1)} %get-tuple-element.9.edge, f32[9,16,128]{2,1,0:T(8,128)S(1)} %collective-permute-done.1.halo_even, ...), custom_call_target="tpu_custom_call" | custom-call | tf_op jit(solution)/shard_map/collect_lines/pallas_call | solution.py:446
  14.2 0.4 %collective-permute-done.4.refs_2_ = f32[9,16,128]{2,1,0:T(8,128)S(1)} collective-permute-done((f32[9,16,128]{2,1,0:T(8,128)S(1)}, f32[9,16,128]{2,1,0:T(8,128)S(1)}, u32[]{:S(2)}, u32[]{:S(2)}) %collective-permute-start.4) | collective-permute-done | bytes 73760 | tf_op jit(solution)/shard_map/ppermute | solution.py:440
  14.6 4.0 %relax_lines.1 = (f32[5,16,256]{2,1,0:T(8,128)}, f32[5,16,256]{2,1,0:T(8,128)}, f32[67,144,128]{2,1,0:T(8,128)S(1)}) custom-call(f32[67,144,128]{2,1,0:T(8,128)S(1)} %collect_lines.1.refs_0_, f32[9,16,128]{2,1,0:T(8,128)S(1)} %collective-permute-done.3.halo_odd.refs_1_, f32[9,16,128]{2,1,0:T(8,128)S(1)} %collective-permute-done.4.refs_2_), custom_call_target="tpu_custom_call", output_to_operand_aliasing={{2}: (0, {})} | custom-call | tf_op jit(solution)/shard_map/relax_lines/pallas_call | solution.py:459
Async XLA Ops:
  2.3 11.0 %collective-permute-start = (f32[75,16,256]{2,1,0:T(8,128)S(1)}, f32[75,16,256]{2,1,0:T(8,128)S(1)}, u32[]{:S(2)}, u32[]{:S(2)}) collective-permute-start(f32[75,16,256]{2,1,0:T(8,128)S(1)} %get-tuple-element.8.bulk), channel_id=1, source_target_pairs={{0,1},{1,0},{2,3},{3,2},{4,5},{5,4},{6,7},{7,6},{8,9},{9,8},{10,11... | collective-permute-start | bytes 3686408 | tf_op jit(solution)/shard_map/ppermute | solution.py:440
  2.8 7.1 %collective-permute-start.1 = (f32[9,16,128]{2,1,0:T(8,128)S(1)}, f32[9,16,128]{2,1,0:T(8,128)S(1)}, u32[]{:S(2)}, u32[]{:S(2)}) collective-permute-start(f32[9,16,128]{2,1,0:T(8,128)S(1)} %get-tuple-element.10), channel_id=1, source_target_pairs={{0,2},{2,0},{4,6},{6,4},{8,10},{10,8},{12,14},{14,12},{16,18},{18,... | collective-permute-start | bytes 221192 | tf_op jit(solution)/shard_map/ppermute | solution.py:436
  5.4 7.9 %collective-permute-start.3 = (f32[9,16,128]{2,1,0:T(8,128)S(1)}, f32[9,16,128]{2,1,0:T(8,128)S(1)}, u32[]{:S(2)}, u32[]{:S(2)}) collective-permute-start(f32[9,16,128]{2,1,0:T(8,128)S(1)} %get-tuple-element.11), channel_id=1, source_target_pairs={{0,30},{2,4},{4,2},{6,8},{8,6},{10,12},{12,10},{14,16},{16,14},{18... | collective-permute-start | bytes 221192 | tf_op jit(solution)/shard_map/ppermute | solution.py:437
  9.9 3.4 %collective-permute-start.2 = (f32[9,16,128]{2,1,0:T(8,128)S(1)}, f32[9,16,128]{2,1,0:T(8,128)S(1)}, u32[]{:S(2)}, u32[]{:S(2)}) collective-permute-start(f32[9,16,128]{2,1,0:T(8,128)S(1)} %collective-permute-done.1.halo_even), channel_id=1, source_target_pairs={{0,1},{1,0},{2,3},{3,2},{4,5},{5,4},{6,7},{7,6},{8,9},{9,8},{10,11... | collective-permute-start | bytes 221192 | tf_op jit(solution)/shard_map/ppermute | solution.py:440
  13.4 1.3 %collective-permute-start.4 = (f32[9,16,128]{2,1,0:T(8,128)S(1)}, f32[9,16,128]{2,1,0:T(8,128)S(1)}, u32[]{:S(2)}, u32[]{:S(2)}) collective-permute-start(f32[9,16,128]{2,1,0:T(8,128)S(1)} %collective-permute-done.3.halo_odd.refs_1_), channel_id=1, source_target_pairs={{0,1},{1,0},{2,3},{3,2},{4,5},{5,4},{6,7},{7,6},{8,9},{9,8},{10,11... | collective-permute-start | bytes 221192 | tf_op jit(solution)/shard_map/ppermute | solution.py:440

commit v5 on v4

--- a/solution.py
+++ b/solution.py
@@ -19,7 +19,7 @@
 VAZ, FAZ, INC = 47, 52, 57
 VALUES = 62
 BELOW, STORED = 62, 67
-SLOTS = 18
+SLOTS = 19
 SOLID_MOST = 4
 NEAR_SLOTS = LANES // NEAR
 FAR_SLOTS = LANES // FAR
@@ -464,7 +464,7 @@
         input_output_aliases={0: 2},
         scratch_shapes=[step(n) for n in (NC * NC, NC * NC, len(PAIRS), NC * NC)]
         + [step(NC)] * 9
-        + [pltpu.VMEM((4 * NC, SUB * SUB, LANES), jnp.float32)],
+        + [pltpu.VMEM((4 * NC, SUB * SUB + SUB, LANES), jnp.float32)],
         name="relax_lines",
         compiler_params=pltpu.CompilerParams(vmem_limit_bytes=24 << 20),
     )(cells, halo_odd, sib_odd)

time: 18.8 us -> 18.8 us (level)
  no operation moved by 1% of the time
where the time goes in v5:
time: 18.8 us; the launch traced here: 18.6 us
  starting transfers between devices  7.62 us (41%)
  Pallas kernels  6.49 us (35%)
  waiting for transfers between devices  3.86 us (21%)
  between operations  0.66 us (4%)
    ppermute x1, starting transfers between devices, per_device(): halo_odd = lax.ppermute(odd, 'az', odd_pairs)  4.53 us
    pallas_call x1, Pallas kernels, per_device(): pl.pallas_call(lambda *refs: main_kernel(points, *refs), out_shape=(out,...  3.99 us
    ppermute x1, waiting for transfers between devices, per_device(): halo_odd = lax.ppermute(odd, 'az', odd_pairs)  3.41 us
    ppermute x1, starting transfers between devices, per_device(): halo_even = lax.ppermute(even, 'az', even_pairs)  2.56 us
    pallas_call x1, Pallas kernels, per_device(): pl.pallas_call(pack_kernel, out_shape=(pack, pack, bulk, jax.ShapeDtypeSt...  1.69 us
    pallas_call x1, Pallas kernels, per_device(): pl.pallas_call(collect_kernel, out_shape=tiles, in_specs=[vmem] * 6, out_...  0.81 us
    ppermute x3, starting transfers between devices, cross(): return lax.ppermute(array, 'wn', [(0, 1), (1, 0)])  0.52 us
    ppermute x3, waiting for transfers between devices, cross(): return lax.ppermute(array, 'wn', [(0, 1), (1, 0)])  0.44 us
  transfers between devices with their start and end apart: 5, of which 2 were waited for; matrix products, arithmetic and copies ran while one was open for 0% of the time, Pallas kernels for 4%

profile of v5, /device:TPU:0, one launch (start us, length us, event | category | flops | bytes accessed | tf_op | source)
XLA Modules:
  0.0 18.6 jit_solution(7864492436541654939)
XLA Ops:
  0.6 1.7 %pack_halo.1 = (f32[9,16,128]{2,1,0:T(8,128)S(1)}, f32[9,16,128]{2,1,0:T(8,128)S(1)}, f32[75,16,256]{2,1,0:T(8,128)S(1)}, s32[1,256]{1,0:T(1,128)S(1)}) custom-call(f32[25,16,256]{2,1,0:T(8,128)} %bitcast.3, f32[25,16,256]{2,1,0:T(8,128)} %bitcast.4, s32[1,256]{1,0:T(1,128)} %bitcast.5, f32[5,16,256]{2,1,0:T(8,128)} %visc_hbm.1, f32[5,16,256]{2,1,0:T(8,128)} %flux_hbm.1, ...), custom_call_target="tpu_custom_call" | custom-call | tf_op jit(solution)/shard_map/pack_halo/pallas_call | solution.py:427
  2.3 0.5 %collective-permute-start = (f32[75,16,256]{2,1,0:T(8,128)S(1)}, f32[75,16,256]{2,1,0:T(8,128)S(1)}, u32[]{:S(2)}, u32[]{:S(2)}) collective-permute-start(f32[75,16,256]{2,1,0:T(8,128)S(1)} %get-tuple-element.8.bulk), channel_id=1, source_target_pairs={{0,1},{1,0},{2,3},{3,2},{4,5},{5,4},{6,7},{7,6},{8,9},{9,8},{10,11... | collective-permute-start | bytes 3686408 | tf_op jit(solution)/shard_map/ppermute | solution.py:440
  2.8 2.6 %collective-permute-start.1 = (f32[9,16,128]{2,1,0:T(8,128)S(1)}, f32[9,16,128]{2,1,0:T(8,128)S(1)}, u32[]{:S(2)}, u32[]{:S(2)}) collective-permute-start(f32[9,16,128]{2,1,0:T(8,128)S(1)} %get-tuple-element.10), channel_id=1, source_target_pairs={{0,2},{2,0},{4,6},{6,4},{8,10},{10,8},{12,14},{14,12},{16,18},{18,... | collective-permute-start | bytes 221192 | tf_op jit(solution)/shard_map/ppermute | solution.py:436
  5.4 4.5 %collective-permute-start.3 = (f32[9,16,128]{2,1,0:T(8,128)S(1)}, f32[9,16,128]{2,1,0:T(8,128)S(1)}, u32[]{:S(2)}, u32[]{:S(2)}) collective-permute-start(f32[9,16,128]{2,1,0:T(8,128)S(1)} %get-tuple-element.11), channel_id=1, source_target_pairs={{0,30},{2,4},{4,2},{6,8},{8,6},{10,12},{12,10},{14,16},{16,14},{18... | collective-permute-start | bytes 221192 | tf_op jit(solution)/shard_map/ppermute | solution.py:437
  9.9 0.0 collective-permute-done.1.halo_even
  9.9 0.0 collective-permute-start.2
  9.9 3.4 %collective-permute-done.3.halo_odd.refs_1_ = f32[9,16,128]{2,1,0:T(8,128)S(1)} collective-permute-done((f32[9,16,128]{2,1,0:T(8,128)S(1)}, f32[9,16,128]{2,1,0:T(8,128)S(1)}, u32[]{:S(2)}, u32[]{:S(2)}) %collective-permute-start.3) | collective-permute-done | bytes 73760 | tf_op jit(solution)/shard_map/ppermute | solution.py:437
  13.4 0.0 collective-permute-start.4
  13.4 0.0 collective-permute-done.2.sib_even
  13.4 0.0 collective-permute-done.sib_bulk
  13.4 0.8 %collect_lines.1.refs_0_ = f32[67,152,128]{2,1,0:T(8,128)S(1)} custom-call(f32[75,16,256]{2,1,0:T(8,128)S(1)} %get-tuple-element.8.bulk, f32[75,16,256]{2,1,0:T(8,128)S(1)} %collective-permute-done.sib_bulk, s32[1,256]{1,0:T(1,128)S(1)} %get-tuple-element.9.edge, f32[9,16,128]{2,1,0:T(8,128)S(1)} %collective-permute-done.1.halo_even, ...), custom_call_target="tpu_custom_call" | custom-call | tf_op jit(solution)/shard_map/collect_lines/pallas_call | solution.py:446
  14.2 0.4 %collective-permute-done.4.refs_2_ = f32[9,16,128]{2,1,0:T(8,128)S(1)} collective-permute-done((f32[9,16,128]{2,1,0:T(8,128)S(1)}, f32[9,16,128]{2,1,0:T(8,128)S(1)}, u32[]{:S(2)}, u32[]{:S(2)}) %collective-permute-start.4) | collective-permute-done | bytes 73760 | tf_op jit(solution)/shard_map/ppermute | solution.py:440
  14.6 4.0 %relax_lines.1 = (f32[5,16,256]{2,1,0:T(8,128)}, f32[5,16,256]{2,1,0:T(8,128)}, f32[67,152,128]{2,1,0:T(8,128)S(1)}) custom-call(f32[67,152,128]{2,1,0:T(8,128)S(1)} %collect_lines.1.refs_0_, f32[9,16,128]{2,1,0:T(8,128)S(1)} %collective-permute-done.3.halo_odd.refs_1_, f32[9,16,128]{2,1,0:T(8,128)S(1)} %collective-permute-done.4.refs_2_), custom_call_target="tpu_custom_call", output_to_operand_aliasing={{2}: (0, {})} | custom-call | tf_op jit(solution)/shard_map/relax_lines/pallas_call | solution.py:459
Async XLA Ops:
  2.3 11.0 %collective-permute-start = (f32[75,16,256]{2,1,0:T(8,128)S(1)}, f32[75,16,256]{2,1,0:T(8,128)S(1)}, u32[]{:S(2)}, u32[]{:S(2)}) collective-permute-start(f32[75,16,256]{2,1,0:T(8,128)S(1)} %get-tuple-element.8.bulk), channel_id=1, source_target_pairs={{0,1},{1,0},{2,3},{3,2},{4,5},{5,4},{6,7},{7,6},{8,9},{9,8},{10,11... | collective-permute-start | bytes 3686408 | tf_op jit(solution)/shard_map/ppermute | solution.py:440
  2.8 7.1 %collective-permute-start.1 = (f32[9,16,128]{2,1,0:T(8,128)S(1)}, f32[9,16,128]{2,1,0:T(8,128)S(1)}, u32[]{:S(2)}, u32[]{:S(2)}) collective-permute-start(f32[9,16,128]{2,1,0:T(8,128)S(1)} %get-tuple-element.10), channel_id=1, source_target_pairs={{0,2},{2,0},{4,6},{6,4},{8,10},{10,8},{12,14},{14,12},{16,18},{18,... | collective-permute-start | bytes 221192 | tf_op jit(solution)/shard_map/ppermute | solution.py:436
  5.4 7.9 %collective-permute-start.3 = (f32[9,16,128]{2,1,0:T(8,128)S(1)}, f32[9,16,128]{2,1,0:T(8,128)S(1)}, u32[]{:S(2)}, u32[]{:S(2)}) collective-permute-start(f32[9,16,128]{2,1,0:T(8,128)S(1)} %get-tuple-element.11), channel_id=1, source_target_pairs={{0,30},{2,4},{4,2},{6,8},{8,6},{10,12},{12,10},{14,16},{16,14},{18... | collective-permute-start | bytes 221192 | tf_op jit(solution)/shard_map/ppermute | solution.py:437
  9.9 3.4 %collective-permute-start.2 = (f32[9,16,128]{2,1,0:T(8,128)S(1)}, f32[9,16,128]{2,1,0:T(8,128)S(1)}, u32[]{:S(2)}, u32[]{:S(2)}) collective-permute-start(f32[9,16,128]{2,1,0:T(8,128)S(1)} %collective-permute-done.1.halo_even), channel_id=1, source_target_pairs={{0,1},{1,0},{2,3},{3,2},{4,5},{5,4},{6,7},{7,6},{8,9},{9,8},{10,11... | collective-permute-start | bytes 221192 | tf_op jit(solution)/shard_map/ppermute | solution.py:440
  13.4 1.3 %collective-permute-start.4 = (f32[9,16,128]{2,1,0:T(8,128)S(1)}, f32[9,16,128]{2,1,0:T(8,128)S(1)}, u32[]{:S(2)}, u32[]{:S(2)}) collective-permute-start(f32[9,16,128]{2,1,0:T(8,128)S(1)} %collective-permute-done.3.halo_odd.refs_1_), channel_id=1, source_target_pairs={{0,1},{1,0},{2,3},{3,2},{4,5},{5,4},{6,7},{7,6},{8,9},{9,8},{10,11... | collective-permute-start | bytes 221192 | tf_op jit(solution)/shard_map/ppermute | solution.py:440

commit v6 on v5

--- a/solution.py
+++ b/solution.py
@@ -203,7 +203,7 @@
 
 
 def main_kernel(points, *refs):
-    cells_in, halo_odd, sib_odd, out_inc, out_defect, cells = refs[0:6]
+    cells, halo_odd, sib_odd, out_inc, out_defect, _ = refs[0:6]
     couple, conv_face, skews, lu, diagonal, upper_diag, lower_diag, sides, solved, vmin, vplus, azd, src, out_cells = refs[6:]
 
     core = lax.axis_index("wn")

time: 18.8 us -> 18.8 us (level)
  no operation moved by 1% of the time
where the time goes in v6:
time: 18.8 us; the launch traced here: 18.6 us
  starting transfers between devices  7.62 us (41%)
  Pallas kernels  6.49 us (35%)
  waiting for transfers between devices  3.86 us (21%)
  between operations  0.66 us (4%)
    ppermute x1, starting transfers between devices, per_device(): halo_odd = lax.ppermute(odd, 'az', odd_pairs)  4.53 us
    pallas_call x1, Pallas kernels, per_device(): pl.pallas_call(lambda *refs: main_kernel(points, *refs), out_shape=(out,...  3.99 us
    ppermute x1, waiting for transfers between devices, per_device(): halo_odd = lax.ppermute(odd, 'az', odd_pairs)  3.41 us
    ppermute x1, starting transfers between devices, per_device(): halo_even = lax.ppermute(even, 'az', even_pairs)  2.56 us
    pallas_call x1, Pallas kernels, per_device(): pl.pallas_call(pack_kernel, out_shape=(pack, pack, bulk, jax.ShapeDtypeSt...  1.69 us
    pallas_call x1, Pallas kernels, per_device(): pl.pallas_call(collect_kernel, out_shape=tiles, in_specs=[vmem] * 6, out_...  0.81 us
    ppermute x3, starting transfers between devices, cross(): return lax.ppermute(array, 'wn', [(0, 1), (1, 0)])  0.52 us
    ppermute x3, waiting for transfers between devices, cross(): return lax.ppermute(array, 'wn', [(0, 1), (1, 0)])  0.44 us
  transfers between devices with their start and end apart: 5, of which 2 were waited for; matrix products, arithmetic and copies ran while one was open for 0% of the time, Pallas kernels for 4%

profile of v6, /device:TPU:0, one launch (start us, length us, event | category | flops | bytes accessed | tf_op | source)
XLA Modules:
  0.0 18.6 jit_solution(13281152772280909828)
XLA Ops:
  0.6 1.7 %pack_halo.1 = (f32[9,16,128]{2,1,0:T(8,128)S(1)}, f32[9,16,128]{2,1,0:T(8,128)S(1)}, f32[75,16,256]{2,1,0:T(8,128)S(1)}, s32[1,256]{1,0:T(1,128)S(1)}) custom-call(f32[25,16,256]{2,1,0:T(8,128)} %bitcast.3, f32[25,16,256]{2,1,0:T(8,128)} %bitcast.4, s32[1,256]{1,0:T(1,128)} %bitcast.5, f32[5,16,256]{2,1,0:T(8,128)} %visc_hbm.1, f32[5,16,256]{2,1,0:T(8,128)} %flux_hbm.1, ...), custom_call_target="tpu_custom_call" | custom-call | tf_op jit(solution)/shard_map/pack_halo/pallas_call | solution.py:427
  2.3 0.5 %collective-permute-start = (f32[75,16,256]{2,1,0:T(8,128)S(1)}, f32[75,16,256]{2,1,0:T(8,128)S(1)}, u32[]{:S(2)}, u32[]{:S(2)}) collective-permute-start(f32[75,16,256]{2,1,0:T(8,128)S(1)} %get-tuple-element.8.bulk), channel_id=1, source_target_pairs={{0,1},{1,0},{2,3},{3,2},{4,5},{5,4},{6,7},{7,6},{8,9},{9,8},{10,11... | collective-permute-start | bytes 3686408 | tf_op jit(solution)/shard_map/ppermute | solution.py:440
  2.8 2.6 %collective-permute-start.1 = (f32[9,16,128]{2,1,0:T(8,128)S(1)}, f32[9,16,128]{2,1,0:T(8,128)S(1)}, u32[]{:S(2)}, u32[]{:S(2)}) collective-permute-start(f32[9,16,128]{2,1,0:T(8,128)S(1)} %get-tuple-element.10), channel_id=1, source_target_pairs={{0,2},{2,0},{4,6},{6,4},{8,10},{10,8},{12,14},{14,12},{16,18},{18,... | collective-permute-start | bytes 221192 | tf_op jit(solution)/shard_map/ppermute | solution.py:436
  5.4 4.5 %collective-permute-start.3 = (f32[9,16,128]{2,1,0:T(8,128)S(1)}, f32[9,16,128]{2,1,0:T(8,128)S(1)}, u32[]{:S(2)}, u32[]{:S(2)}) collective-permute-start(f32[9,16,128]{2,1,0:T(8,128)S(1)} %get-tuple-element.11), channel_id=1, source_target_pairs={{0,30},{2,4},{4,2},{6,8},{8,6},{10,12},{12,10},{14,16},{16,14},{18... | collective-permute-start | bytes 221192 | tf_op jit(solution)/shard_map/ppermute | solution.py:437
  9.9 0.0 collective-permute-done.1.halo_even
  9.9 0.0 collective-permute-start.2
  9.9 3.4 %collective-permute-done.3.halo_odd.refs_1_ = f32[9,16,128]{2,1,0:T(8,128)S(1)} collective-permute-done((f32[9,16,128]{2,1,0:T(8,128)S(1)}, f32[9,16,128]{2,1,0:T(8,128)S(1)}, u32[]{:S(2)}, u32[]{:S(2)}) %collective-permute-start.3) | collective-permute-done | bytes 73760 | tf_op jit(solution)/shard_map/ppermute | solution.py:437
  13.4 0.0 collective-permute-start.4
  13.4 0.0 collective-permute-done.2.sib_even
  13.4 0.0 collective-permute-done.sib_bulk
  13.4 0.8 %collect_lines.1.refs_0_ = f32[67,152,128]{2,1,0:T(8,128)S(1)} custom-call(f32[75,16,256]{2,1,0:T(8,128)S(1)} %get-tuple-element.8.bulk, f32[75,16,256]{2,1,0:T(8,128)S(1)} %collective-permute-done.sib_bulk, s32[1,256]{1,0:T(1,128)S(1)} %get-tuple-element.9.edge, f32[9,16,128]{2,1,0:T(8,128)S(1)} %collective-permute-done.1.halo_even, ...), custom_call_target="tpu_custom_call" | custom-call | tf_op jit(solution)/shard_map/collect_lines/pallas_call | solution.py:446
  14.2 0.4 %collective-permute-done.4.refs_2_ = f32[9,16,128]{2,1,0:T(8,128)S(1)} collective-permute-done((f32[9,16,128]{2,1,0:T(8,128)S(1)}, f32[9,16,128]{2,1,0:T(8,128)S(1)}, u32[]{:S(2)}, u32[]{:S(2)}) %collective-permute-start.4) | collective-permute-done | bytes 73760 | tf_op jit(solution)/shard_map/ppermute | solution.py:440
  14.6 4.0 %relax_lines.1 = (f32[5,16,256]{2,1,0:T(8,128)}, f32[5,16,256]{2,1,0:T(8,128)}, f32[67,152,128]{2,1,0:T(8,128)S(1)}) custom-call(f32[67,152,128]{2,1,0:T(8,128)S(1)} %collect_lines.1.refs_0_, f32[9,16,128]{2,1,0:T(8,128)S(1)} %collective-permute-done.3.halo_odd.refs_1_, f32[9,16,128]{2,1,0:T(8,128)S(1)} %collective-permute-done.4.refs_2_), custom_call_target="tpu_custom_call", output_to_operand_aliasing={{2}: (0, {})} | custom-call | tf_op jit(solution)/shard_map/relax_lines/pallas_call | solution.py:459
Async XLA Ops:
  2.3 11.0 %collective-permute-start = (f32[75,16,256]{2,1,0:T(8,128)S(1)}, f32[75,16,256]{2,1,0:T(8,128)S(1)}, u32[]{:S(2)}, u32[]{:S(2)}) collective-permute-start(f32[75,16,256]{2,1,0:T(8,128)S(1)} %get-tuple-element.8.bulk), channel_id=1, source_target_pairs={{0,1},{1,0},{2,3},{3,2},{4,5},{5,4},{6,7},{7,6},{8,9},{9,8},{10,11... | collective-permute-start | bytes 3686408 | tf_op jit(solution)/shard_map/ppermute | solution.py:440
  2.8 7.1 %collective-permute-start.1 = (f32[9,16,128]{2,1,0:T(8,128)S(1)}, f32[9,16,128]{2,1,0:T(8,128)S(1)}, u32[]{:S(2)}, u32[]{:S(2)}) collective-permute-start(f32[9,16,128]{2,1,0:T(8,128)S(1)} %get-tuple-element.10), channel_id=1, source_target_pairs={{0,2},{2,0},{4,6},{6,4},{8,10},{10,8},{12,14},{14,12},{16,18},{18,... | collective-permute-start | bytes 221192 | tf_op jit(solution)/shard_map/ppermute | solution.py:436
  5.4 7.9 %collective-permute-start.3 = (f32[9,16,128]{2,1,0:T(8,128)S(1)}, f32[9,16,128]{2,1,0:T(8,128)S(1)}, u32[]{:S(2)}, u32[]{:S(2)}) collective-permute-start(f32[9,16,128]{2,1,0:T(8,128)S(1)} %get-tuple-element.11), channel_id=1, source_target_pairs={{0,30},{2,4},{4,2},{6,8},{8,6},{10,12},{12,10},{14,16},{16,14},{18... | collective-permute-start | bytes 221192 | tf_op jit(solution)/shard_map/ppermute | solution.py:437
  9.9 3.4 %collective-permute-start.2 = (f32[9,16,128]{2,1,0:T(8,128)S(1)}, f32[9,16,128]{2,1,0:T(8,128)S(1)}, u32[]{:S(2)}, u32[]{:S(2)}) collective-permute-start(f32[9,16,128]{2,1,0:T(8,128)S(1)} %collective-permute-done.1.halo_even), channel_id=1, source_target_pairs={{0,1},{1,0},{2,3},{3,2},{4,5},{5,4},{6,7},{7,6},{8,9},{9,8},{10,11... | collective-permute-start | bytes 221192 | tf_op jit(solution)/shard_map/ppermute | solution.py:440
  13.4 1.3 %collective-permute-start.4 = (f32[9,16,128]{2,1,0:T(8,128)S(1)}, f32[9,16,128]{2,1,0:T(8,128)S(1)}, u32[]{:S(2)}, u32[]{:S(2)}) collective-permute-start(f32[9,16,128]{2,1,0:T(8,128)S(1)} %collective-permute-done.3.halo_odd.refs_1_), channel_id=1, source_target_pairs={{0,1},{1,0},{2,3},{3,2},{4,5},{5,4},{6,7},{7,6},{8,9},{9,8},{10,11... | collective-permute-start | bytes 221192 | tf_op jit(solution)/shard_map/ppermute | solution.py:440

commit v7 on v6

--- a/solution.py
+++ b/solution.py
@@ -354,9 +354,10 @@
         for k in reversed(range(points)):
             inner = None
             if k:
-                shift = times(block(couple, k - 1), x)
-                y_here = vector(sides, k - 1)
-                inner = [y_here[c] - shift[c] for c in range(NC)]
+                y_here, inner = vector(sides, k - 1), []
+                for c, row_c in enumerate(block(couple, k - 1)):
+                    terms = [row_c[r] * x[r] for r in range(NC)]
+                    inner.append(((y_here[c] - terms[0]) - (terms[1] + terms[2])) - (terms[3] + terms[4]))
             visit(k, inner, x, beyond)
             x, beyond = inner, x
 

time: 18.8 us -> 18.8 us (level)
  no operation moved by 1% of the time
where the time goes in v7:
time: 18.8 us; the launch traced here: 18.6 us
  starting transfers between devices  7.62 us (41%)
  Pallas kernels  6.47 us (34%)
  waiting for transfers between devices  3.86 us (21%)
  between operations  0.66 us (4%)
    ppermute x1, starting transfers between devices, per_device(): halo_odd = lax.ppermute(odd, 'az', odd_pairs)  4.53 us
    pallas_call x1, Pallas kernels, per_device(): pl.pallas_call(lambda *refs: main_kernel(points, *refs), out_shape=(out,...  3.97 us
    ppermute x1, waiting for transfers between devices, per_device(): halo_odd = lax.ppermute(odd, 'az', odd_pairs)  3.41 us
    ppermute x1, starting transfers between devices, per_device(): halo_even = lax.ppermute(even, 'az', even_pairs)  2.56 us
    pallas_call x1, Pallas kernels, per_device(): pl.pallas_call(pack_kernel, out_shape=(pack, pack, bulk, jax.ShapeDtypeSt...  1.69 us
    pallas_call x1, Pallas kernels, per_device(): pl.pallas_call(collect_kernel, out_shape=tiles, in_specs=[vmem] * 6, out_...  0.81 us
    ppermute x3, starting transfers between devices, cross(): return lax.ppermute(array, 'wn', [(0, 1), (1, 0)])  0.52 us
    ppermute x3, waiting for transfers between devices, cross(): return lax.ppermute(array, 'wn', [(0, 1), (1, 0)])  0.44 us
  transfers between devices with their start and end apart: 5, of which 2 were waited for; matrix products, arithmetic and copies ran while one was open for 0% of the time, Pallas kernels for 4%

profile of v7, /device:TPU:0, one launch (start us, length us, event | category | flops | bytes accessed | tf_op | source)
XLA Modules:
  0.0 18.6 jit_solution(2796501768075930908)
XLA Ops:
  0.6 1.7 %pack_halo.1 = (f32[9,16,128]{2,1,0:T(8,128)S(1)}, f32[9,16,128]{2,1,0:T(8,128)S(1)}, f32[75,16,256]{2,1,0:T(8,128)S(1)}, s32[1,256]{1,0:T(1,128)S(1)}) custom-call(f32[25,16,256]{2,1,0:T(8,128)} %bitcast.3, f32[25,16,256]{2,1,0:T(8,128)} %bitcast.4, s32[1,256]{1,0:T(1,128)} %bitcast.5, f32[5,16,256]{2,1,0:T(8,128)} %visc_hbm.1, f32[5,16,256]{2,1,0:T(8,128)} %flux_hbm.1, ...), custom_call_target="tpu_custom_call" | custom-call | tf_op jit(solution)/shard_map/pack_halo/pallas_call | solution.py:428
  2.3 0.5 %collective-permute-start = (f32[75,16,256]{2,1,0:T(8,128)S(1)}, f32[75,16,256]{2,1,0:T(8,128)S(1)}, u32[]{:S(2)}, u32[]{:S(2)}) collective-permute-start(f32[75,16,256]{2,1,0:T(8,128)S(1)} %get-tuple-element.8.bulk), channel_id=1, source_target_pairs={{0,1},{1,0},{2,3},{3,2},{4,5},{5,4},{6,7},{7,6},{8,9},{9,8},{10,11... | collective-permute-start | bytes 3686408 | tf_op jit(solution)/shard_map/ppermute | solution.py:441
  2.8 2.6 %collective-permute-start.1 = (f32[9,16,128]{2,1,0:T(8,128)S(1)}, f32[9,16,128]{2,1,0:T(8,128)S(1)}, u32[]{:S(2)}, u32[]{:S(2)}) collective-permute-start(f32[9,16,128]{2,1,0:T(8,128)S(1)} %get-tuple-element.10), channel_id=1, source_target_pairs={{0,2},{2,0},{4,6},{6,4},{8,10},{10,8},{12,14},{14,12},{16,18},{18,... | collective-permute-start | bytes 221192 | tf_op jit(solution)/shard_map/ppermute | solution.py:437
  5.4 4.5 %collective-permute-start.3 = (f32[9,16,128]{2,1,0:T(8,128)S(1)}, f32[9,16,128]{2,1,0:T(8,128)S(1)}, u32[]{:S(2)}, u32[]{:S(2)}) collective-permute-start(f32[9,16,128]{2,1,0:T(8,128)S(1)} %get-tuple-element.11), channel_id=1, source_target_pairs={{0,30},{2,4},{4,2},{6,8},{8,6},{10,12},{12,10},{14,16},{16,14},{18... | collective-permute-start | bytes 221192 | tf_op jit(solution)/shard_map/ppermute | solution.py:438
  9.9 0.0 collective-permute-done.1.halo_even
  9.9 0.0 collective-permute-start.2
  9.9 3.4 %collective-permute-done.3.halo_odd.refs_1_ = f32[9,16,128]{2,1,0:T(8,128)S(1)} collective-permute-done((f32[9,16,128]{2,1,0:T(8,128)S(1)}, f32[9,16,128]{2,1,0:T(8,128)S(1)}, u32[]{:S(2)}, u32[]{:S(2)}) %collective-permute-start.3) | collective-permute-done | bytes 73760 | tf_op jit(solution)/shard_map/ppermute | solution.py:438
  13.4 0.0 collective-permute-start.4
  13.4 0.0 collective-permute-done.2.sib_even
  13.4 0.0 collective-permute-done.sib_bulk
  13.4 0.8 %collect_lines.1.refs_0_ = f32[67,152,128]{2,1,0:T(8,128)S(1)} custom-call(f32[75,16,256]{2,1,0:T(8,128)S(1)} %get-tuple-element.8.bulk, f32[75,16,256]{2,1,0:T(8,128)S(1)} %collective-permute-done.sib_bulk, s32[1,256]{1,0:T(1,128)S(1)} %get-tuple-element.9.edge, f32[9,16,128]{2,1,0:T(8,128)S(1)} %collective-permute-done.1.halo_even, ...), custom_call_target="tpu_custom_call" | custom-call | tf_op jit(solution)/shard_map/collect_lines/pallas_call | solution.py:447
  14.2 0.4 %collective-permute-done.4.refs_2_ = f32[9,16,128]{2,1,0:T(8,128)S(1)} collective-permute-done((f32[9,16,128]{2,1,0:T(8,128)S(1)}, f32[9,16,128]{2,1,0:T(8,128)S(1)}, u32[]{:S(2)}, u32[]{:S(2)}) %collective-permute-start.4) | collective-permute-done | bytes 73760 | tf_op jit(solution)/shard_map/ppermute | solution.py:441
  14.6 4.0 %relax_lines.1 = (f32[5,16,256]{2,1,0:T(8,128)}, f32[5,16,256]{2,1,0:T(8,128)}, f32[67,152,128]{2,1,0:T(8,128)S(1)}) custom-call(f32[67,152,128]{2,1,0:T(8,128)S(1)} %collect_lines.1.refs_0_, f32[9,16,128]{2,1,0:T(8,128)S(1)} %collective-permute-done.3.halo_odd.refs_1_, f32[9,16,128]{2,1,0:T(8,128)S(1)} %collective-permute-done.4.refs_2_), custom_call_target="tpu_custom_call", output_to_operand_aliasing={{2}: (0, {})} | custom-call | tf_op jit(solution)/shard_map/relax_lines/pallas_call | solution.py:460
Async XLA Ops:
  2.3 11.0 %collective-permute-start = (f32[75,16,256]{2,1,0:T(8,128)S(1)}, f32[75,16,256]{2,1,0:T(8,128)S(1)}, u32[]{:S(2)}, u32[]{:S(2)}) collective-permute-start(f32[75,16,256]{2,1,0:T(8,128)S(1)} %get-tuple-element.8.bulk), channel_id=1, source_target_pairs={{0,1},{1,0},{2,3},{3,2},{4,5},{5,4},{6,7},{7,6},{8,9},{9,8},{10,11... | collective-permute-start | bytes 3686408 | tf_op jit(solution)/shard_map/ppermute | solution.py:441
  2.8 7.1 %collective-permute-start.1 = (f32[9,16,128]{2,1,0:T(8,128)S(1)}, f32[9,16,128]{2,1,0:T(8,128)S(1)}, u32[]{:S(2)}, u32[]{:S(2)}) collective-permute-start(f32[9,16,128]{2,1,0:T(8,128)S(1)} %get-tuple-element.10), channel_id=1, source_target_pairs={{0,2},{2,0},{4,6},{6,4},{8,10},{10,8},{12,14},{14,12},{16,18},{18,... | collective-permute-start | bytes 221192 | tf_op jit(solution)/shard_map/ppermute | solution.py:437
  5.4 7.9 %collective-permute-start.3 = (f32[9,16,128]{2,1,0:T(8,128)S(1)}, f32[9,16,128]{2,1,0:T(8,128)S(1)}, u32[]{:S(2)}, u32[]{:S(2)}) collective-permute-start(f32[9,16,128]{2,1,0:T(8,128)S(1)} %get-tuple-element.11), channel_id=1, source_target_pairs={{0,30},{2,4},{4,2},{6,8},{8,6},{10,12},{12,10},{14,16},{16,14},{18... | collective-permute-start | bytes 221192 | tf_op jit(solution)/shard_map/ppermute | solution.py:438
  9.9 3.4 %collective-permute-start.2 = (f32[9,16,128]{2,1,0:T(8,128)S(1)}, f32[9,16,128]{2,1,0:T(8,128)S(1)}, u32[]{:S(2)}, u32[]{:S(2)}) collective-permute-start(f32[9,16,128]{2,1,0:T(8,128)S(1)} %collective-permute-done.1.halo_even), channel_id=1, source_target_pairs={{0,1},{1,0},{2,3},{3,2},{4,5},{5,4},{6,7},{7,6},{8,9},{9,8},{10,11... | collective-permute-start | bytes 221192 | tf_op jit(solution)/shard_map/ppermute | solution.py:441
  13.4 1.3 %collective-permute-start.4 = (f32[9,16,128]{2,1,0:T(8,128)S(1)}, f32[9,16,128]{2,1,0:T(8,128)S(1)}, u32[]{:S(2)}, u32[]{:S(2)}) collective-permute-start(f32[9,16,128]{2,1,0:T(8,128)S(1)} %collective-permute-done.3.halo_odd.refs_1_), channel_id=1, source_target_pairs={{0,1},{1,0},{2,3},{3,2},{4,5},{5,4},{6,7},{7,6},{8,9},{9,8},{10,11... | collective-permute-start | bytes 221192 | tf_op jit(solution)/shard_map/ppermute | solution.py:441
